TPU v7x, 32 devices: a whole 2x2x4 slice. The times are simulated.
32 devices in a mesh: dp: 8 (over z, y), mp: 4 (over x, core).
Axes of the slice: x: 2, y: 2, z: 4, core: 2. Of those that a mesh axis runs over, the one named last changes fastest.
Arguments:
- tokens: bfloat16 [8192, 1024], P('dp'), may hold values from -6 to 6
- doc_lengths: int32 [8], P('dp'), may hold values from 256 to 1024, as said below
- cls_pos: int32 [8, 4], P('dp'), may hold values from 0 to 1023, as said below
- cls_count: int32 [8], P('dp'), may hold values from 1 to 4, as said below
- q_weight: bfloat16 [1024, 1024], P(None, 'mp'), may hold values from -0.1875 to 0.1875
- q_bias: bfloat16 [1024], P('mp'), may hold values from -2 to 2
- k_weight: bfloat16 [1024, 1024], P(None, 'mp'), may hold values from -0.1875 to 0.1875
- v_weight: bfloat16 [1024, 1024], P(None, 'mp'), may hold values from -0.1875 to 0.1875
- v_bias: bfloat16 [1024], P('mp'), may hold values from -2 to 2
- o_weight: bfloat16 [1024, 1024], P('mp'), may hold values from -1.5 to 1.5
- o_bias: bfloat16 [1024], replicated, may hold values from -2 to 2
- ln1_gain: bfloat16 [1024], replicated, may hold values from 0.5 to 1.5
- ln1_bias: bfloat16 [1024], replicated, may hold values from -2 to 2
- up_weight: bfloat16 [1024, 4096], P(None, 'mp'), may hold values from -0.1875 to 0.1875
- up_bias: bfloat16 [4096], P('mp'), may hold values from -2 to 2
- down_weight: bfloat16 [4096, 1024], P('mp'), may hold values from -0.09375 to 0.09375
- down_bias: bfloat16 [1024], replicated, may hold values from -2 to 2
- ln2_gain: bfloat16 [1024], replicated, may hold values from 0.5 to 1.5
- ln2_bias: bfloat16 [1024], replicated, may hold values from -2 to 2
- out_grad: bfloat16 [8192, 1024], P('dp'), may hold values from -6 to 6
- pooled_grad: float32 [8, 4, 1024], P('dp'), may hold values from -6 to 6
Outputs:
- out: bfloat16 [8192, 1024], P('dp')
- pooled: float32 [8, 4, 1024], P('dp')
- in_grad: float32 [8192, 1024], P('dp')
- q_weight_grad: float32 [1024, 1024], P('dp', 'mp')
- q_bias_grad: float32 [1024], P('mp')
- k_weight_grad: float32 [1024, 1024], P('dp', 'mp')
- v_weight_grad: float32 [1024, 1024], P('dp', 'mp')
- v_bias_grad: float32 [1024], P('mp')
- o_weight_grad: float32 [1024, 1024], P('mp', 'dp')
- o_bias_grad: float32 [1024], replicated
- ln1_gain_grad: float32 [1024], replicated
- ln1_bias_grad: float32 [1024], replicated
- up_weight_grad: float32 [1024, 4096], P('dp', 'mp')
- up_bias_grad: float32 [4096], P('mp')
- down_weight_grad: float32 [4096, 1024], P('mp', 'dp')
- down_bias_grad: float32 [1024], replicated
- ln2_gain_grad: float32 [1024], replicated
- ln2_bias_grad: float32 [1024], replicated
Inputs may be any that keep to these rules, and one draw needn't show every extreme that they name: `doc_lengths`: in every draw some document fills all 1024 slots. `cls_count`: A document's length divided by 256, rounded up; some document has 4. `cls_pos`: for j below the document's cls_count, entry j lies in [j * 256, (j + 1) * 256) and below the document's length; later entries are 0. In a document of 1024 tokens the last entry is 1023.
All inputs are finite; a program needn't handle non-finite values.
Results may differ from a plain program's by a relative error of at most 0.014.
The roundings to bfloat16 on the way count: a program that leaves them out, or rounds other values in their place, can miss the bound.
Values sent between devices are 32-bit elements; how exact they have to be, the bound alone decides.
No kernel may reach another device: no remote copies, remote signals or barrier semaphores. Data moves between devices by JAX's collectives and lax.ppermute only.
A program may use at most 128 MiB of HBM per device.

v0:
```python
import functools

import jax
import jax.numpy as jnp
from jax import lax
from jax.experimental import pallas as pl
from jax.experimental.pallas import tpu as pltpu
from jax.sharding import PartitionSpec as P

HEAD_DIM = 64
NORM_EPS = 1e-05
ROOT_HALF = 0.7071067811865476
INV_ROOT_TAU = 0.3989422804014327
LOG2E = 1.4426950408889634
SCORE_SCALE = 0.125 * LOG2E
MASKED = -1e30

f32 = jnp.float32
bf16 = jnp.bfloat16
VMEM_LIMIT = 20 * 1024 * 1024


def dot_nn(a, b):
    return lax.dot_general(a, b, (((1,), (0,)), ((), ())), preferred_element_type=f32)


def dot_nt(a, b):
    return lax.dot_general(a, b, (((1,), (1,)), ((), ())), preferred_element_type=f32)


def dot_tn(a, b):
    return lax.dot_general(a, b, (((0,), (0,)), ((), ())), preferred_element_type=f32)


def attn_fwd_kernel(q_ref, k_ref, v_ref, bias_ref, o_ref, lse_ref):
    rows, width = q_ref.shape
    heads = width // HEAD_DIM
    lane = lax.broadcasted_iota(jnp.int32, (1, width), 1) // HEAD_DIM
    lse_lane = lax.broadcasted_iota(jnp.int32, (1, 128), 1)
    q = q_ref[...]
    k = k_ref[...]
    v = v_ref[...]
    bias = bias_ref[...]
    out = jnp.zeros((rows, width), f32)
    lse = jnp.zeros((rows, 128), f32)
    for h in range(heads):
        qh = jnp.where(lane == h, q, jnp.zeros_like(q))
        s = dot_nt(qh, k) * SCORE_SCALE + bias
        top = jnp.max(s, axis=1, keepdims=True)
        e = jnp.exp2(s - top)
        total = jnp.sum(e, axis=1, keepdims=True)
        p = (e * (1.0 / total)).astype(bf16)
        c = dot_nn(p, v)
        out = jnp.where(lane == h, c, out)
        lse = jnp.where(lse_lane == h, top + jnp.log2(total), lse)
    o_ref[...] = out.astype(o_ref.dtype)
    lse_ref[...] = lse


def attn_fwd(q, k, v, bias, block, dtype):
    rows, width = q.shape
    keys = k.shape[0]
    full = pl.BlockSpec((keys, width), lambda i: (0, 0))
    return pl.pallas_call(
        attn_fwd_kernel,
        grid=(rows // block,),
        in_specs=[
            pl.BlockSpec((block, width), lambda i: (i, 0)),
            full,
            full,
            pl.BlockSpec((1, keys), lambda i: (0, 0)),
        ],
        out_specs=[
            pl.BlockSpec((block, width), lambda i: (i, 0)),
            pl.BlockSpec((block, 128), lambda i: (i, 0)),
        ],
        out_shape=[
            jax.ShapeDtypeStruct((rows, width), dtype),
            jax.ShapeDtypeStruct((rows, 128), f32),
        ],
        compiler_params=pltpu.CompilerParams(vmem_limit_bytes=VMEM_LIMIT),
        cost_estimate=pl.CostEstimate(flops=1024, bytes_accessed=1024, transcendentals=0),
        name="attn_fwd",
    )(q, k, v, bias)


def attn_bwd_kernel(carried, *refs):
    q_ref, g_ref, k_ref, v_ref, bias_ref, lse_ref = refs[:6]
    refs = refs[6:]
    if carried:
        gk_in, gv_in = refs[:2]
        refs = refs[2:]
    gq_ref, gk_ref, gv_ref, gk_acc, gv_acc, gq_acc = refs
    step = pl.program_id(0)
    width = q_ref.shape[1]
    lane = lax.broadcasted_iota(jnp.int32, (1, width), 1) // HEAD_DIM
    lse_lane = lax.broadcasted_iota(jnp.int32, (1, 128), 1)

    @pl.when(step == 0)
    def _():
        gk_acc[...] = gk_in[...] if carried else jnp.zeros_like(gk_acc)
        gv_acc[...] = gv_in[...] if carried else jnp.zeros_like(gv_acc)

    @pl.loop(0, width // HEAD_DIM)
    def _(h):
        mine = lane == h
        zero = jnp.zeros(q_ref.shape, bf16)
        qh = jnp.where(mine, q_ref[...], zero)
        gh = jnp.where(mine, g_ref[...].astype(bf16), zero)
        lse = jnp.sum(jnp.where(lse_lane == h, lse_ref[...], 0.0), axis=1, keepdims=True)
        s = dot_nt(qh, k_ref[...]) * SCORE_SCALE + bias_ref[...]
        p = jnp.exp2(s - lse)
        dp = dot_nt(gh, v_ref[...])
        inner = jnp.sum(p * dp, axis=1, keepdims=True)
        ds = (p * (dp - inner)).astype(bf16)
        gq_acc[...] = jnp.where(mine, dot_nn(ds, k_ref[...]), gq_acc[...])
        gk_acc[...] += dot_tn(ds, qh)
        gv_acc[...] += dot_tn(p.astype(bf16), gh)

    gq_ref[...] = (gq_acc[...] * 0.125).astype(bf16)

    @pl.when(step == pl.num_programs(0) - 1)
    def _():
        scale = 0.125 if carried else 1.0
        gk_ref[...] = (gk_acc[...] * scale).astype(gk_ref.dtype)
        gv_ref[...] = gv_acc[...].astype(gv_ref.dtype)


def attn_bwd(q, g, k, v, bias, lse, block, sums=()):
    rows, width = q.shape
    keys = k.shape[0]
    full = pl.BlockSpec((keys, width), lambda i: (0, 0))
    part = pl.BlockSpec((block, width), lambda i: (i, 0))
    sum_type = bf16 if sums else f32
    return pl.pallas_call(
        functools.partial(attn_bwd_kernel, bool(sums)),
        grid=(rows // block,),
        in_specs=[
            part,
            part,
            full,
            full,
            pl.BlockSpec((1, keys), lambda i: (0, 0)),
            pl.BlockSpec((block, 128), lambda i: (i, 0)),
        ]
        + [full] * len(sums),
        out_specs=[part, full, full],
        out_shape=[
            jax.ShapeDtypeStruct((rows, width), bf16),
            jax.ShapeDtypeStruct((keys, width), sum_type),
            jax.ShapeDtypeStruct((keys, width), sum_type),
        ],
        scratch_shapes=[pltpu.VMEM((keys, width), f32)] * 2 + [pltpu.VMEM((block, width), f32)],
        compiler_params=pltpu.CompilerParams(vmem_limit_bytes=VMEM_LIMIT),
        cost_estimate=pl.CostEstimate(flops=1024, bytes_accessed=1024, transcendentals=0),
        name="attn_bwd",
    )(q, g, k, v, bias, lse, *sums)


in_vmem = pl.BlockSpec(memory_space=pltpu.VMEM)
STRIP = 256
LENGTH, COUNT, MARKS, BITS = 4, 5, 6, 10
O_BIAS, GAIN_ONE, SHIFT_ONE, GAIN_TWO, SHIFT_TWO, DOWN_BIAS, UP_BIAS, QV_BIAS = range(8)


def row_of(ref, index):
    return ref[index : index + 1, :]


def strip(index, size=STRIP):
    return pl.ds(pl.multiple_of(index * size, size), size)


def shape(rows, cols, dtype=f32):
    return jax.ShapeDtypeStruct((rows, cols), dtype)


def whole(kernel, name, inputs, outputs, scalars=None, filled=(), sems=0, scratch=(), limit=8, far=False):
    lead = [] if scalars is None else [scalars]
    anywhere = pl.BlockSpec(memory_space=pl.ANY)
    given = [v for v in filled if not isinstance(v, jax.ShapeDtypeStruct)]
    begun = [jax.ShapeDtypeStruct(v.shape, v.dtype) for v in filled]
    first = len(lead) + len(inputs)
    return pl.pallas_call(
        kernel,
        in_specs=[pl.BlockSpec(memory_space=pltpu.SMEM)] * len(lead)
        + [in_vmem] * len(inputs)
        + [anywhere] * len(given),
        out_specs=[pl.BlockSpec(memory_space=pltpu.HBM) if far else anywhere] * len(begun)
        + [in_vmem] * len(outputs),
        out_shape=begun + list(outputs),
        scratch_shapes=list(scratch) + ([pltpu.SemaphoreType.DMA((sems,))] if sems else []),
        input_output_aliases={first + p: p for p in range(len(given))},
        compiler_params=pltpu.CompilerParams(vmem_limit_bytes=limit * 1024 * 1024),
        cost_estimate=pl.CostEstimate(flops=1024, bytes_accessed=1024, transcendentals=0),
        name=name,
    )(*lead, *inputs, *given)


class Copies:
    def __init__(self, sems):
        self.sems, self.made = sems, []

    def start(self, source, target):
        copy = pltpu.make_async_copy(source, target, self.sems.at[len(self.made)])
        copy.start()
        self.made.append(copy)

    def wait(self):
        for copy in self.made:
            copy.wait()


def project_kernel(meta_ref, near_ref, other_ref, o_near_ref, o_got_ref, o_other_ref, own_ref, sib_ref, low_ref, o_far_ref):
    rows = own_ref.shape[0]
    part = o_got_ref.shape[0]
    first = meta_ref[BITS] == 0
    o_far_ref[:part, :] = jnp.where(first, o_got_ref[...], o_other_ref[...]).astype(bf16)
    o_far_ref[part:, :] = jnp.where(first, o_other_ref[...], o_got_ref[...]).astype(bf16)
    low_ref[...] = other_ref[...].astype(bf16)
    both = dot_nn(near_ref[...], o_near_ref[...]) + dot_nn(low_ref[...], o_far_ref[...])
    own_ref[...] = both[:rows]
    sib_ref[...] = both[rows:]


def mean_of(values):
    return jnp.sum(values, axis=-1, keepdims=True) * (1.0 / values.shape[-1])


def norm_rows(values):
    centre = values - mean_of(values)
    scale_inv = lax.rsqrt(mean_of(centre * centre) + NORM_EPS)
    return centre * scale_inv, scale_inv


def norm_rows_back(grad_rows, unit_rows, scale_inv, gain):
    scaled = grad_rows * gain
    return scale_inv * (scaled - mean_of(scaled) - unit_rows * mean_of(scaled * unit_rows))


def first_norm_kernel(own_ref, near_ref, tok_ref, vec_ref, na_ref, nb_ref, all_ref, unit_ref, inv_ref):
    gain = row_of(vec_ref, GAIN_ONE)
    shift = row_of(vec_ref, SHIFT_ONE)
    for half, out_ref in enumerate((na_ref, nb_ref)):
        size = out_ref.shape[0]
        rows = pl.ds(half * size, size)
        values = tok_ref[rows, :].astype(f32) + (own_ref[rows, :] + near_ref[rows, :] + row_of(vec_ref, O_BIAS))
        unit, scale_inv = norm_rows(values)
        unit_ref[rows, :] = unit
        inv_ref[rows, :] = jnp.broadcast_to(scale_inv, (size, inv_ref.shape[1]))
        normed = unit * gain + shift
        out_ref[...] = normed
        all_ref[rows, :] = normed


def move_columns(source, target, blocks):
    wide = source.shape[1] // len(blocks)
    for place, block in enumerate(blocks):
        target[:, place * wide : (place + 1) * wide] = source[:, block * wide : (block + 1) * wide]


def order_kernel(blocks_a, blocks_b, in_ref, a_ref, b_ref):
    move_columns(in_ref, a_ref, blocks_a)
    move_columns(in_ref, b_ref, blocks_b)


def prepare_kernel(meta_ref, o_ref, *refs):
    given = refs[:7]
    part_ref, vec_ref, o_in = refs[7:10]
    lines = refs[10:17]
    sems = refs[17]
    copies = Copies(sems)
    copies.start(o_ref.at[strip(meta_ref[BITS], part_ref.shape[0]), :], o_in)
    for line_ref, vector_ref in zip(lines, given):
        copies.start(vector_ref, line_ref)
    copies.wait()
    part_ref[...] = o_in[...].astype(f32)
    vec_ref[...] = jnp.zeros_like(vec_ref)
    for k, line_ref in enumerate(lines):
        vec_ref[k, :] = line_ref[...].astype(f32)


def prepare(meta, o_weight, vectors):
    rows, width = o_weight.shape
    far = pl.BlockSpec(memory_space=pltpu.HBM)
    return pl.pallas_call(
        prepare_kernel,
        in_specs=[pl.BlockSpec(memory_space=pltpu.SMEM)] + [far] * 8,
        out_specs=[in_vmem] * 2,
        out_shape=[shape(rows // 2, width), shape(8, width)],
        scratch_shapes=[pltpu.VMEM((rows // 2, width), bf16)]
        + [pltpu.VMEM((width,), bf16)] * 7
        + [pltpu.SemaphoreType.DMA((8,))],
        compiler_params=pltpu.CompilerParams(vmem_limit_bytes=60 * 1024 * 1024),
        cost_estimate=pl.CostEstimate(flops=1024, bytes_accessed=1024, transcendentals=0),
        name="prepare",
    )(meta, o_weight, *vectors)


def widen_kernel(a_ref, b_ref, vec_ref, wide_ref):
    rows = a_ref.shape[0]
    step = 64

    @pl.loop(0, rows // step)
    def _(i):
        wide_ref[strip(i, step), :] = a_ref[strip(i, step), :].astype(f32)

    @pl.loop(0, b_ref.shape[0] // step)
    def _(i):
        wide_ref[strip(i + rows // step, step), :] = b_ref[strip(i, step), :].astype(f32)

    wide_ref[rows + b_ref.shape[0] :, :] = vec_ref[...]


def qkv_kernel(meta_ref, all_ref, qw_ref, kw_ref, vw_ref, *refs):
    given = refs[:2]
    vec_ref, local_ref, near_ref, far_ref, k_ref, v_ref, q_in, k_in, v_in, qb_in, vb_in, sems = refs[2:]
    half, wide = near_ref.shape
    rows = half // 2
    copies = Copies(sems)
    copies.start(given[0], qb_in)
    copies.start(given[1], vb_in)
    for p in range(4):
        copies.start(all_ref.at[strip(meta_ref[p], rows), :], local_ref.at[pl.ds(p * rows, rows), :])
    copies.start(kw_ref, k_in)
    copies.start(qw_ref, q_in)
    copies.start(vw_ref, v_in)
    copies.wait()
    k_ref[...] = dot_nn(local_ref[...], k_in[...]).astype(bf16)
    vec_ref[0, :] = qb_in[...].astype(f32)
    vec_ref[1, :] = vb_in[...].astype(f32)
    q = (dot_nn(local_ref[...], q_in[...]) + vec_ref[0:1, :]).astype(bf16)
    near_ref[...] = q[:half]
    far_ref[...] = q[half:]
    v_ref[...] = (dot_nn(local_ref[...], v_in[...]) + vec_ref[1:2, :]).astype(bf16)


def qkv(meta, tokens, weights, biases):
    rows, width = tokens.shape
    wide = weights[0].shape[1]
    far = pl.BlockSpec(memory_space=pltpu.HBM)
    return pl.pallas_call(
        qkv_kernel,
        in_specs=[pl.BlockSpec(memory_space=pltpu.SMEM)] + [far] * 6,
        out_specs=[in_vmem] * 6,
        out_shape=[shape(8, wide), shape(rows, width, bf16)]
        + [shape(rows // 2, wide, bf16)] * 2
        + [shape(rows, wide, bf16)] * 2,
        scratch_shapes=[pltpu.VMEM((width, wide), bf16)] * 3
        + [pltpu.VMEM((wide,), bf16)] * 2
        + [pltpu.SemaphoreType.DMA((9,))],
        compiler_params=pltpu.CompilerParams(vmem_limit_bytes=58 * 1024 * 1024),
        cost_estimate=pl.CostEstimate(flops=1024, bytes_accessed=1024, transcendentals=0),
        name="qkv",
    )(meta, tokens, *weights, *biases)[1:]


def add_kernel(*refs):
    step = 64

    @pl.loop(0, refs[0].shape[0] // step)
    def _(i):
        here = strip(i, step)
        total = refs[0][here, :]
        for ref in refs[1:-1]:
            total = total + ref[here, :]
        refs[-1][here, :] = total


def add(*values):
    return whole(add_kernel, "add", list(values), [shape(*values[0].shape)])[0]


def pair_kernel(side, fill, bit, meta_ref, left_ref, right_ref, *refs):
    mine = meta_ref[BITS + bit]
    half = left_ref.shape[1] // 2
    hidden = right_ref.shape[1] // 2
    right = right_ref[:, side * hidden : (side + 1) * hidden]
    for kept in range(2):
        start = pl.multiple_of((mine if kept else 1 - mine) * half, 128)
        value = dot_tn(left_ref[:, pl.ds(start, half)], right)
        if fill:
            refs[1 + kept][...] = value + refs[0][kept * half : (kept + 1) * half, :]
        else:
            refs[0][kept * half : (kept + 1) * half, :] = value


def fold_kernel(riders, ends, bit, meta_ref, total_ref, got_ref, *refs):
    rows = total_ref.shape[0]
    if riders:
        extra_ref = refs[0]
        refs = refs[1:]
        extra = extra_ref[...] + got_ref[rows:, :]
    if ends:
        refs[0][...] = total_ref[...] + got_ref[:rows, :]
        if riders:
            refs[1][...] = extra
        return
    half = rows // 2
    mine = meta_ref[BITS + bit]
    step = min(64, half)

    @pl.loop(0, half // step)
    def _(i):
        away = strip((1 - mine) * (half // step) + i, step)
        kept = strip(mine * (half // step) + i, step)
        refs[0][strip(i, step), :] = total_ref[away, :] + got_ref[away, :]
        refs[1][strip(i, step), :] = total_ref[kept, :] + got_ref[kept, :]

    if riders:
        refs[0][half:, :] = extra
        refs[2][...] = extra
    elif refs[0].shape[0] > half:
        refs[0][half:, :] = jnp.zeros((refs[0].shape[0] - half, refs[0].shape[1]), f32)


def qk_kernel(bit, meta_ref, left_ref, near_ref, far_ref, gk_ref, away_ref, kept_ref):
    mine = meta_ref[BITS + bit]
    half = left_ref.shape[1] // 2
    rows = near_ref.shape[0]
    wide = near_ref.shape[1]
    for kept, ref in enumerate((away_ref, kept_ref)):
        cols = pl.ds(pl.multiple_of((mine if kept else 1 - mine) * half, 128), half)
        ref[:, :wide] = dot_tn(left_ref[:rows, cols], near_ref[...]) + dot_tn(left_ref[rows:, cols], far_ref[...])
        ref[:, wide:] = dot_tn(left_ref[:, cols], gk_ref[...])


def vo_kernel(bit, meta_ref, left_ref, gv_ref, kept_o_ref, got_a_ref, got_b_ref, near_ref, far_ref, chip_ref, far_sums_ref, ub_ref, sib_ref, away_ref, kept_ref, extra_ref):
    mine = meta_ref[BITS + bit]
    half = left_ref.shape[1] // 2
    wide = gv_ref.shape[1]
    riders = chip_ref.shape[0]
    extra_ref[...] = jnp.zeros_like(extra_ref)
    shared = chip_ref[...] + far_sums_ref[far_sums_ref.shape[0] - riders :, :]
    extra_ref[: riders // 2, :wide] = shared[: riders // 2]
    extra_ref[: riders // 2, wide:] = shared[riders // 2 :]
    row = riders // 2
    ones = (jnp.sum(near_ref[...].astype(f32), axis=0, keepdims=True) + jnp.sum(far_ref[...].astype(f32), axis=0, keepdims=True))
    extra_ref[row : row + 1, :wide] = ones
    extra_ref[row : row + 1, wide:] = jnp.sum(gv_ref[...].astype(f32), axis=0, keepdims=True)
    place = sib_ref.shape[0] - 8
    for k in range(ub_ref.shape[1] // (2 * wide)):
        cols = slice(2 * k * wide, 2 * (k + 1) * wide)
        extra_ref[row + 1 + k : row + 2 + k, :] = ub_ref[:, cols] + sib_ref[place : place + 1, cols]
    for kept, ref in enumerate((away_ref, kept_ref)):
        start = pl.multiple_of((mine if kept else 1 - mine) * half, 128)
        ref[:half, :wide] = dot_tn(left_ref[:, pl.ds(start, half)], gv_ref[...])
        rows = pl.ds(start, half)
        top = jnp.where(start == 0, got_a_ref[...], got_b_ref[...])
        ref[:half, wide:] = kept_o_ref[rows, :] + top
    away_ref[half:, :] = extra_ref[...]


def o_kernel(cols_ref, other_ref, near_ref, first_ref, second_ref, kept_ref):
    half = first_ref.shape[0]
    first_ref[...] = dot_tn(cols_ref[:, :half], other_ref[...])
    second_ref[...] = dot_tn(cols_ref[:, half:], other_ref[...])
    kept_ref[...] = dot_tn(cols_ref[...], near_ref[...])


def round_kernel(wide_ref, a_ref, b_ref, vec_ref):
    rows = a_ref.shape[0]
    step = 64

    @pl.loop(0, rows // step)
    def _(i):
        a_ref[strip(i, step), :] = wide_ref[strip(i, step), :].astype(bf16)

    @pl.loop(0, b_ref.shape[0] // step)
    def _(i):
        b_ref[strip(i, step), :] = wide_ref[strip(i + rows // step, step), :].astype(bf16)

    vec_ref[...] = wide_ref[rows + b_ref.shape[0] :, :]


def feed_kernel(own, unit, blocks, targets, fresh, *refs):
    in_ref, up_ref, up2_ref, vec_ref, vec2_ref, down_ref, down2_ref = refs[:7]
    refs = refs[7 + (0 if fresh else 2) :]
    lo_full, act_full, slope_ref = refs[:3]
    parts = refs[3:-4]
    low_ref, act_ref, cols_ref, sems = refs[-4:]
    hidden = up_ref.shape[1]
    copies = Copies(sems)
    low_ref[...] = in_ref[...].astype(bf16)
    if blocks:
        move_columns(low_ref, cols_ref, blocks)
    else:
        cols_ref[...] = low_ref[...]
    for p, target in enumerate(targets):
        copies.start(cols_ref.at[pl.ds(p * unit, unit), :], lo_full.at[pl.ds(target * unit, unit), :])
    for side, (weight_ref, bias_ref) in enumerate(((up_ref, vec_ref), (up2_ref, vec2_ref))):

        @pl.loop(0, hidden // STRIP)
        def _(i):
            there = strip(i + side * (hidden // STRIP))
            pre = dot_nn(low_ref[...], weight_ref[:, strip(i)]) + bias_ref[UP_BIAS : UP_BIAS + 1, strip(i)]
            normal_cdf = 0.5 * (1.0 + lax.erf(pre * ROOT_HALF))
            density = jnp.exp(-0.5 * pre * pre) * INV_ROOT_TAU
            act_ref[:, there] = (pre * normal_cdf).astype(bf16)
            slope_ref[:, there] = normal_cdf + pre * density

    for p, target in enumerate(targets):
        copies.start(act_ref.at[pl.ds(p * unit, unit), :], act_full.at[pl.ds(target * unit, unit), :])

    @pl.loop(0, down_ref.shape[1] // STRIP)
    def _(i):
        cols = strip(i)
        part = dot_nn(act_ref[:, :hidden], down_ref[:, cols]) + dot_nn(act_ref[:, hidden:], down2_ref[:, cols])
        if own:
            part = part + (in_ref[:, cols] + vec_ref[DOWN_BIAS : DOWN_BIAS + 1, cols])
        for p, part_ref in enumerate(parts):
            part_ref[:, cols] = part[p * unit : (p + 1) * unit]

    copies.wait()


def feed(own, unit, blocks, targets, rows_in, ups, vectors, downs, filled):
    rows, width = rows_in.shape
    hidden = 2 * ups[0].shape[1]
    return whole(
        functools.partial(feed_kernel, own, unit, blocks, targets, not filled),
        "feed",
        [rows_in, *ups, *vectors, *downs],
        [shape(rows, hidden)] + [shape(unit, width)] * len(targets),
        filled=filled or [shape(4 * unit, width, bf16), shape(4 * unit, hidden, bf16)],
        scratch=[
            pltpu.VMEM((rows, width), bf16),
            pltpu.VMEM((rows, hidden), bf16),
            pltpu.VMEM((rows, width), bf16),
        ],
        sems=2 * len(targets),
    )


def back_kernel(own, blocks, offset, target, fresh, block, part, meta_ref, y_ref, og_ref, extra_ref, vec_ref, slope_ref, down_ref, down2_ref, up_ref, up2_ref, *refs):
    refs = refs[0 if fresh else 3 :]
    out_full, gf_full, gp_full, part_ref, ub_ref, mark_ref = refs[:6]
    refs = refs[6:]
    if own:
        two_ref, sums_ref = refs[:2]
        refs = refs[2:]
    gf_ref, out_ref, gp_ref, cols_ref, sems = refs
    rows = y_ref.shape[0]
    hidden = up_ref.shape[1]
    gain = row_of(vec_ref, GAIN_TWO)
    shift = row_of(vec_ref, SHIFT_TWO)
    copies = Copies(sems)
    ids = lax.broadcasted_iota(jnp.int32, (rows, 1), 0)
    number = meta_ref[block]
    base = pl.multiple_of((2 * number + part) * rows, rows)
    limit = meta_ref[LENGTH] - base
    spot = jnp.where(number < meta_ref[COUNT], meta_ref[MARKS + number] - base, -1)
    there = pl.ds(target * rows, rows)
    keep = (ids < limit).astype(f32)
    unit, scale_inv = norm_rows(y_ref[...])
    out_ref[...] = (unit * gain + shift) * keep
    copies.start(out_ref, out_full.at[there, :])
    grad_out = (og_ref[pl.ds(base, rows), :].astype(f32) + jnp.where(ids == spot, extra_ref[pl.ds(number, 1), :], 0.0)) * keep
    grad_two = norm_rows_back(grad_out, unit, scale_inv, gain)
    grad_low = grad_two.astype(bf16)
    gf_ref[...] = grad_low
    if own:
        two_ref[...] = grad_two
        sums_ref[0:1, :] = jnp.sum(grad_low.astype(f32), axis=0, keepdims=True)
        sums_ref[1:2, :] = jnp.sum(grad_out * unit, axis=0, keepdims=True)
        sums_ref[2:3, :] = jnp.sum(grad_out, axis=0, keepdims=True)
        sums_ref[3:8, :] = jnp.zeros((5, sums_ref.shape[1]), f32)
    mark_ref[...] = jnp.zeros_like(mark_ref)

    @pl.when((spot >= 0) & (spot < rows))
    def _():
        row, _ = norm_rows(y_ref[pl.ds(jnp.clip(spot, 0, rows - 1), 1), :])
        mark_ref[0:1, :] = row * gain + shift

    if blocks:
        move_columns(gf_ref, cols_ref, blocks)
    else:
        cols_ref[...] = gf_ref[...]
    copies.start(cols_ref, gf_full.at[there, :])
    for side, weight_ref in enumerate((down_ref, down2_ref)):

        @pl.loop(0, hidden // STRIP)
        def _(i):
            cols = strip(i + side * (hidden // STRIP))
            grad_act = dot_nt(gf_ref[...], weight_ref[strip(i), :])
            grad_pre = (grad_act * slope_ref[pl.ds(offset, rows), cols]).astype(bf16)
            gp_ref[:, cols] = grad_pre
            ub_ref[:, cols] = jnp.sum(grad_pre.astype(f32), axis=0, keepdims=True)

    copies.start(gp_ref, gp_full.at[there, :])

    @pl.loop(0, up_ref.shape[0] // STRIP)
    def _(i):
        cols = strip(i)
        part_ref[:, cols] = dot_nt(gp_ref[:, :hidden], up_ref[cols, :]) + dot_nt(gp_ref[:, hidden:], up2_ref[cols, :])

    copies.wait()


def back(own, blocks, offset, target, block, part, meta, y, out_grad, extra, vectors, slope, downs, ups, filled):
    rows, width = y.shape
    hidden = 2 * ups[0].shape[1]
    outputs = [shape(rows, width), shape(1, hidden), shape(8, width)]
    if own:
        outputs += [shape(rows, width), shape(8, width)]
    return whole(
        functools.partial(back_kernel, own, blocks, offset, target, not filled, block, part),
        "feed_back",
        [y, out_grad, extra, vectors, slope, *downs, *ups],
        outputs,
        scalars=meta,
        filled=filled
        or [shape(4 * rows, width), shape(4 * rows, width, bf16), shape(4 * rows, hidden, bf16)],
        scratch=[
            pltpu.VMEM((rows, width), bf16),
            pltpu.VMEM((rows, width), f32),
            pltpu.VMEM((rows, hidden), bf16),
            pltpu.VMEM((rows, width), bf16),
        ],
        sems=3,
    )


def context_back_kernel(blocks, own_ref, first_ref, sib_ref, near_w_ref, far_w_ref, far_ref, near_ref, sums_ref, *refs):
    low_ref = refs[-1]
    rows = own_ref.shape[0]
    low_ref[:rows, :] = own_ref[...]
    low_ref[rows:, :] = sib_ref[:rows, :].astype(bf16)
    wide = far_ref.shape[1]
    far_ref[: 2 * rows, :] = dot_nt(low_ref[...], far_w_ref[...])
    near_ref[...] = dot_nt(low_ref[...], near_w_ref[...]).astype(bf16)
    for k in range(first_ref.shape[1] // wide):
        cols = slice(k * wide, (k + 1) * wide)
        chip = first_ref[rows : rows + 8, cols] + sib_ref[rows : rows + 8, cols]
        sums_ref[8 * k : 8 * k + 8, :] = chip
        far_ref[2 * rows + 8 * k : 2 * rows + 8 * k + 8, :] = chip
    if blocks:
        move_columns(low_ref, refs[0], blocks)


def first_back_kernel(*refs):
    streams = (refs[:3], refs[3:6])
    chip_ref = refs[6]
    ub_refs = refs[7:11]
    marks = refs[11:15]
    unit_ref, inv_ref, vec_ref, first_ref, low_ref, ub_ref = refs[15:]
    hidden = ub_ref.shape[1]
    ub = ub_refs[0][...] + ub_refs[1][...] + ub_refs[2][...] + ub_refs[3][...]
    ub_ref[...] = ub[:, :hidden]
    gain = row_of(vec_ref, GAIN_ONE)
    size, width = streams[0][0].shape
    rows = 2 * size
    sums = [0.0] * 6
    for half, (two_ref, own_ref, ffn_ref) in enumerate(streams):
        here = pl.ds(half * size, size)
        grad_normed = two_ref[...] + own_ref[...]
        if half:
            grad_normed = grad_normed + chip_ref[...]
        unit = unit_ref[here, :]
        first = norm_rows_back(grad_normed, unit, inv_ref[here, 0:1], gain)
        low = first.astype(bf16)
        first_ref[here, :] = first
        low_ref[here, :] = low
        terms = [low.astype(f32), grad_normed * unit, grad_normed]
        for k in range(3):
            sums[k] = sums[k] + jnp.sum(terms[k], axis=0, keepdims=True)
            sums[k + 3] = sums[k + 3] + ffn_ref[k : k + 1, :]
    for k in range(6):
        first_ref[rows + k : rows + k + 1, :] = sums[k]
    first_ref[rows + 6 : rows + 8, :] = jnp.zeros((2, width), f32)
    first_ref[rows + 8 : rows + 9, :] = ub[:, hidden:]
    first_ref[rows + 9 : rows + 10, :] = marks[0][0:1, :] + marks[1][0:1, :]
    first_ref[rows + 10 : rows + 11, :] = marks[2][0:1, :] + marks[3][0:1, :]
    first_ref[rows + 11 : rows + 16, :] = jnp.zeros((5, width), f32)


def input_kernel(near_ref, far_ref, gk_ref, gv_ref, qw_ref, kw_ref, vw_ref, first_ref, mine_ref, away_ref):
    rows = near_ref.shape[0] // 2
    for p in range(4):
        gq_ref = (near_ref, far_ref)[p // 2]
        here = pl.ds(p * rows, rows)
        value = (
            dot_nt(gq_ref[pl.ds((p % 2) * rows, rows), :], qw_ref[...])
            + dot_nt(gk_ref[here, :], kw_ref[...])
            + dot_nt(gv_ref[here, :], vw_ref[...])
        )
        if p == 0:
            value = value + first_ref[:rows, :]
        (mine_ref, away_ref)[p % 2][pl.ds((p // 2) * rows, rows), :] = value


def chip_kernel(mine_ref, got_ref, keep_ref, send_ref):
    rows = mine_ref.shape[0] // 2
    step = 64

    @pl.loop(0, rows // step)
    def _(i):
        for p in range(2):
            here = strip(i + p * (rows // step), step)
            there = strip(i + (1 - p) * (rows // step), step)
            value = mine_ref[here, :] + got_ref[here, :]
            keep_ref[here, :] = value
            send_ref[there, :] = value


def place_kernel(meta_ref, mine_ref, other_ref, out_ref, sems):
    rows = mine_ref.shape[0] // 2
    copies = Copies(sems)
    for p, block in enumerate((0, 2, 1, 3)):
        ref = (mine_ref, other_ref)[p // 2]
        copies.start(ref.at[pl.ds((p % 2) * rows, rows), :], out_ref.at[strip(meta_ref[block], rows), :])
    copies.wait()


def round_place_kernel(meta_ref, near_ref, far_ref, out_ref, low_ref, sems):
    rows = near_ref.shape[0] // 2
    copies = Copies(sems)
    for p, block in enumerate((0, 2, 1, 3)):
        ref = (near_ref, far_ref)[p // 2]
        low_ref[p * rows : (p + 1) * rows, :] = ref[(p % 2) * rows : (p % 2 + 1) * rows, :].astype(bf16)
        copies.start(low_ref.at[pl.ds(p * rows, rows), :], out_ref.at[strip(meta_ref[block], rows), :])
    copies.wait()


def swap_core(value):
    return lax.ppermute(value, "mp", [(i, i ^ 1) for i in range(4)])


def swap_chip(value):
    return lax.ppermute(value, "mp", [(i, i ^ 2) for i in range(4)])


def gather_rows(own):
    other = swap_chip(own)
    sibling = swap_core(own)
    diagonal = swap_core(other)
    return own, sibling, other, diagonal


def bit_order_blocks(parts, order):
    bits = len(order)
    blocks = []
    for position in range(parts):
        block = 0
        for level, bit in enumerate(order):
            block |= ((position >> (bits - 1 - level)) & 1) << bit
        blocks.append(block)
    return blocks


def bit_order_columns(matrix, parts, order):
    width = matrix.shape[1] // parts
    return jnp.concatenate(
        [matrix[:, b * width : (b + 1) * width] for b in bit_order_blocks(parts, order)], axis=1
    )


def dp_swap(value, parts, bit):
    return lax.ppermute(value, "dp", [(i, i ^ (1 << bit)) for i in range(parts)])


class Sum:
    def __init__(self, parts, order, meta, line, spare=0):
        self.parts, self.order, self.meta, self.line = parts, list(order), meta, line
        self.spare = spare
        self.extra = self.total = self.got = None

    def begin(self, away, total, extra=None):
        self.total, self.extra = total, extra
        self.level = 0
        self.ship(away)

    def ship(self, away):
        self.got = dp_swap(away, self.parts, self.order[self.level])
        self.level += 1

    def step(self):
        if self.got is None:
            return
        got = self.line.hold(self.got)
        self.got = None
        rows, cols = self.total.shape
        ends = self.level == len(self.order)
        riders = 0 if self.extra is None else self.extra.shape[0]
        bit = 0 if ends else self.order[self.level]
        rest = [shape(riders, cols)] if riders else []
        outputs = [shape(rows, cols)]
        if not ends:
            outputs = [shape(rows // 2 + riders + self.spare, cols), shape(rows // 2, cols)]
        given = [self.total, got] + ([self.extra] if riders else [])
        result = whole(
            functools.partial(fold_kernel, riders, ends, bit), "fold", given, outputs + rest, scalars=self.meta
        )
        if riders:
            self.extra = result[-1]
        if ends:
            self.total = result[0]
            self.line.mark(self.total)
        else:
            self.total = result[1]
            self.ship(result[0])
            self.line.mark(result[0])

    def finish(self):
        while self.got is not None:
            self.step()
        return self.total


class Line:
    def __init__(self):
        self.token = None

    def mark(self, *values):
        self.token = values

    def hold(self, *values):
        if self.token is not None:
            values = lax.optimization_barrier(tuple(values) + self.token)[: len(values)]
        return values if len(values) > 1 else values[0]


def shards(
    dp_size,
    tokens,
    doc_lengths,
    cls_pos,
    cls_count,
    q_weight,
    q_bias,
    k_weight,
    v_weight,
    v_bias,
    o_weight,
    o_bias,
    ln1_gain,
    ln1_bias,
    up_weight,
    up_bias,
    down_weight,
    down_bias,
    ln2_gain,
    ln2_bias,
    out_grad,
    pooled_grad,
):
    slot_len, width = tokens.shape
    rows = slot_len // 4
    half = 2 * rows
    head_width = q_weight.shape[1]
    rank = lax.axis_index("mp")
    place_id = lax.axis_index("dp")
    bits = dp_size.bit_length() - 1
    order_a = list(range(bits))
    order_b = [1, 0] + list(range(2, bits)) if bits > 1 else order_a
    length = doc_lengths[0]
    blocks = [rank ^ j for j in range(4)]

    line = Line()
    sizes = width // dp_size
    fixed_a = bit_order_blocks(dp_size, order_a) if sizes % 128 == 0 else None
    fixed_b = bit_order_blocks(dp_size, order_b) if sizes % 128 == 0 else None
    unit = rows // 2

    row_ids = lax.iota(jnp.int32, rows)
    positions = jnp.concatenate([row_ids + blocks[j] * rows for j in range(4)])
    bias = jnp.where(positions < length, 0.0, MASKED).astype(f32)[None, :]
    meta = jnp.concatenate(
        [
            jnp.stack(blocks).astype(jnp.int32),
            doc_lengths,
            cls_count,
            cls_pos[0],
            jnp.stack([(place_id >> bit) & 1 for bit in range(max(bits, 1))]).astype(jnp.int32),
        ]
    )
    hidden = up_bias.shape[0]

    meta, bias = lax.optimization_barrier((meta, bias))

    o_part, vectors = prepare(
        meta, o_weight, [o_bias, ln1_gain, ln1_bias, ln2_gain, ln2_bias, down_bias, up_bias]
    )
    o_got = swap_chip(o_part)
    line.mark(o_part)
    local, queries_near, queries_far, key_rows, value_rows = qkv(
        meta, line.hold(tokens), (q_weight, k_weight, v_weight), (q_bias, v_bias)
    )
    away_context, lse_far = attn_fwd(queries_far, key_rows, value_rows, bias, 256, f32)
    arrived = swap_chip(away_context)
    line.mark(away_context)
    o_got = line.hold(o_got)
    o_other = dp_swap(o_got, dp_size, 0)
    line.mark(o_got)
    up_held, down_held = line.hold(up_weight, down_weight)
    wide = whole(
        widen_kernel,
        "widen",
        [up_held, down_held, vectors],
        [shape(width + hidden + 8, width)],
        limit=20,
    )[0]
    line.mark(wide)
    wide = swap_core(wide)
    context_near, lse_near = attn_fwd(line.hold(queries_near), key_rows, value_rows, bias, 256, bf16)
    line.mark(context_near)
    if fixed_a:
        local_a, local_b = whole(
            functools.partial(order_kernel, fixed_a, fixed_b),
            "order",
            [line.hold(local)],
            [shape(slot_len, width, bf16)] * 2,
        )
    else:
        local_a = bit_order_columns(local, dp_size, order_a)
        local_b = bit_order_columns(local, dp_size, order_b)
    line.mark(local_a)
    own, sib, context_other, o_far = whole(
        project_kernel,
        "project",
        [context_near, line.hold(arrived), o_weight, o_got, line.hold(o_other)],
        [shape(rows, width), shape(rows, width), shape(half, head_width, bf16), shape(head_width, width, bf16)],
        scalars=meta,
    )
    n_a, n_b, normed, unit_one, inv_one = whole(
        first_norm_kernel,
        "first_norm",
        [own, swap_core(sib), local, vectors],
        [shape(unit, width), shape(unit, width), shape(rows, width), shape(rows, width), shape(rows, 128)],
    )
    line.mark(n_a)
    chip_a = swap_chip(n_a)
    chip_b = swap_chip(n_b)
    up_far, down_far, vectors_far = whole(
        round_kernel,
        "round",
        [line.hold(wide)],
        [shape(width, hidden, bf16), shape(hidden, width, bf16), shape(8, width)],
        limit=20,
    )
    ups = (up_weight, up_far)
    downs = (down_weight, down_far)
    both = (vectors, vectors_far)
    lo, act, slope_near, own_a, own_b = feed(True, unit, fixed_b, (0, 1), normed, ups, both, downs, ())
    line.mark(own_a)
    lo, act, slope_a, part = feed(
        False, unit, fixed_b, (2,), line.hold(chip_a), ups, both, downs, (lo, act)
    )
    got_a = swap_chip(part)
    line.mark(part)
    lo, act, slope_b, part = feed(
        False, unit, fixed_b, (3,), line.hold(chip_b), ups, both, downs, (lo, act)
    )
    got_b = swap_chip(part)
    line.mark(part)

    def back_rows(own, k, y, slope, offset, filled):
        place = k if own else 2 + k
        return back(
            own, fixed_a, offset, place, 0 if own else 2, k, meta, y, out_grad, pooled_grad[0], vectors,
            slope, downs, ups, filled,
        )

    y_a = add(own_a, line.hold(got_a))
    chip_a = swap_chip(y_a)
    *filled, back_a, ub_a, mark_a, two_a, sums_a = back_rows(True, 0, y_a, slope_near, 0, ())
    line.mark(back_a)
    y_b = add(own_b, line.hold(got_b))
    chip_b = swap_chip(y_b)
    *filled, back_b, ub_b, mark_b, two_b, sums_b = back_rows(True, 1, y_b, slope_near, unit, filled)
    line.mark(back_b)
    *filled, part, ub_c, mark_c = back_rows(False, 0, line.hold(chip_a), slope_a, 0, filled)
    got_a = swap_chip(part)
    line.mark(part)
    *filled, part, ub_d, mark_d = back_rows(False, 1, line.hold(chip_b), slope_b, 0, filled)
    got_b = swap_chip(part)
    line.mark(part)
    back_a = add(back_a, line.hold(got_a))
    line.mark(back_a)
    out_wide, grad_fed, grad_pre = filled

    def in_order(value, fixed, order):
        return value if fixed else bit_order_columns(value, dp_size, order)

    gf_cols, lo_cols = in_order(grad_fed, fixed_a, order_a), in_order(lo, fixed_b, order_b)
    down_sum = Sum(dp_size, order_a, meta, line, 16)
    up_sum = Sum(dp_size, order_b, meta, line, 16)

    def pair(side, sum_of, left, right, given=()):
        half_rows = width // 2
        return whole(
            functools.partial(pair_kernel, side, bool(given), sum_of.order[0]),
            "pair",
            [left, right, *given],
            [shape(half_rows, hidden)] * 2 if given else [shape(width, hidden)],
            scalars=meta,
        )

    down_other = pair(1, down_sum, line.hold(gf_cols), act)[0]
    down_given = swap_core(down_other)
    line.mark(down_other)
    up_other = pair(1, up_sum, lo_cols, line.hold(grad_pre))[0]
    up_given = swap_core(up_other)
    line.mark(up_other)

    down_sum.begin(*pair(0, down_sum, gf_cols, act, [line.hold(down_given)]))
    up_sum.begin(*pair(0, up_sum, lo_cols, grad_pre, [line.hold(up_given)]))

    line.mark(down_sum.total, up_sum.total)
    got_b = line.hold(got_b)
    first_ext, grad_attended_own, up_bias_own = whole(
        first_back_kernel,
        "first_norm_back",
        [two_a, back_a, sums_a, two_b, back_b, sums_b, got_b, ub_a, ub_b, ub_c, ub_d]
        + [mark_a, mark_b, mark_c, mark_d, unit_one, inv_one, vectors],
        [shape(rows + 16, width), shape(rows, width, bf16), shape(1, hidden)],
    )
    sib_ext = swap_core(first_ext)
    riders = 8 * width // head_width
    context_far_grad, grad_context_near, chip_sums, *ga_cols = whole(
        functools.partial(context_back_kernel, fixed_b),
        "context_back",
        [grad_attended_own, first_ext, sib_ext, o_weight, o_far],
        [shape(half + riders, head_width), shape(half, head_width, bf16), shape(riders, head_width)]
        + [shape(half, width, bf16)] * (2 if fixed_b else 1),
    )
    ga_cols = in_order(ga_cols[0], fixed_b, order_b)
    grad_context_far = swap_chip(context_far_grad)
    line.mark(context_far_grad)
    *o_away, o_kept = whole(
        o_kernel,
        "o_grad",
        [line.hold(ga_cols), context_other, context_near],
        [shape(width // 2, head_width)] * 2 + [shape(width, head_width)],
    )
    o_got = [swap_chip(v) for v in o_away]
    line.mark(o_kept)

    queries_near = line.hold(queries_near)
    grad_q_near, key_sum, value_sum = attn_bwd(
        queries_near, grad_context_near, key_rows, value_rows, bias, lse_near, 256
    )
    line.mark(grad_q_near)
    grad_context_far = line.hold(grad_context_far)
    line.mark(grad_context_far)
    queries_far = line.hold(queries_far)
    grad_q_far, grad_k, grad_v = attn_bwd(
        queries_far, grad_context_far, key_rows, value_rows, bias, lse_far, 256, (key_sum, value_sum)
    )
    line.mark(grad_k)

    qk_sum = Sum(dp_size, order_a, meta, line)
    vo_sum = Sum(dp_size, order_b, meta, line)
    qk_away, qk_kept = whole(
        functools.partial(qk_kernel, qk_sum.order[0]),
        "qk_grad",
        [local_a, line.hold(grad_q_near), grad_q_far, grad_k],
        [shape(width // 2, 2 * head_width)] * 2,
        scalars=meta,
    )
    line.mark(qk_away)
    riders = 8 * width // head_width
    extra_rows = -(-(riders // 2 + 1 + hidden // (2 * head_width)) // 8) * 8
    o_got = line.hold(*o_got)
    line.mark(*o_got)
    in_mine, in_away = whole(
        input_kernel,
        "input_grad",
        [line.hold(grad_q_near), grad_q_far, grad_k, grad_v, q_weight, k_weight, v_weight, first_ext],
        [shape(half, width)] * 2,
    )
    in_got = swap_core(in_away)
    line.mark(in_mine)
    down_sum.step()
    up_sum.step()
    qk_sum.begin(qk_away, qk_kept)
    in_kept, in_sent = whole(
        chip_kernel, "chip_sum", [in_mine, line.hold(in_got)], [shape(half, width)] * 2
    )
    in_got = swap_chip(in_sent)
    line.mark(in_sent)
    vo_away, vo_kept, vo_extra = whole(
        functools.partial(vo_kernel, vo_sum.order[0]),
        "vo_grad",
        [local_b, line.hold(grad_v), o_kept, *o_got, grad_q_near, grad_q_far, chip_sums, grad_context_far]
        + [up_bias_own, sib_ext],
        [
            shape(width // 2 + extra_rows, 2 * head_width),
            shape(width // 2, 2 * head_width),
            shape(extra_rows, 2 * head_width),
        ],
        scalars=meta,
    )
    vo_sum.begin(vo_away, vo_kept, vo_extra)
    line.mark(vo_away)
    for bit in range(bits):
        down_sum.step()
        up_sum.step()
        qk_sum.step()
        vo_sum.step()
        if bit == min(1, bits - 1):
            in_final = add(in_kept, line.hold(in_got))
            in_other = swap_core(in_final)
            out_far = swap_core(line.hold(out_wide))
            line.mark(in_final)
            in_grad = whole(
                place_kernel,
                "place",
                [in_final, line.hold(in_other)],
                [],
                scalars=meta,
                filled=[shape(slot_len, width)],
                sems=4,
                far=True,
            )[0]
            line.mark(in_grad)
            out = whole(
                round_place_kernel,
                "round_place",
                [out_wide, line.hold(out_far)],
                [],
                scalars=meta,
                filled=[shape(slot_len, width, bf16)],
                scratch=[pltpu.VMEM((slot_len, width), bf16)],
                sems=4,
                far=True,
            )[0]
            line.mark(out)
    qk_sum, vo_total = qk_sum.finish(), vo_sum.finish()
    riding = vo_sum.extra
    row = riders // 2
    shared = jnp.concatenate([riding[:row, :head_width], riding[:row, head_width:]], axis=0)
    shared = shared.reshape(-1, 8, head_width).transpose(1, 0, 2).reshape(8, width)
    biases = riding[row].reshape(2, head_width)
    up_bias_sum = riding[row + 1 : row + 1 + hidden // (2 * head_width)].reshape(-1)
    v_sum = vo_total[:, :head_width]
    o_sum = vo_total[:, head_width:].T
    down_sum = down_sum.finish().T
    up_sum = up_sum.finish()

    mine = first_ext[rows + 9 : rows + 11]
    theirs = sib_ext[rows + 9 : rows + 11]
    marks = jnp.concatenate([mine[:1], theirs[:1], mine[1:], theirs[1:]], axis=0)
    pooled = jnp.concatenate(
        [lax.dynamic_index_in_dim(marks, blocks[j], keepdims=True) for j in range(4)], axis=0
    )[None]
    return (
        out,
        pooled,
        in_grad,
        qk_sum[:, :head_width],
        biases[0],
        qk_sum[:, head_width:],
        v_sum,
        biases[1],
        o_sum,
        shared[0],
        shared[1],
        shared[2],
        up_sum,
        up_bias_sum,
        down_sum,
        shared[3],
        shared[4],
        shared[5],
    )


def solution(mesh):
    return jax.shard_map(
        functools.partial(shards, mesh.shape["dp"]),
        mesh=mesh,
        in_specs=(
            P("dp", None),
            P("dp"),
            P("dp", None),
            P("dp"),
            P(None, "mp"),
            P("mp"),
            P(None, "mp"),
            P(None, "mp"),
            P("mp"),
            P("mp", None),
            P(),
            P(),
            P(),
            P(None, "mp"),
            P("mp"),
            P("mp", None),
            P(),
            P(),
            P(),
            P("dp", None),
            P("dp", None, None),
        ),
        out_specs=(
            P("dp", None),
            P("dp", None, None),
            P("dp", None),
            P("dp", "mp"),
            P("mp"),
            P("dp", "mp"),
            P("dp", "mp"),
            P("mp"),
            P("mp", "dp"),
            P(),
            P(),
            P(),
            P("dp", "mp"),
            P("mp"),
            P("mp", "dp"),
            P(),
            P(),
            P(),
        ),
        check_vma=False,
    )
```

profile of v0, /device:TPU:0, one launch (start us, length us, event | category | flops | bytes accessed | tf_op | source)
XLA Modules:
  0.0 324.1 jit_solution(3453319236507064974)
XLA Ops:
  8.9 5.6 %qkv.1 = (f32[8,256]{1,0:T(8,128)}, bf16[1024,1024]{1,0:T(8,128)(2,1)}, bf16[512,256]{1,0:T(8,128)(2,1)}, bf16[512,256]{1,0:T(8,128)(2,1)}, bf16[1024,256]{1,0:T(8,128)(2,1)}, /*index=5*/bf16[1024,256]{1,0:T(8,128)(2,1)}) custom-call(s32[13]{0:T(128)} %concatenate.30.meta_ref, bf16[1024,1024]{1,0:T(8,128)(2,1)} %all_ref, bf16[1024,256]{1,0:T(8,128)(2,1)} %qw_ref.3, ...), custom_call_target="tpu_custom_call" | custom-call | flops 1024 | bytes 1024 | tf_op jit(solution)/shard_map/qkv/pallas_call | solution.py:342
  17.5 4.1 %attn_fwd.2 = (f32[512,256]{1,0:T(8,128)S(1)}, f32[512,128]{1,0:T(8,128)S(1)}) custom-call(bf16[512,256]{1,0:T(8,128)(2,1)S(1)} %copy-done.16, bf16[1024,256]{1,0:T(8,128)(2,1)S(1)} %copy-done.3, bf16[1024,256]{1,0:T(8,128)(2,1)S(1)} %copy-done.5, f32[1,1024]{1,0:T(1,128)S(1)} %compare_select_fusion.bias_ref.refs_4_), custom_call_target="tpu_custom_call" | custom-call | flops 1024 | bytes 1024 | tf_op jit(solution)/shard_map/attn_fwd/pallas_call | solution.py:64
  25.9 4.1 %attn_fwd.3 = (bf16[512,256]{1,0:T(8,128)(2,1)S(1)}, f32[512,128]{1,0:T(8,128)S(1)}) custom-call(bf16[512,256]{1,0:T(8,128)(2,1)S(1)} %copy-done.18, bf16[1024,256]{1,0:T(8,128)(2,1)S(1)} %copy-done.3, bf16[1024,256]{1,0:T(8,128)(2,1)S(1)} %copy-done.5, f32[1,1024]{1,0:T(1,128)S(1)} %compare_select_fusion.bias_ref.refs_4_), custom_call_target="tpu_custom_call" | custom-call | flops 1024 | bytes 1024 | tf_op jit(solution)/shard_map/attn_fwd/pallas_call | solution.py:64
  30.8 6.7 %collective-permute-done.1.other_ref = f32[512,256]{1,0:T(8,128)S(1)} collective-permute-done((f32[512,256]{1,0:T(8,128)S(1)}, f32[512,256]{1,0:T(8,128)S(1)}, u32[]{:S(2)}, u32[]{:S(2)}) %collective-permute-start.1) | collective-permute-done | bytes 524320 | tf_op jit(solution)/shard_map/ppermute | solution.py:730
  45.5 5.2 %feed.3 = (bf16[512,1024]{1,0:T(8,128)(2,1)S(1)}, bf16[512,2048]{1,0:T(8,128)(2,1)S(1)}, f32[256,2048]{1,0:T(8,128)S(1)}, f32[128,1024]{1,0:T(8,128)S(1)}, f32[128,1024]{1,0:T(8,128)S(1)}) custom-call(f32[256,1024]{1,0:T(8,128)S(1)} %get-tuple-element.204.refs_0_, bf16[1024,1024]{1,0:T(8,128)(2,1)S(1)} %copy-done, ...), custom_call_target="tpu_custom_call" | custom-call | flops 1024 | bytes 1024 | tf_op jit(solution)/shard_map/feed/pallas_call | solution.py:184
  50.8 7.0 %collective-permute-done.6.refs_0_ = f32[128,1024]{1,0:T(8,128)S(1)} collective-permute-done((f32[128,1024]{1,0:T(8,128)S(1)}, f32[128,1024]{1,0:T(8,128)S(1)}, u32[]{:S(2)}, u32[]{:S(2)}) %collective-permute-start.6) | collective-permute-done | bytes 524320 | tf_op jit(solution)/shard_map/ppermute | solution.py:730
  57.7 3.8 %feed.4 = (bf16[512,1024]{1,0:T(8,128)(2,1)S(1)}, bf16[512,2048]{1,0:T(8,128)(2,1)S(1)}, f32[128,2048]{1,0:T(8,128)S(1)}, f32[128,1024]{1,0:T(8,128)S(1)}) custom-call(f32[128,1024]{1,0:T(8,128)S(1)} %collective-permute-done.6.refs_0_, bf16[1024,1024]{1,0:T(8,128)(2,1)S(1)} %copy-done, ...), custom_call_target="tpu_custom_call", output_to_operand_aliasing={{0}: (7, {}), {1}: (8, {})} | custom-call | flops 1024 | bytes 1024 | tf_op jit(solution)/shard_map/feed/pallas_call | solution.py:184
  62.5 6.4 %collective-permute-done.5.refs_0_ = f32[128,1024]{1,0:T(8,128)S(1)} collective-permute-done((f32[128,1024]{1,0:T(8,128)S(1)}, f32[128,1024]{1,0:T(8,128)S(1)}, u32[]{:S(2)}, u32[]{:S(2)}) %collective-permute-start.5) | collective-permute-done | bytes 524320 | tf_op jit(solution)/shard_map/ppermute | solution.py:730
  69.0 3.8 %feed.5 = (bf16[512,1024]{1,0:T(8,128)(2,1)S(1)}, bf16[512,2048]{1,0:T(8,128)(2,1)S(1)}, f32[128,2048]{1,0:T(8,128)S(1)}, f32[128,1024]{1,0:T(8,128)S(1)}) custom-call(f32[128,1024]{1,0:T(8,128)S(1)} %collective-permute-done.5.refs_0_, bf16[1024,1024]{1,0:T(8,128)(2,1)S(1)} %copy-done, ...), custom_call_target="tpu_custom_call", output_to_operand_aliasing={{0}: (7, {}), {1}: (8, {})} | custom-call | flops 1024 | bytes 1024 | tf_op jit(solution)/shard_map/feed/pallas_call | solution.py:184
  73.8 6.4 %collective-permute-done.8.refs_1_ = f32[128,1024]{1,0:T(8,128)S(1)} collective-permute-done((f32[128,1024]{1,0:T(8,128)S(1)}, f32[128,1024]{1,0:T(8,128)S(1)}, u32[]{:S(2)}, u32[]{:S(2)}) %collective-permute-start.8) | collective-permute-done | bytes 524320 | tf_op jit(solution)/shard_map/ppermute | solution.py:730
  81.3 6.0 %feed_back.4 = (f32[512,1024]{1,0:T(8,128)}, bf16[512,1024]{1,0:T(8,128)(2,1)S(1)}, bf16[512,2048]{1,0:T(8,128)(2,1)S(1)}, f32[128,1024]{1,0:T(8,128)S(1)}, f32[...) custom-call(s32[13]{0:T(128)S(1)} %copy-done.19, ...), custom_call_target="tpu_custom_call" | custom-call | flops 1024 | bytes 1024 | tf_op jit(solution)/shard_map/feed_back/pallas_call | solution.py:184
  87.2 4.2 %collective-permute-done.7.refs_1_ = f32[128,1024]{1,0:T(8,128)S(1)} collective-permute-done((f32[128,1024]{1,0:T(8,128)S(1)}, f32[128,1024]{1,0:T(8,128)S(1)}, u32[]{:S(2)}, u32[]{:S(2)}) %collective-permute-start.7) | collective-permute-done | bytes 524320 | tf_op jit(solution)/shard_map/ppermute | solution.py:730
  92.5 6.0 %feed_back.5 = (f32[512,1024]{1,0:T(8,128)}, bf16[512,1024]{1,0:T(8,128)(2,1)S(1)}, bf16[512,2048]{1,0:T(8,128)(2,1)S(1)}, f32[128,1024]{1,0:T(8,128)S(1)}, f32[...) custom-call(s32[13]{0:T(128)S(1)} %copy-done.19, ...), custom_call_target="tpu_custom_call", output_to_operand_aliasing={{0}: (10, {}), {1}: (11, {}), {2}: (12, {})} | custom-call | flops 1024 | bytes 1024 | tf_op jit(solution)/shard_map/feed_back/pallas_call | solution.py:184
  98.5 4.2 %collective-permute-done.10.y_ref = f32[128,1024]{1,0:T(8,128)S(1)} collective-permute-done((f32[128,1024]{1,0:T(8,128)S(1)}, f32[128,1024]{1,0:T(8,128)S(1)}, u32[]{:S(2)}, u32[]{:S(2)}) %collective-permute-start.10) | collective-permute-done | bytes 524320 | tf_op jit(solution)/shard_map/ppermute | solution.py:730
  102.7 5.7 %feed_back.6 = (f32[512,1024]{1,0:T(8,128)}, bf16[512,1024]{1,0:T(8,128)(2,1)S(1)}, bf16[512,2048]{1,0:T(8,128)(2,1)S(1)}, f32[128,1024]{1,0:T(8,128)S(1)}, f32[...) custom-call(s32[13]{0:T(128)S(1)} %copy-done.19, ...), custom_call_target="tpu_custom_call", output_to_operand_aliasing={{0}: (10, {}), {1}: (11, {}), {2}: (12, {})} | custom-call | flops 1024 | bytes 1024 | tf_op jit(solution)/shard_map/feed_back/pallas_call | solution.py:184
  109.4 4.5 %collective-permute-done.9.y_ref = f32[128,1024]{1,0:T(8,128)S(1)} collective-permute-done((f32[128,1024]{1,0:T(8,128)S(1)}, f32[128,1024]{1,0:T(8,128)S(1)}, u32[]{:S(2)}, u32[]{:S(2)}) %collective-permute-start.9) | collective-permute-done | bytes 524320 | tf_op jit(solution)/shard_map/ppermute | solution.py:730
  113.9 5.9 %feed_back.7 = (f32[512,1024]{1,0:T(8,128)}, bf16[512,1024]{1,0:T(8,128)(2,1)S(1)}, bf16[512,2048]{1,0:T(8,128)(2,1)S(1)}, f32[128,1024]{1,0:T(8,128)S(1)}, f32[...) custom-call(s32[13]{0:T(128)S(1)} %copy-done.19, ...), custom_call_target="tpu_custom_call", output_to_operand_aliasing={{0}: (10, {}), {1}: (11, {}), {2}: (12, {})} | custom-call | flops 1024 | bytes 1024 | tf_op jit(solution)/shard_map/feed_back/pallas_call | solution.py:184
  119.8 4.6 %collective-permute-done.11.refs_1_ = f32[128,1024]{1,0:T(8,128)S(1)} collective-permute-done((f32[128,1024]{1,0:T(8,128)S(1)}, f32[128,1024]{1,0:T(8,128)S(1)}, u32[]{:S(2)}, u32[]{:S(2)}) %collective-permute-start.11) | collective-permute-done | bytes 524320 | tf_op jit(solution)/shard_map/ppermute | solution.py:730
  129.6 3.8 %collective-permute-done.13.refs_0_ = f32[1024,1024]{1,0:T(8,128)S(1)} collective-permute-done((f32[1024,1024]{1,0:T(8,128)S(1)}, f32[1024,1024]{1,0:T(8,128)S(1)}, u32[]{:S(2)}, u32[]{:S(2)}) %collective-permute-start.13) | collective-permute-done | bytes 4194336 | tf_op jit(solution)/shard_map/ppermute | solution.py:726
  135.3 4.2 %collective-permute-done.14.refs_0_ = f32[1024,1024]{1,0:T(8,128)S(1)} collective-permute-done((f32[1024,1024]{1,0:T(8,128)S(1)}, f32[1024,1024]{1,0:T(8,128)S(1)}, u32[]{:S(2)}, u32[]{:S(2)}) %collective-permute-start.14) | collective-permute-done | bytes 4194336 | tf_op jit(solution)/shard_map/ppermute | solution.py:726
  154.8 9.6 %attn_bwd.2 = (bf16[512,256]{1,0:T(8,128)(2,1)S(1)}, f32[1024,256]{1,0:T(8,128)S(1)}, f32[1024,256]{1,0:T(8,128)S(1)}) custom-call(bf16[512,256]{1,0:T(8,128)(2,1)S(1)} %copy-done.18, bf16[512,256]{1,0:T(8,128)(2,1)S(1)} %get-tuple-element.278.refs_1_, bf16[1024,256]{1,0:T(8,128)(2,1)S(1)} %copy-done.4, bf16[1024,256]{1,0:T(8,128)(2,1)S(1)} %copy-done.6, ...), custom_call_target="tpu_custom_call" | custom-call | flops 1024 | bytes 1024 | tf_op jit(solution)/shard_map/attn_bwd/pallas_call | solution.py:135
  164.4 9.8 %attn_bwd.3 = (bf16[512,256]{1,0:T(8,128)(2,1)S(1)}, bf16[1024,256]{1,0:T(8,128)(2,1)S(1)}, bf16[1024,256]{1,0:T(8,128)(2,1)S(1)}) custom-call(bf16[512,256]{1,0:T(8,128)(2,1)S(1)} %copy-done.17, f32[544,256]{1,0:T(8,128)S(1)} %collective-permute-done.16.refs_1_.far_sums_ref, bf16[1024,256]{1,0:T(8,128)(2,1)S(1)} %copy-done.4, ...), custom_call_target="tpu_custom_call" | custom-call | flops 1024 | bytes 1024 | tf_op jit(solution)/shard_map/attn_bwd/pallas_call | solution.py:135
  176.2 8.9 %collective-permute-done.18.got_b_ref = f32[512,256]{1,0:T(8,128)S(1)} collective-permute-done((f32[512,256]{1,0:T(8,128)S(1)}, f32[512,256]{1,0:T(8,128)S(1)}, u32[]{:S(2)}, u32[]{:S(2)}) %collective-permute-start.18) | collective-permute-done | bytes 524320 | tf_op jit(solution)/shard_map/ppermute | solution.py:730
  187.0 12.9 %collective-permute-done.21.got_ref = f32[512,1024]{1,0:T(8,128)S(1)} collective-permute-done((f32[512,1024]{1,0:T(8,128)S(1)}, f32[512,1024]{1,0:T(8,128)S(1)}, u32[]{:S(2)}, u32[]{:S(2)}) %collective-permute-start.21) | collective-permute-done | bytes 2097184 | tf_op jit(solution)/shard_map/ppermute | solution.py:759
  208.7 34.4 %collective-permute-done.25.got_ref = f32[272,1024]{1,0:T(8,128)S(1)} collective-permute-done((f32[272,1024]{1,0:T(8,128)S(1)}, f32[272,1024]{1,0:T(8,128)S(1)}, u32[]{:S(2)}, u32[]{:S(2)}) %collective-permute-start.25) | collective-permute-done | bytes 1114144 | tf_op jit(solution)/shard_map/ppermute | solution.py:759
  250.5 17.4 %collective-permute-done.22.got_ref = f32[536,512]{1,0:T(8,128)S(1)} collective-permute-done((f32[536,512]{1,0:T(8,128)S(1)}, f32[536,512]{1,0:T(8,128)S(1)}, u32[]{:S(2)}, u32[]{:S(2)}) %collective-permute-start.22) | collective-permute-done | bytes 1097760 | tf_op jit(solution)/shard_map/ppermute | solution.py:759
  270.2 8.3 %collective-permute-done.29.got_ref = f32[144,1024]{1,0:T(8,128)S(1)} collective-permute-done((f32[144,1024]{1,0:T(8,128)S(1)}, f32[144,1024]{1,0:T(8,128)S(1)}, u32[]{:S(2)}, u32[]{:S(2)}) %collective-permute-start.29) | collective-permute-done | bytes 589856 | tf_op jit(solution)/shard_map/ppermute | solution.py:759
  279.9 6.4 %collective-permute-done.28.got_ref = f32[144,1024]{1,0:T(8,128)S(1)} collective-permute-done((f32[144,1024]{1,0:T(8,128)S(1)}, f32[144,1024]{1,0:T(8,128)S(1)}, u32[]{:S(2)}, u32[]{:S(2)}) %collective-permute-start.28) | collective-permute-done | bytes 589856 | tf_op jit(solution)/shard_map/ppermute | solution.py:759
  298.0 3.6 %place.1 = f32[1024,1024]{1,0:T(8,128)} custom-call(s32[13]{0:T(128)S(1)} %copy-done.19, f32[512,1024]{1,0:T(8,128)S(1)} %add.94.mine_ref, f32[512,1024]{1,0:T(8,128)} %collective-permute-done.32.other_ref), custom_call_target="tpu_custom_call" | custom-call | flops 1024 | bytes 1024 | tf_op jit(solution)/shard_map/place/pallas_call | solution.py:184
  301.6 3.7 %round_place.1 = bf16[1024,1024]{1,0:T(8,128)(2,1)} custom-call(s32[13]{0:T(128)S(1)} %copy-done.19, f32[512,1024]{1,0:T(8,128)} %get-tuple-element.334.near_ref, f32[512,1024]{1,0:T(8,128)} %collective-permute-done.30.far_ref), custom_call_target="tpu_custom_call" | custom-call | flops 1024 | bytes 1024 | tf_op jit(solution)/shard_map/round_place/pallas_call | solution.py:184
  305.3 8.4 %collective-permute-done.33.got_ref = f32[128,512]{1,0:T(8,128)S(1)} collective-permute-done((f32[128,512]{1,0:T(8,128)}, f32[128,512]{1,0:T(8,128)S(1)}, u32[]{:S(2)}, u32[]{:S(2)}) %collective-permute-start.33) | collective-permute-done | bytes 262176 | tf_op jit(solution)/shard_map/ppermute | solution.py:759
  315.0 5.3 %collective-permute-done.34.got_ref = f32[152,512]{1,0:T(8,128)S(1)} collective-permute-done((f32[152,512]{1,0:T(8,128)}, f32[152,512]{1,0:T(8,128)S(1)}, u32[]{:S(2)}, u32[]{:S(2)}) %collective-permute-start.34) | collective-permute-done | bytes 311328 | tf_op jit(solution)/shard_map/ppermute | solution.py:759
  (156 shorter events, 90.8 us)
Async XLA Ops:
  5.9 15.8 %collective-permute-start = (f32[128,1024]{1,0:T(8,128)}, f32[128,1024]{1,0:T(8,128)S(1)}, u32[]{:S(2)}, u32[]{:S(2)}) collective-permute-start(f32[128,1024]{1,0:T(8,128)} %get-tuple-element.183), channel_id=1, source_target_pairs={{0,2},{1,3},{2,0},{3,1},{4,6},{5,7},{6,4},{7,5},{8,10},{9,11},{10,... | collective-permute-start | bytes 1572872 | tf_op jit(solution)/shard_map/ppermute | solution.py:730
  23.1 21.9 %collective-permute-start.4 = (f32[2056,1024]{1,0:T(8,128)S(1)}, f32[2056,1024]{1,0:T(8,128)S(1)}, u32[]{:S(2)}, u32[]{:S(2)}) collective-permute-start(f32[2056,1024]{1,0:T(8,128)S(1)} %widen.1), channel_id=1, source_target_pairs={{0,1},{1,0},{2,3},{3,2},{4,5},{5,4},{6,7},{7,6},{8,9},{9,8},{10,11... | collective-permute-start | bytes 25264136 | tf_op jit(solution)/shard_map/ppermute | solution.py:726
  23.2 14.3 %collective-permute-start.1 = (f32[512,256]{1,0:T(8,128)S(1)}, f32[512,256]{1,0:T(8,128)S(1)}, u32[]{:S(2)}, u32[]{:S(2)}) collective-permute-start(f32[512,256]{1,0:T(8,128)S(1)} %get-tuple-element.190), channel_id=1, source_target_pairs={{0,2},{1,3},{2,0},{3,1},{4,6},{5,7},{6,4},{7,5},{8,10},{9,11},{10,... | collective-permute-start | bytes 1572872 | tf_op jit(solution)/shard_map/ppermute | solution.py:730
  24.3 14.0 %collective-permute-start.2 = (f32[128,1024]{1,0:T(8,128)S(1)}, f32[128,1024]{1,0:T(8,128)S(1)}, u32[]{:S(2)}, u32[]{:S(2)}) collective-permute-start(f32[128,1024]{1,0:T(8,128)S(1)} %collective-permute-done.o_got_ref), channel_id=1, source_target_pairs={{0,4},{4,0},{8,12},{12,8},{16,20},{20,16},{24,28},{28,24},{1,5},{5... | collective-permute-start | bytes 1572872 | tf_op jit(solution)/shard_map/ppermute | solution.py:759
  42.9 14.8 %collective-permute-start.6 = (f32[128,1024]{1,0:T(8,128)S(1)}, f32[128,1024]{1,0:T(8,128)S(1)}, u32[]{:S(2)}, u32[]{:S(2)}) collective-permute-start(f32[128,1024]{1,0:T(8,128)S(1)} %get-tuple-element.205), channel_id=1, source_target_pairs={{0,2},{1,3},{2,0},{3,1},{4,6},{5,7},{6,4},{7,5},{8,10},{9,11},{10,... | collective-permute-start | bytes 1572872 | tf_op jit(solution)/shard_map/ppermute | solution.py:730
  43.9 25.1 %collective-permute-start.5 = (f32[128,1024]{1,0:T(8,128)S(1)}, f32[128,1024]{1,0:T(8,128)S(1)}, u32[]{:S(2)}, u32[]{:S(2)}) collective-permute-start(f32[128,1024]{1,0:T(8,128)S(1)} %get-tuple-element.211), channel_id=1, source_target_pairs={{0,2},{1,3},{2,0},{3,1},{4,6},{5,7},{6,4},{7,5},{8,10},{9,11},{10,... | collective-permute-start | bytes 1572872 | tf_op jit(solution)/shard_map/ppermute | solution.py:730
  61.5 18.7 %collective-permute-start.8 = (f32[128,1024]{1,0:T(8,128)S(1)}, f32[128,1024]{1,0:T(8,128)S(1)}, u32[]{:S(2)}, u32[]{:S(2)}) collective-permute-start(f32[128,1024]{1,0:T(8,128)S(1)} %get-tuple-element.216), channel_id=1, source_target_pairs={{0,2},{1,3},{2,0},{3,1},{4,6},{5,7},{6,4},{7,5},{8,10},{9,11},{10,... | collective-permute-start | bytes 1572872 | tf_op jit(solution)/shard_map/ppermute | solution.py:730
  72.8 18.7 %collective-permute-start.7 = (f32[128,1024]{1,0:T(8,128)S(1)}, f32[128,1024]{1,0:T(8,128)S(1)}, u32[]{:S(2)}, u32[]{:S(2)}) collective-permute-start(f32[128,1024]{1,0:T(8,128)S(1)} %get-tuple-element.220), channel_id=1, source_target_pairs={{0,2},{1,3},{2,0},{3,1},{4,6},{5,7},{6,4},{7,5},{8,10},{9,11},{10,... | collective-permute-start | bytes 1572872 | tf_op jit(solution)/shard_map/ppermute | solution.py:730
  80.3 22.4 %collective-permute-start.10 = (f32[128,1024]{1,0:T(8,128)S(1)}, f32[128,1024]{1,0:T(8,128)S(1)}, u32[]{:S(2)}, u32[]{:S(2)}) collective-permute-start(f32[128,1024]{1,0:T(8,128)S(1)} %add.91.y_ref), channel_id=1, source_target_pairs={{0,2},{1,3},{2,0},{3,1},{4,6},{5,7},{6,4},{7,5},{8,10},{9,11},{10,... | collective-permute-start | bytes 1572872 | tf_op jit(solution)/shard_map/ppermute | solution.py:730
  91.5 22.4 %collective-permute-start.9 = (f32[128,1024]{1,0:T(8,128)S(1)}, f32[128,1024]{1,0:T(8,128)S(1)}, u32[]{:S(2)}, u32[]{:S(2)}) collective-permute-start(f32[128,1024]{1,0:T(8,128)S(1)} %add.92.y_ref), channel_id=1, source_target_pairs={{0,2},{1,3},{2,0},{3,1},{4,6},{5,7},{6,4},{7,5},{8,10},{9,11},{10,... | collective-permute-start | bytes 1572872 | tf_op jit(solution)/shard_map/ppermute | solution.py:730
  108.4 16.0 %collective-permute-start.11 = (f32[128,1024]{1,0:T(8,128)S(1)}, f32[128,1024]{1,0:T(8,128)S(1)}, u32[]{:S(2)}, u32[]{:S(2)}) collective-permute-start(f32[128,1024]{1,0:T(8,128)S(1)} %get-tuple-element.234), channel_id=1, source_target_pairs={{0,2},{1,3},{2,0},{3,1},{4,6},{5,7},{6,4},{7,5},{8,10},{9,11},{10,... | collective-permute-start | bytes 1572872 | tf_op jit(solution)/shard_map/ppermute | solution.py:730
  128.1 11.3 %collective-permute-start.14 = (f32[1024,1024]{1,0:T(8,128)S(1)}, f32[1024,1024]{1,0:T(8,128)S(1)}, u32[]{:S(2)}, u32[]{:S(2)}) collective-permute-start(f32[1024,1024]{1,0:T(8,128)S(1)} %pair.5), channel_id=1, source_target_pairs={{0,1},{1,0},{2,3},{3,2},{4,5},{5,4},{6,7},{7,6},{8,9},{9,8},{10,11... | collective-permute-start | bytes 12582920 | tf_op jit(solution)/shard_map/ppermute | solution.py:726
  128.7 13.9 %collective-permute-start.12 = (f32[128,1024]{1,0:T(8,128)S(1)}, f32[128,1024]{1,0:T(8,128)S(1)}, u32[]{:S(2)}, u32[]{:S(2)}) collective-permute-start(f32[128,1024]{1,0:T(8,128)S(1)} %get-tuple-element.243), channel_id=1, source_target_pairs={{0,2},{1,3},{2,0},{3,1},{4,6},{5,7},{6,4},{7,5},{8,10},{9,11},{10,... | collective-permute-start | bytes 1572872 | tf_op jit(solution)/shard_map/ppermute | solution.py:730
  147.9 16.5 %collective-permute-start.16 = (f32[544,256]{1,0:T(8,128)S(1)}, f32[544,256]{1,0:T(8,128)S(1)}, u32[]{:S(2)}, u32[]{:S(2)}) collective-permute-start(f32[544,256]{1,0:T(8,128)S(1)} %get-tuple-element.272), channel_id=1, source_target_pairs={{0,2},{1,3},{2,0},{3,1},{4,6},{5,7},{6,4},{7,5},{8,10},{9,11},{10,... | collective-permute-start | bytes 1671176 | tf_op jit(solution)/shard_map/ppermute | solution.py:730
  149.6 26.5 %collective-permute-start.17 = (f32[512,256]{1,0:T(8,128)S(1)}, f32[512,256]{1,0:T(8,128)S(1)}, u32[]{:S(2)}, u32[]{:S(2)}) collective-permute-start(f32[512,256]{1,0:T(8,128)S(1)} %get-tuple-element.287), channel_id=1, source_target_pairs={{0,2},{1,3},{2,0},{3,1},{4,6},{5,7},{6,4},{7,5},{8,10},{9,11},{10,... | collective-permute-start | bytes 1572872 | tf_op jit(solution)/shard_map/ppermute | solution.py:730
  150.8 34.3 %collective-permute-start.18 = (f32[512,256]{1,0:T(8,128)S(1)}, f32[512,256]{1,0:T(8,128)S(1)}, u32[]{:S(2)}, u32[]{:S(2)}) collective-permute-start(f32[512,256]{1,0:T(8,128)S(1)} %get-tuple-element.288), channel_id=1, source_target_pairs={{0,2},{1,3},{2,0},{3,1},{4,6},{5,7},{6,4},{7,5},{8,10},{9,11},{10,... | collective-permute-start | bytes 1572872 | tf_op jit(solution)/shard_map/ppermute | solution.py:730
  151.7 48.9 %collective-permute-start.20 = (f32[512,1024]{1,0:T(8,128)S(1)}, f32[512,1024]{1,0:T(8,128)S(1)}, u32[]{:S(2)}, u32[]{:S(2)}) collective-permute-start(f32[512,1024]{1,0:T(8,128)S(1)} %get-tuple-element.298), channel_id=1, source_target_pairs={{0,8},{4,12},{8,0},{12,4},{16,24},{20,28},{24,16},{28,20},{1,9},{5... | collective-permute-start | bytes 6291464 | tf_op jit(solution)/shard_map/ppermute | solution.py:759
  153.3 46.5 %collective-permute-start.21 = (f32[512,1024]{1,0:T(8,128)S(1)}, f32[512,1024]{1,0:T(8,128)S(1)}, u32[]{:S(2)}, u32[]{:S(2)}) collective-permute-start(f32[512,1024]{1,0:T(8,128)S(1)} %get-tuple-element.299), channel_id=1, source_target_pairs={{0,4},{4,0},{8,12},{12,8},{16,20},{20,16},{24,28},{28,24},{1,5},{5... | collective-permute-start | bytes 6291464 | tf_op jit(solution)/shard_map/ppermute | solution.py:759
  186.9 14.5 %collective-permute-start.19 = (f32[512,1024]{1,0:T(8,128)S(1)}, f32[512,1024]{1,0:T(8,128)S(1)}, u32[]{:S(2)}, u32[]{:S(2)}) collective-permute-start(f32[512,1024]{1,0:T(8,128)S(1)} %get-tuple-element.297), channel_id=1, source_target_pairs={{0,1},{1,0},{2,3},{3,2},{4,5},{5,4},{6,7},{7,6},{8,9},{9,8},{10,11... | collective-permute-start | bytes 6291464 | tf_op jit(solution)/shard_map/ppermute | solution.py:726
  201.8 88.2 %collective-permute-start.31 = (f32[512,1024]{1,0:T(8,128)S(1)}, f32[512,1024]{1,0:T(8,128)S(1)}, u32[]{:S(2)}, u32[]{:S(2)}) collective-permute-start(f32[512,1024]{1,0:T(8,128)S(1)} %get-tuple-element.305), channel_id=1, source_target_pairs={{0,2},{1,3},{2,0},{3,1},{4,6},{5,7},{6,4},{7,5},{8,10},{9,11},{10,... | collective-permute-start | bytes 6291464 | tf_op jit(solution)/shard_map/ppermute | solution.py:730
  202.9 40.1 %collective-permute-start.25 = (f32[272,1024]{1,0:T(8,128)S(1)}, f32[272,1024]{1,0:T(8,128)S(1)}, u32[]{:S(2)}, u32[]{:S(2)}) collective-permute-start(f32[272,1024]{1,0:T(8,128)S(1)} %get-tuple-element.301), channel_id=1, source_target_pairs={{0,8},{4,12},{8,0},{12,4},{16,24},{20,28},{24,16},{28,20},{1,9},{5... | collective-permute-start | bytes 3342344 | tf_op jit(solution)/shard_map/ppermute | solution.py:759
  203.4 41.0 %collective-permute-start.24 = (f32[272,1024]{1,0:T(8,128)S(1)}, f32[272,1024]{1,0:T(8,128)S(1)}, u32[]{:S(2)}, u32[]{:S(2)}) collective-permute-start(f32[272,1024]{1,0:T(8,128)S(1)} %get-tuple-element.303), channel_id=1, source_target_pairs={{0,4},{4,0},{8,12},{12,8},{16,20},{20,16},{24,28},{28,24},{1,5},{5... | collective-permute-start | bytes 3342344 | tf_op jit(solution)/shard_map/ppermute | solution.py:759
  206.5 61.4 %collective-permute-start.22 = (f32[536,512]{1,0:T(8,128)S(1)}, f32[536,512]{1,0:T(8,128)S(1)}, u32[]{:S(2)}, u32[]{:S(2)}) collective-permute-start(f32[536,512]{1,0:T(8,128)S(1)} %get-tuple-element.310), channel_id=1, source_target_pairs={{0,8},{4,12},{8,0},{12,4},{16,24},{20,28},{24,16},{28,20},{1,9},{5... | collective-permute-start | bytes 3293192 | tf_op jit(solution)/shard_map/ppermute | solution.py:759
  208.2 41.7 %collective-permute-start.23 = (f32[512,512]{1,0:T(8,128)S(1)}, f32[512,512]{1,0:T(8,128)S(1)}, u32[]{:S(2)}, u32[]{:S(2)}) collective-permute-start(f32[512,512]{1,0:T(8,128)S(1)} %get-tuple-element.292), channel_id=1, source_target_pairs={{0,4},{4,0},{8,12},{12,8},{16,20},{20,16},{24,28},{28,24},{1,5},{5... | collective-permute-start | bytes 3145736 | tf_op jit(solution)/shard_map/ppermute | solution.py:759
  243.7 34.8 %collective-permute-start.29 = (f32[144,1024]{1,0:T(8,128)S(1)}, f32[144,1024]{1,0:T(8,128)S(1)}, u32[]{:S(2)}, u32[]{:S(2)}) collective-permute-start(f32[144,1024]{1,0:T(8,128)S(1)} %get-tuple-element.315), channel_id=1, source_target_pairs={{0,16},{4,20},{8,24},{12,28},{16,0},{20,4},{24,8},{28,12},{1,17},{... | collective-permute-start | bytes 1769480 | tf_op jit(solution)/shard_map/ppermute | solution.py:759
  245.0 41.3 %collective-permute-start.28 = (f32[144,1024]{1,0:T(8,128)S(1)}, f32[144,1024]{1,0:T(8,128)S(1)}, u32[]{:S(2)}, u32[]{:S(2)}) collective-permute-start(f32[144,1024]{1,0:T(8,128)S(1)} %get-tuple-element.317), channel_id=1, source_target_pairs={{0,16},{4,20},{8,24},{12,28},{16,0},{20,4},{24,8},{28,12},{1,17},{... | collective-permute-start | bytes 1769480 | tf_op jit(solution)/shard_map/ppermute | solution.py:759
  268.6 20.8 %collective-permute-start.26 = (f32[280,512]{1,0:T(8,128)S(1)}, f32[280,512]{1,0:T(8,128)S(1)}, u32[]{:S(2)}, u32[]{:S(2)}) collective-permute-start(f32[280,512]{1,0:T(8,128)S(1)} %get-tuple-element.323), channel_id=1, source_target_pairs={{0,4},{4,0},{8,12},{12,8},{16,20},{20,16},{24,28},{28,24},{1,5},{5... | collective-permute-start | bytes 1720328 | tf_op jit(solution)/shard_map/ppermute | solution.py:759
  270.2 18.5 %collective-permute-start.27 = (f32[256,512]{1,0:T(8,128)S(1)}, f32[256,512]{1,0:T(8,128)S(1)}, u32[]{:S(2)}, u32[]{:S(2)}) collective-permute-start(f32[256,512]{1,0:T(8,128)S(1)} %get-tuple-element.319), channel_id=1, source_target_pairs={{0,8},{4,12},{8,0},{12,4},{16,24},{20,28},{24,16},{28,20},{1,9},{5... | collective-permute-start | bytes 1572872 | tf_op jit(solution)/shard_map/ppermute | solution.py:759
  290.7 7.3 %collective-permute-start.32 = (f32[512,1024]{1,0:T(8,128)S(1)}, f32[512,1024]{1,0:T(8,128)}, u32[]{:S(2)}, u32[]{:S(2)}) collective-permute-start(f32[512,1024]{1,0:T(8,128)S(1)} %add.94.mine_ref), channel_id=1, source_target_pairs={{0,1},{1,0},{2,3},{3,2},{4,5},{5,4},{6,7},{7,6},{8,9},{9,8},{10,11... | collective-permute-start | bytes 6291464 | tf_op jit(solution)/shard_map/ppermute | solution.py:726
  290.7 10.9 %collective-permute-start.30 = (f32[512,1024]{1,0:T(8,128)}, f32[512,1024]{1,0:T(8,128)}, u32[]{:S(2)}, u32[]{:S(2)}) collective-permute-start(f32[512,1024]{1,0:T(8,128)} %get-tuple-element.334.near_ref), channel_id=1, source_target_pairs={{0,1},{1,0},{2,3},{3,2},{4,5},{5,4},{6,7},{7,6},{8,9},{9,8},{10,11... | collective-permute-start | bytes 6291464 | tf_op jit(solution)/shard_map/ppermute | solution.py:726
  292.1 21.6 %collective-permute-start.33 = (f32[128,512]{1,0:T(8,128)}, f32[128,512]{1,0:T(8,128)S(1)}, u32[]{:S(2)}, u32[]{:S(2)}) collective-permute-start(f32[128,512]{1,0:T(8,128)} %copy-done.24), channel_id=1, source_target_pairs={{0,16},{4,20},{8,24},{12,28},{16,0},{20,4},{24,8},{28,12},{1,17},{... | collective-permute-start | bytes 786440 | tf_op jit(solution)/shard_map/ppermute | solution.py:759
  293.3 26.9 %collective-permute-start.34 = (f32[152,512]{1,0:T(8,128)}, f32[152,512]{1,0:T(8,128)S(1)}, u32[]{:S(2)}, u32[]{:S(2)}) collective-permute-start(f32[152,512]{1,0:T(8,128)} %copy-done.23), channel_id=1, source_target_pairs={{0,16},{4,20},{8,24},{12,28},{16,0},{20,4},{24,8},{28,12},{1,17},{... | collective-permute-start | bytes 933896 | tf_op jit(solution)/shard_map/ppermute | solution.py:759
  (28 other events, 250.1 us)
where the time goes:
time: 325 us; the launch traced here: 324 us
  waiting for transfers between devices  165 us (51%)
  Pallas kernels  108 us (33%)
  starting transfers between devices  34.2 us (11%)
  local copies, waits for them, and re-layouts  13.2 us (4%)
    ppermute x13, waiting for transfers between devices, dp_swap(): return lax.ppermute(value, 'dp', [(i, i ^ 1 << bit) for i in range(parts)])  97.2 us
    pallas_call x41, Pallas kernels, whole(): pl.pallas_call(kernel, in_specs=[pl.BlockSpec(memory_space=pltpu.SMEM)] *...  72.8 us
    ppermute x14, waiting for transfers between devices, swap_chip(): return lax.ppermute(value, 'mp', [(i, i ^ 2) for i in range(4)])  54.1 us
    pallas_call x2, Pallas kernels, attn_bwd(): pl.pallas_call(functools.partial(attn_bwd_kernel, bool(sums)), grid=(rows...  19.3 us
    ppermute x13, starting transfers between devices, dp_swap(): return lax.ppermute(value, 'dp', [(i, i ^ 1 << bit) for i in range(parts)])  16.4 us
    ppermute x14, starting transfers between devices, swap_chip(): return lax.ppermute(value, 'mp', [(i, i ^ 2) for i in range(4)])  16.4 us
    ppermute x8, waiting for transfers between devices, swap_core(): return lax.ppermute(value, 'mp', [(i, i ^ 1) for i in range(4)])  13.5 us
    unnamed x54, local copies, waits for them, and re-layouts  8.48 us
  transfers between devices with their start and end apart: 35, of which 25 were waited for; matrix products, arithmetic and copies ran while one was open for 1% of the time, Pallas kernels for 31%

commit v1 on v0

--- a/solution.py
+++ b/solution.py
@@ -391,6 +391,11 @@
         extra_ref = refs[0]
         refs = refs[1:]
         extra = extra_ref[...] + got_ref[rows:, :]
+    if ends and len(refs) == 2 and not riders:
+        wide = total_ref.shape[1] // 2
+        refs[0][...] = total_ref[:, :wide] + got_ref[:rows, :wide]
+        refs[1][...] = (total_ref[:, wide:] + got_ref[:rows, wide:]).T
+        return
     if ends:
         refs[0][...] = total_ref[...] + got_ref[:rows, :]
         if riders:
@@ -414,41 +419,41 @@
         refs[0][half:, :] = jnp.zeros((refs[0].shape[0] - half, refs[0].shape[1]), f32)
 
 
-def qk_kernel(bit, meta_ref, left_ref, near_ref, far_ref, gk_ref, away_ref, kept_ref):
+def qk_kernel(bit, meta_ref, left_ref, near_ref, far_ref, gk_ref, gv_ref, chip_ref, far_sums_ref, ub_ref, sib_ref, away_ref, kept_ref, extra_ref):
     mine = meta_ref[BITS + bit]
     half = left_ref.shape[1] // 2
     rows = near_ref.shape[0]
     wide = near_ref.shape[1]
-    for kept, ref in enumerate((away_ref, kept_ref)):
-        cols = pl.ds(pl.multiple_of((mine if kept else 1 - mine) * half, 128), half)
-        ref[:, :wide] = dot_tn(left_ref[:rows, cols], near_ref[...]) + dot_tn(left_ref[rows:, cols], far_ref[...])
-        ref[:, wide:] = dot_tn(left_ref[:, cols], gk_ref[...])
-
-
-def vo_kernel(bit, meta_ref, left_ref, gv_ref, kept_o_ref, got_a_ref, got_b_ref, near_ref, far_ref, chip_ref, far_sums_ref, ub_ref, sib_ref, away_ref, kept_ref, extra_ref):
-    mine = meta_ref[BITS + bit]
-    half = left_ref.shape[1] // 2
-    wide = gv_ref.shape[1]
     riders = chip_ref.shape[0]
     extra_ref[...] = jnp.zeros_like(extra_ref)
     shared = chip_ref[...] + far_sums_ref[far_sums_ref.shape[0] - riders :, :]
     extra_ref[: riders // 2, :wide] = shared[: riders // 2]
     extra_ref[: riders // 2, wide:] = shared[riders // 2 :]
     row = riders // 2
-    ones = (jnp.sum(near_ref[...].astype(f32), axis=0, keepdims=True) + jnp.sum(far_ref[...].astype(f32), axis=0, keepdims=True))
-    extra_ref[row : row + 1, :wide] = ones
+    query_sum = jnp.sum(near_ref[...].astype(f32), axis=0, keepdims=True)
+    extra_ref[row : row + 1, :wide] = query_sum + jnp.sum(far_ref[...].astype(f32), axis=0, keepdims=True)
     extra_ref[row : row + 1, wide:] = jnp.sum(gv_ref[...].astype(f32), axis=0, keepdims=True)
     place = sib_ref.shape[0] - 8
     for k in range(ub_ref.shape[1] // (2 * wide)):
         cols = slice(2 * k * wide, 2 * (k + 1) * wide)
         extra_ref[row + 1 + k : row + 2 + k, :] = ub_ref[:, cols] + sib_ref[place : place + 1, cols]
     for kept, ref in enumerate((away_ref, kept_ref)):
+        cols = pl.ds(pl.multiple_of((mine if kept else 1 - mine) * half, 128), half)
+        ref[:half, :wide] = dot_tn(left_ref[:rows, cols], near_ref[...]) + dot_tn(left_ref[rows:, cols], far_ref[...])
+        ref[:half, wide:] = dot_tn(left_ref[:, cols], gk_ref[...])
+    away_ref[half:, :] = extra_ref[...]
+
+
+def vo_kernel(bit, meta_ref, left_ref, gv_ref, kept_o_ref, got_a_ref, got_b_ref, away_ref, kept_ref):
+    mine = meta_ref[BITS + bit]
+    half = left_ref.shape[1] // 2
+    wide = gv_ref.shape[1]
+    for kept, ref in enumerate((away_ref, kept_ref)):
         start = pl.multiple_of((mine if kept else 1 - mine) * half, 128)
-        ref[:half, :wide] = dot_tn(left_ref[:, pl.ds(start, half)], gv_ref[...])
+        ref[:, :wide] = dot_tn(left_ref[:, pl.ds(start, half)], gv_ref[...])
         rows = pl.ds(start, half)
         top = jnp.where(start == 0, got_a_ref[...], got_b_ref[...])
-        ref[:half, wide:] = kept_o_ref[rows, :] + top
-    away_ref[half:, :] = extra_ref[...]
+        ref[:, wide:] = kept_o_ref[rows, :] + top
 
 
 def o_kernel(cols_ref, other_ref, near_ref, first_ref, second_ref, kept_ref):
@@ -763,6 +768,8 @@
     def __init__(self, parts, order, meta, line, spare=0):
         self.parts, self.order, self.meta, self.line = parts, list(order), meta, line
         self.spare = spare
+        self.turned = False
+        self.second = None
         self.extra = self.total = self.got = None
 
     def begin(self, away, total, extra=None):
@@ -787,6 +794,8 @@
         outputs = [shape(rows, cols)]
         if not ends:
             outputs = [shape(rows // 2 + riders + self.spare, cols), shape(rows // 2, cols)]
+        if ends and self.turned and rows % 128 == 0:
+            outputs = [shape(rows, cols // 2), shape(cols // 2, rows)]
         given = [self.total, got] + ([self.extra] if riders else [])
         result = whole(
             functools.partial(fold_kernel, riders, ends, bit), "fold", given, outputs + rest, scalars=self.meta
@@ -795,6 +804,7 @@
             self.extra = result[-1]
         if ends:
             self.total = result[0]
+            self.second = result[1] if len(outputs) == 2 else None
             self.line.mark(self.total)
         else:
             self.total = result[1]
@@ -983,8 +993,8 @@
         return value if fixed else bit_order_columns(value, dp_size, order)
 
     gf_cols, lo_cols = in_order(grad_fed, fixed_a, order_a), in_order(lo, fixed_b, order_b)
-    down_sum = Sum(dp_size, order_a, meta, line, 16)
-    up_sum = Sum(dp_size, order_b, meta, line, 16)
+    down_sum = Sum(dp_size, order_a, meta, line, 0)
+    up_sum = Sum(dp_size, order_b, meta, line, 0)
 
     def pair(side, sum_of, left, right, given=()):
         half_rows = width // 2
@@ -1051,38 +1061,13 @@
 
     qk_sum = Sum(dp_size, order_a, meta, line)
     vo_sum = Sum(dp_size, order_b, meta, line)
-    qk_away, qk_kept = whole(
+    vo_sum.turned = True
+    riders = 8 * width // head_width
+    extra_rows = -(-(riders // 2 + 1 + hidden // (2 * head_width)) // 8) * 8
+    qk_away, qk_kept, qk_extra = whole(
         functools.partial(qk_kernel, qk_sum.order[0]),
         "qk_grad",
-        [local_a, line.hold(grad_q_near), grad_q_far, grad_k],
-        [shape(width // 2, 2 * head_width)] * 2,
-        scalars=meta,
-    )
-    line.mark(qk_away)
-    riders = 8 * width // head_width
-    extra_rows = -(-(riders // 2 + 1 + hidden // (2 * head_width)) // 8) * 8
-    o_got = line.hold(*o_got)
-    line.mark(*o_got)
-    in_mine, in_away = whole(
-        input_kernel,
-        "input_grad",
-        [line.hold(grad_q_near), grad_q_far, grad_k, grad_v, q_weight, k_weight, v_weight, first_ext],
-        [shape(half, width)] * 2,
-    )
-    in_got = swap_core(in_away)
-    line.mark(in_mine)
-    down_sum.step()
-    up_sum.step()
-    qk_sum.begin(qk_away, qk_kept)
-    in_kept, in_sent = whole(
-        chip_kernel, "chip_sum", [in_mine, line.hold(in_got)], [shape(half, width)] * 2
-    )
-    in_got = swap_chip(in_sent)
-    line.mark(in_sent)
-    vo_away, vo_kept, vo_extra = whole(
-        functools.partial(vo_kernel, vo_sum.order[0]),
-        "vo_grad",
-        [local_b, line.hold(grad_v), o_kept, *o_got, grad_q_near, grad_q_far, chip_sums, grad_context_far]
+        [local_a, line.hold(grad_q_near), grad_q_far, grad_k, grad_v, chip_sums, grad_context_far]
         + [up_bias_own, sib_ext],
         [
             shape(width // 2 + extra_rows, 2 * head_width),
@@ -1091,13 +1076,45 @@
         ],
         scalars=meta,
     )
-    vo_sum.begin(vo_away, vo_kept, vo_extra)
+    line.mark(qk_away)
+    o_got = line.hold(*o_got)
+    line.mark(*o_got)
+    down_sum.step()
+    up_sum.step()
+    in_mine, in_away = whole(
+        input_kernel,
+        "input_grad",
+        [line.hold(grad_q_near), grad_q_far, grad_k, grad_v, q_weight, k_weight, v_weight, first_ext],
+        [shape(half, width)] * 2,
+    )
+    in_got = swap_core(in_away)
+    line.mark(in_mine)
+    in_kept, in_sent = whole(
+        chip_kernel, "chip_sum", [in_mine, line.hold(in_got)], [shape(half, width)] * 2
+    )
+    in_got = swap_chip(in_sent)
+    line.mark(in_sent)
+    vo_away, vo_kept = whole(
+        functools.partial(vo_kernel, vo_sum.order[0]),
+        "vo_grad",
+        [local_b, line.hold(grad_v), o_kept, *o_got],
+        [shape(width // 2, 2 * head_width)] * 2,
+        scalars=meta,
+    )
     line.mark(vo_away)
+    down_sum.step()
+    up_sum.step()
+    qk_sum.begin(line.hold(qk_away), qk_kept, qk_extra)
+    vo_sum.begin(line.hold(vo_away), vo_kept)
     for bit in range(bits):
-        down_sum.step()
-        up_sum.step()
         qk_sum.step()
+        if bit == 0:
+            down_sum.step()
+            up_sum.step()
         vo_sum.step()
+        if bit > 1:
+            down_sum.step()
+            up_sum.step()
         if bit == min(1, bits - 1):
             in_final = add(in_kept, line.hold(in_got))
             in_other = swap_core(in_final)
@@ -1126,15 +1143,17 @@
                 far=True,
             )[0]
             line.mark(out)
-    qk_sum, vo_total = qk_sum.finish(), vo_sum.finish()
-    riding = vo_sum.extra
+    qk_total, vo_total = qk_sum.finish(), vo_sum.finish()
+    riding = qk_sum.extra
     row = riders // 2
     shared = jnp.concatenate([riding[:row, :head_width], riding[:row, head_width:]], axis=0)
     shared = shared.reshape(-1, 8, head_width).transpose(1, 0, 2).reshape(8, width)
     biases = riding[row].reshape(2, head_width)
     up_bias_sum = riding[row + 1 : row + 1 + hidden // (2 * head_width)].reshape(-1)
-    v_sum = vo_total[:, :head_width]
-    o_sum = vo_total[:, head_width:].T
+    if vo_sum.second is None:
+        v_sum, o_sum = vo_total[:, :head_width], vo_total[:, head_width:].T
+    else:
+        v_sum, o_sum = vo_total, vo_sum.second
     down_sum = down_sum.finish().T
     up_sum = up_sum.finish()
 
@@ -1148,9 +1167,9 @@
         out,
         pooled,
         in_grad,
-        qk_sum[:, :head_width],
+        qk_total[:, :head_width],
         biases[0],
-        qk_sum[:, head_width:],
+        qk_total[:, head_width:],
         v_sum,
         biases[1],
         o_sum,

time: 325 us -> 316 us (0.972)
  waiting for transfers between devices: 165 us -> 151 us
  starting transfers between devices: 34.2 us -> 38.4 us
    ppermute x13, waiting for transfers between devices: 97.2 us -> 85.1 us  [dp_swap(): return lax.ppermute(value, 'dp', [(i, i ^ 1 << bit) for i in range(parts)])]
    unnamed x54 -> x53, local copies, waits for them, and re-layouts: 8.48 us -> 8.06 us
  transfers between devices with their start and end apart: 35 -> 35, of which waited for: 25 -> 27; matrix products, arithmetic and copies ran while one was open for 1% -> 2% of each run, Pallas kernels for 31% -> 32%
where the time goes in v1:
time: 316 us
  waiting for transfers between devices  151 us (48%)
  Pallas kernels  111 us (35%)
  starting transfers between devices  38.4 us (12%)
  local copies, waits for them, and re-layouts  12.1 us (4%)
    ppermute x13, waiting for transfers between devices, dp_swap(): return lax.ppermute(value, 'dp', [(i, i ^ 1 << bit) for i in range(parts)])  85.1 us
    pallas_call x41, Pallas kernels, whole(): pl.pallas_call(kernel, in_specs=[pl.BlockSpec(memory_space=pltpu.SMEM)] *...  74 us
    ppermute x14, waiting for transfers between devices, swap_chip(): return lax.ppermute(value, 'mp', [(i, i ^ 2) for i in range(4)])  53.7 us
    pallas_call x2, Pallas kernels, attn_bwd(): pl.pallas_call(functools.partial(attn_bwd_kernel, bool(sums)), grid=(rows...  19.6 us
    ppermute x13, starting transfers between devices, dp_swap(): return lax.ppermute(value, 'dp', [(i, i ^ 1 << bit) for i in range(parts)])  18.8 us
    ppermute x14, starting transfers between devices, swap_chip(): return lax.ppermute(value, 'mp', [(i, i ^ 2) for i in range(4)])  18.2 us
    ppermute x8, waiting for transfers between devices, swap_core(): return lax.ppermute(value, 'mp', [(i, i ^ 1) for i in range(4)])  12.4 us
    pallas_call x2, Pallas kernels, attn_fwd(): pl.pallas_call(attn_fwd_kernel, grid=(rows // block,), in_specs=[pl.Block...  8.78 us
  transfers between devices with their start and end apart: 35, of which 27 were waited for; matrix products, arithmetic and copies ran while one was open for 2% of the time, Pallas kernels for 32%

profile of v1, /device:TPU:0, one launch (start us, length us, event | category | flops | bytes accessed | tf_op | source)
XLA Modules:
  0.0 315.7 jit_solution(1996929002476795130)
XLA Ops:
  8.9 5.6 %qkv.1 = (f32[8,256]{1,0:T(8,128)}, bf16[1024,1024]{1,0:T(8,128)(2,1)}, bf16[512,256]{1,0:T(8,128)(2,1)}, bf16[512,256]{1,0:T(8,128)(2,1)}, bf16[1024,256]{1,0:T(8,128)(2,1)}, /*index=5*/bf16[1024,256]{1,0:T(8,128)(2,1)}) custom-call(s32[13]{0:T(128)} %concatenate.30.meta_ref, bf16[1024,1024]{1,0:T(8,128)(2,1)} %all_ref, bf16[1024,256]{1,0:T(8,128)(2,1)} %qw_ref.3, ...), custom_call_target="tpu_custom_call" | custom-call | flops 1024 | bytes 1024 | tf_op jit(solution)/shard_map/qkv/pallas_call | solution.py:342
  17.5 4.4 %attn_fwd.2 = (f32[512,256]{1,0:T(8,128)S(1)}, f32[512,128]{1,0:T(8,128)S(1)}) custom-call(bf16[512,256]{1,0:T(8,128)(2,1)S(1)} %copy-done.16, bf16[1024,256]{1,0:T(8,128)(2,1)S(1)} %copy-done.3, bf16[1024,256]{1,0:T(8,128)(2,1)S(1)} %copy-done.5, f32[1,1024]{1,0:T(1,128)S(1)} %compare_select_fusion.bias_ref.refs_4_), custom_call_target="tpu_custom_call" | custom-call | flops 1024 | bytes 1024 | tf_op jit(solution)/shard_map/attn_fwd/pallas_call | solution.py:64
  25.9 4.4 %attn_fwd.3 = (bf16[512,256]{1,0:T(8,128)(2,1)S(1)}, f32[512,128]{1,0:T(8,128)S(1)}) custom-call(bf16[512,256]{1,0:T(8,128)(2,1)S(1)} %copy-done.18, bf16[1024,256]{1,0:T(8,128)(2,1)S(1)} %copy-done.3, bf16[1024,256]{1,0:T(8,128)(2,1)S(1)} %copy-done.5, f32[1,1024]{1,0:T(1,128)S(1)} %compare_select_fusion.bias_ref.refs_4_), custom_call_target="tpu_custom_call" | custom-call | flops 1024 | bytes 1024 | tf_op jit(solution)/shard_map/attn_fwd/pallas_call | solution.py:64
  31.1 6.7 %collective-permute-done.1.other_ref = f32[512,256]{1,0:T(8,128)S(1)} collective-permute-done((f32[512,256]{1,0:T(8,128)S(1)}, f32[512,256]{1,0:T(8,128)S(1)}, u32[]{:S(2)}, u32[]{:S(2)}) %collective-permute-start.1) | collective-permute-done | bytes 524320 | tf_op jit(solution)/shard_map/ppermute | solution.py:735
  45.5 5.2 %feed.3 = (bf16[512,1024]{1,0:T(8,128)(2,1)S(1)}, bf16[512,2048]{1,0:T(8,128)(2,1)S(1)}, f32[256,2048]{1,0:T(8,128)S(1)}, f32[128,1024]{1,0:T(8,128)S(1)}, f32[128,1024]{1,0:T(8,128)S(1)}) custom-call(f32[256,1024]{1,0:T(8,128)S(1)} %get-tuple-element.208.refs_0_, bf16[1024,1024]{1,0:T(8,128)(2,1)S(1)} %copy-done, ...), custom_call_target="tpu_custom_call" | custom-call | flops 1024 | bytes 1024 | tf_op jit(solution)/shard_map/feed/pallas_call | solution.py:184
  50.7 7.0 %collective-permute-done.6.refs_0_ = f32[128,1024]{1,0:T(8,128)S(1)} collective-permute-done((f32[128,1024]{1,0:T(8,128)S(1)}, f32[128,1024]{1,0:T(8,128)S(1)}, u32[]{:S(2)}, u32[]{:S(2)}) %collective-permute-start.6) | collective-permute-done | bytes 524320 | tf_op jit(solution)/shard_map/ppermute | solution.py:735
  57.7 3.7 %feed.4 = (bf16[512,1024]{1,0:T(8,128)(2,1)S(1)}, bf16[512,2048]{1,0:T(8,128)(2,1)S(1)}, f32[128,2048]{1,0:T(8,128)S(1)}, f32[128,1024]{1,0:T(8,128)S(1)}) custom-call(f32[128,1024]{1,0:T(8,128)S(1)} %collective-permute-done.6.refs_0_, bf16[1024,1024]{1,0:T(8,128)(2,1)S(1)} %copy-done, ...), custom_call_target="tpu_custom_call", output_to_operand_aliasing={{0}: (7, {}), {1}: (8, {})} | custom-call | flops 1024 | bytes 1024 | tf_op jit(solution)/shard_map/feed/pallas_call | solution.py:184
  62.7 6.2 %collective-permute-done.5.refs_0_ = f32[128,1024]{1,0:T(8,128)S(1)} collective-permute-done((f32[128,1024]{1,0:T(8,128)S(1)}, f32[128,1024]{1,0:T(8,128)S(1)}, u32[]{:S(2)}, u32[]{:S(2)}) %collective-permute-start.5) | collective-permute-done | bytes 524320 | tf_op jit(solution)/shard_map/ppermute | solution.py:735
  69.0 3.7 %feed.5 = (bf16[512,1024]{1,0:T(8,128)(2,1)S(1)}, bf16[512,2048]{1,0:T(8,128)(2,1)S(1)}, f32[128,2048]{1,0:T(8,128)S(1)}, f32[128,1024]{1,0:T(8,128)S(1)}) custom-call(f32[128,1024]{1,0:T(8,128)S(1)} %collective-permute-done.5.refs_0_, bf16[1024,1024]{1,0:T(8,128)(2,1)S(1)} %copy-done, ...), custom_call_target="tpu_custom_call", output_to_operand_aliasing={{0}: (7, {}), {1}: (8, {})} | custom-call | flops 1024 | bytes 1024 | tf_op jit(solution)/shard_map/feed/pallas_call | solution.py:184
  74.0 6.2 %collective-permute-done.8.refs_1_ = f32[128,1024]{1,0:T(8,128)S(1)} collective-permute-done((f32[128,1024]{1,0:T(8,128)S(1)}, f32[128,1024]{1,0:T(8,128)S(1)}, u32[]{:S(2)}, u32[]{:S(2)}) %collective-permute-start.8) | collective-permute-done | bytes 524320 | tf_op jit(solution)/shard_map/ppermute | solution.py:735
  81.5 6.2 %feed_back.4 = (f32[512,1024]{1,0:T(8,128)}, bf16[512,1024]{1,0:T(8,128)(2,1)S(1)}, bf16[512,2048]{1,0:T(8,128)(2,1)S(1)}, f32[128,1024]{1,0:T(8,128)S(1)}, f32[...) custom-call(s32[13]{0:T(128)S(1)} %copy-done.19, ...), custom_call_target="tpu_custom_call" | custom-call | flops 1024 | bytes 1024 | tf_op jit(solution)/shard_map/feed_back/pallas_call | solution.py:184
  87.7 3.7 %collective-permute-done.7.refs_1_ = f32[128,1024]{1,0:T(8,128)S(1)} collective-permute-done((f32[128,1024]{1,0:T(8,128)S(1)}, f32[128,1024]{1,0:T(8,128)S(1)}, u32[]{:S(2)}, u32[]{:S(2)}) %collective-permute-start.7) | collective-permute-done | bytes 524320 | tf_op jit(solution)/shard_map/ppermute | solution.py:735
  92.8 5.9 %feed_back.5 = (f32[512,1024]{1,0:T(8,128)}, bf16[512,1024]{1,0:T(8,128)(2,1)S(1)}, bf16[512,2048]{1,0:T(8,128)(2,1)S(1)}, f32[128,1024]{1,0:T(8,128)S(1)}, f32[...) custom-call(s32[13]{0:T(128)S(1)} %copy-done.19, ...), custom_call_target="tpu_custom_call", output_to_operand_aliasing={{0}: (10, {}), {1}: (11, {}), {2}: (12, {})} | custom-call | flops 1024 | bytes 1024 | tf_op jit(solution)/shard_map/feed_back/pallas_call | solution.py:184
  98.7 4.0 %collective-permute-done.10.y_ref = f32[128,1024]{1,0:T(8,128)S(1)} collective-permute-done((f32[128,1024]{1,0:T(8,128)S(1)}, f32[128,1024]{1,0:T(8,128)S(1)}, u32[]{:S(2)}, u32[]{:S(2)}) %collective-permute-start.10) | collective-permute-done | bytes 524320 | tf_op jit(solution)/shard_map/ppermute | solution.py:735
  102.7 5.9 %feed_back.6 = (f32[512,1024]{1,0:T(8,128)}, bf16[512,1024]{1,0:T(8,128)(2,1)S(1)}, bf16[512,2048]{1,0:T(8,128)(2,1)S(1)}, f32[128,1024]{1,0:T(8,128)S(1)}, f32[...) custom-call(s32[13]{0:T(128)S(1)} %copy-done.19, ...), custom_call_target="tpu_custom_call", output_to_operand_aliasing={{0}: (10, {}), {1}: (11, {}), {2}: (12, {})} | custom-call | flops 1024 | bytes 1024 | tf_op jit(solution)/shard_map/feed_back/pallas_call | solution.py:184
  109.9 4.0 %collective-permute-done.9.y_ref = f32[128,1024]{1,0:T(8,128)S(1)} collective-permute-done((f32[128,1024]{1,0:T(8,128)S(1)}, f32[128,1024]{1,0:T(8,128)S(1)}, u32[]{:S(2)}, u32[]{:S(2)}) %collective-permute-start.9) | collective-permute-done | bytes 524320 | tf_op jit(solution)/shard_map/ppermute | solution.py:735
  113.9 5.7 %feed_back.7 = (f32[512,1024]{1,0:T(8,128)}, bf16[512,1024]{1,0:T(8,128)(2,1)S(1)}, bf16[512,2048]{1,0:T(8,128)(2,1)S(1)}, f32[128,1024]{1,0:T(8,128)S(1)}, f32[...) custom-call(s32[13]{0:T(128)S(1)} %copy-done.19, ...), custom_call_target="tpu_custom_call", output_to_operand_aliasing={{0}: (10, {}), {1}: (11, {}), {2}: (12, {})} | custom-call | flops 1024 | bytes 1024 | tf_op jit(solution)/shard_map/feed_back/pallas_call | solution.py:184
  119.7 4.7 %collective-permute-done.11.refs_1_ = f32[128,1024]{1,0:T(8,128)S(1)} collective-permute-done((f32[128,1024]{1,0:T(8,128)S(1)}, f32[128,1024]{1,0:T(8,128)S(1)}, u32[]{:S(2)}, u32[]{:S(2)}) %collective-permute-start.11) | collective-permute-done | bytes 524320 | tf_op jit(solution)/shard_map/ppermute | solution.py:735
  129.9 3.5 %collective-permute-done.13.refs_0_ = f32[1024,1024]{1,0:T(8,128)S(1)} collective-permute-done((f32[1024,1024]{1,0:T(8,128)S(1)}, f32[1024,1024]{1,0:T(8,128)S(1)}, u32[]{:S(2)}, u32[]{:S(2)}) %collective-permute-start.13) | collective-permute-done | bytes 4194336 | tf_op jit(solution)/shard_map/ppermute | solution.py:731
  152.5 9.8 %attn_bwd.2 = (bf16[512,256]{1,0:T(8,128)(2,1)S(1)}, f32[1024,256]{1,0:T(8,128)S(1)}, f32[1024,256]{1,0:T(8,128)S(1)}) custom-call(bf16[512,256]{1,0:T(8,128)(2,1)S(1)} %copy-done.18, bf16[512,256]{1,0:T(8,128)(2,1)S(1)} %get-tuple-element.282.refs_1_, bf16[1024,256]{1,0:T(8,128)(2,1)S(1)} %copy-done.4, bf16[1024,256]{1,0:T(8,128)(2,1)S(1)} %copy-done.6, ...), custom_call_target="tpu_custom_call" | custom-call | flops 1024 | bytes 1024 | tf_op jit(solution)/shard_map/attn_bwd/pallas_call | solution.py:135
  163.8 9.8 %attn_bwd.3 = (bf16[512,256]{1,0:T(8,128)(2,1)S(1)}, bf16[1024,256]{1,0:T(8,128)(2,1)S(1)}, bf16[1024,256]{1,0:T(8,128)(2,1)S(1)}) custom-call(bf16[512,256]{1,0:T(8,128)(2,1)S(1)} %copy-done.17, f32[544,256]{1,0:T(8,128)S(1)} %collective-permute-done.16.refs_1_.far_sums_ref, bf16[1024,256]{1,0:T(8,128)(2,1)S(1)} %copy-done.4, ...), custom_call_target="tpu_custom_call" | custom-call | flops 1024 | bytes 1024 | tf_op jit(solution)/shard_map/attn_bwd/pallas_call | solution.py:135
  175.7 9.7 %collective-permute-done.20.got_b_ref = f32[512,256]{1,0:T(8,128)S(1)} collective-permute-done((f32[512,256]{1,0:T(8,128)S(1)}, f32[512,256]{1,0:T(8,128)S(1)}, u32[]{:S(2)}, u32[]{:S(2)}) %collective-permute-start.20) | collective-permute-done | bytes 524320 | tf_op jit(solution)/shard_map/ppermute | solution.py:735
  199.7 18.2 %collective-permute-done.23.got_ref = f32[256,1024]{1,0:T(8,128)S(1)} collective-permute-done((f32[256,1024]{1,0:T(8,128)S(1)}, f32[256,1024]{1,0:T(8,128)S(1)}, u32[]{:S(2)}, u32[]{:S(2)}) %collective-permute-start.23) | collective-permute-done | bytes 1048608 | tf_op jit(solution)/shard_map/ppermute | solution.py:764
  225.4 20.1 %collective-permute-done.27.got_ref = f32[536,512]{1,0:T(8,128)S(1)} collective-permute-done((f32[536,512]{1,0:T(8,128)S(1)}, f32[536,512]{1,0:T(8,128)S(1)}, u32[]{:S(2)}, u32[]{:S(2)}) %collective-permute-start.27) | collective-permute-done | bytes 1097760 | tf_op jit(solution)/shard_map/ppermute | solution.py:764
  247.4 9.9 %collective-permute-done.26.got_ref = f32[128,1024]{1,0:T(8,128)S(1)} collective-permute-done((f32[128,1024]{1,0:T(8,128)S(1)}, f32[128,1024]{1,0:T(8,128)S(1)}, u32[]{:S(2)}, u32[]{:S(2)}) %collective-permute-start.26) | collective-permute-done | bytes 524320 | tf_op jit(solution)/shard_map/ppermute | solution.py:764
  258.7 9.8 %collective-permute-done.25.got_ref = f32[128,1024]{1,0:T(8,128)S(1)} collective-permute-done((f32[128,1024]{1,0:T(8,128)S(1)}, f32[128,1024]{1,0:T(8,128)S(1)}, u32[]{:S(2)}, u32[]{:S(2)}) %collective-permute-start.25) | collective-permute-done | bytes 524320 | tf_op jit(solution)/shard_map/ppermute | solution.py:764
  271.3 9.1 %collective-permute-done.29.got_ref = f32[280,512]{1,0:T(8,128)S(1)} collective-permute-done((f32[280,512]{1,0:T(8,128)S(1)}, f32[280,512]{1,0:T(8,128)S(1)}, u32[]{:S(2)}, u32[]{:S(2)}) %collective-permute-start.29) | collective-permute-done | bytes 573472 | tf_op jit(solution)/shard_map/ppermute | solution.py:764
  284.1 3.4 %collective-permute-start.33 = (f32[152,512]{1,0:T(8,128)}, f32[152,512]{1,0:T(8,128)S(1)}, u32[]{:S(2)}, u32[]{:S(2)}) collective-permute-start(f32[152,512]{1,0:T(8,128)} %copy-done.23), channel_id=1, source_target_pairs={{0,16},{4,20},{8,24},{12,28},{16,0},{20,4},{24,8},{28,12},{1,17},{... | collective-permute-start | bytes 933896 | tf_op jit(solution)/shard_map/ppermute | solution.py:764
  290.2 3.6 %place.1 = f32[1024,1024]{1,0:T(8,128)} custom-call(s32[13]{0:T(128)S(1)} %copy-done.19, f32[512,1024]{1,0:T(8,128)S(1)} %add.94.mine_ref, f32[512,1024]{1,0:T(8,128)} %collective-permute-done.32.other_ref), custom_call_target="tpu_custom_call" | custom-call | flops 1024 | bytes 1024 | tf_op jit(solution)/shard_map/place/pallas_call | solution.py:184
  293.9 3.7 %round_place.1 = bf16[1024,1024]{1,0:T(8,128)(2,1)} custom-call(s32[13]{0:T(128)S(1)} %copy-done.19, f32[512,1024]{1,0:T(8,128)} %get-tuple-element.340.near_ref, f32[512,1024]{1,0:T(8,128)} %collective-permute-done.30.far_ref), custom_call_target="tpu_custom_call" | custom-call | flops 1024 | bytes 1024 | tf_op jit(solution)/shard_map/round_place/pallas_call | solution.py:184
  297.6 10.6 %collective-permute-done.33.got_ref = f32[152,512]{1,0:T(8,128)S(1)} collective-permute-done((f32[152,512]{1,0:T(8,128)}, f32[152,512]{1,0:T(8,128)S(1)}, u32[]{:S(2)}, u32[]{:S(2)}) %collective-permute-start.33) | collective-permute-done | bytes 311328 | tf_op jit(solution)/shard_map/ppermute | solution.py:764
  310.1 3.1 collective-permute-done.34.got_ref
  (154 shorter events, 95.4 us)
Async XLA Ops:
  5.9 16.1 %collective-permute-start = (f32[128,1024]{1,0:T(8,128)}, f32[128,1024]{1,0:T(8,128)S(1)}, u32[]{:S(2)}, u32[]{:S(2)}) collective-permute-start(f32[128,1024]{1,0:T(8,128)} %get-tuple-element.187), channel_id=1, source_target_pairs={{0,2},{1,3},{2,0},{3,1},{4,6},{5,7},{6,4},{7,5},{8,10},{9,11},{10,... | collective-permute-start | bytes 1572872 | tf_op jit(solution)/shard_map/ppermute | solution.py:735
  23.4 21.6 %collective-permute-start.4 = (f32[2056,1024]{1,0:T(8,128)S(1)}, f32[2056,1024]{1,0:T(8,128)S(1)}, u32[]{:S(2)}, u32[]{:S(2)}) collective-permute-start(f32[2056,1024]{1,0:T(8,128)S(1)} %widen.1), channel_id=1, source_target_pairs={{0,1},{1,0},{2,3},{3,2},{4,5},{5,4},{6,7},{7,6},{8,9},{9,8},{10,11... | collective-permute-start | bytes 25264136 | tf_op jit(solution)/shard_map/ppermute | solution.py:731
  23.5 14.3 %collective-permute-start.1 = (f32[512,256]{1,0:T(8,128)S(1)}, f32[512,256]{1,0:T(8,128)S(1)}, u32[]{:S(2)}, u32[]{:S(2)}) collective-permute-start(f32[512,256]{1,0:T(8,128)S(1)} %get-tuple-element.194), channel_id=1, source_target_pairs={{0,2},{1,3},{2,0},{3,1},{4,6},{5,7},{6,4},{7,5},{8,10},{9,11},{10,... | collective-permute-start | bytes 1572872 | tf_op jit(solution)/shard_map/ppermute | solution.py:735
  24.3 14.0 %collective-permute-start.2 = (f32[128,1024]{1,0:T(8,128)S(1)}, f32[128,1024]{1,0:T(8,128)S(1)}, u32[]{:S(2)}, u32[]{:S(2)}) collective-permute-start(f32[128,1024]{1,0:T(8,128)S(1)} %collective-permute-done.o_got_ref), channel_id=1, source_target_pairs={{0,4},{4,0},{8,12},{12,8},{16,20},{20,16},{24,28},{28,24},{1,5},{5... | collective-permute-start | bytes 1572872 | tf_op jit(solution)/shard_map/ppermute | solution.py:764
  42.9 14.8 %collective-permute-start.6 = (f32[128,1024]{1,0:T(8,128)S(1)}, f32[128,1024]{1,0:T(8,128)S(1)}, u32[]{:S(2)}, u32[]{:S(2)}) collective-permute-start(f32[128,1024]{1,0:T(8,128)S(1)} %get-tuple-element.209), channel_id=1, source_target_pairs={{0,2},{1,3},{2,0},{3,1},{4,6},{5,7},{6,4},{7,5},{8,10},{9,11},{10,... | collective-permute-start | bytes 1572872 | tf_op jit(solution)/shard_map/ppermute | solution.py:735
  44.2 24.8 %collective-permute-start.5 = (f32[128,1024]{1,0:T(8,128)S(1)}, f32[128,1024]{1,0:T(8,128)S(1)}, u32[]{:S(2)}, u32[]{:S(2)}) collective-permute-start(f32[128,1024]{1,0:T(8,128)S(1)} %get-tuple-element.215), channel_id=1, source_target_pairs={{0,2},{1,3},{2,0},{3,1},{4,6},{5,7},{6,4},{7,5},{8,10},{9,11},{10,... | collective-permute-start | bytes 1572872 | tf_op jit(solution)/shard_map/ppermute | solution.py:735
  61.4 18.8 %collective-permute-start.8 = (f32[128,1024]{1,0:T(8,128)S(1)}, f32[128,1024]{1,0:T(8,128)S(1)}, u32[]{:S(2)}, u32[]{:S(2)}) collective-permute-start(f32[128,1024]{1,0:T(8,128)S(1)} %get-tuple-element.220), channel_id=1, source_target_pairs={{0,2},{1,3},{2,0},{3,1},{4,6},{5,7},{6,4},{7,5},{8,10},{9,11},{10,... | collective-permute-start | bytes 1572872 | tf_op jit(solution)/shard_map/ppermute | solution.py:735
  72.7 18.7 %collective-permute-start.7 = (f32[128,1024]{1,0:T(8,128)S(1)}, f32[128,1024]{1,0:T(8,128)S(1)}, u32[]{:S(2)}, u32[]{:S(2)}) collective-permute-start(f32[128,1024]{1,0:T(8,128)S(1)} %get-tuple-element.224), channel_id=1, source_target_pairs={{0,2},{1,3},{2,0},{3,1},{4,6},{5,7},{6,4},{7,5},{8,10},{9,11},{10,... | collective-permute-start | bytes 1572872 | tf_op jit(solution)/shard_map/ppermute | solution.py:735
  80.3 22.4 %collective-permute-start.10 = (f32[128,1024]{1,0:T(8,128)S(1)}, f32[128,1024]{1,0:T(8,128)S(1)}, u32[]{:S(2)}, u32[]{:S(2)}) collective-permute-start(f32[128,1024]{1,0:T(8,128)S(1)} %add.91.y_ref), channel_id=1, source_target_pairs={{0,2},{1,3},{2,0},{3,1},{4,6},{5,7},{6,4},{7,5},{8,10},{9,11},{10,... | collective-permute-start | bytes 1572872 | tf_op jit(solution)/shard_map/ppermute | solution.py:735
  91.5 22.4 %collective-permute-start.9 = (f32[128,1024]{1,0:T(8,128)S(1)}, f32[128,1024]{1,0:T(8,128)S(1)}, u32[]{:S(2)}, u32[]{:S(2)}) collective-permute-start(f32[128,1024]{1,0:T(8,128)S(1)} %add.92.y_ref), channel_id=1, source_target_pairs={{0,2},{1,3},{2,0},{3,1},{4,6},{5,7},{6,4},{7,5},{8,10},{9,11},{10,... | collective-permute-start | bytes 1572872 | tf_op jit(solution)/shard_map/ppermute | solution.py:735
  108.6 15.7 %collective-permute-start.11 = (f32[128,1024]{1,0:T(8,128)S(1)}, f32[128,1024]{1,0:T(8,128)S(1)}, u32[]{:S(2)}, u32[]{:S(2)}) collective-permute-start(f32[128,1024]{1,0:T(8,128)S(1)} %get-tuple-element.238), channel_id=1, source_target_pairs={{0,2},{1,3},{2,0},{3,1},{4,6},{5,7},{6,4},{7,5},{8,10},{9,11},{10,... | collective-permute-start | bytes 1572872 | tf_op jit(solution)/shard_map/ppermute | solution.py:735
  126.2 7.2 %collective-permute-start.13 = (f32[1024,1024]{1,0:T(8,128)S(1)}, f32[1024,1024]{1,0:T(8,128)S(1)}, u32[]{:S(2)}, u32[]{:S(2)}) collective-permute-start(f32[1024,1024]{1,0:T(8,128)S(1)} %pair.4), channel_id=1, source_target_pairs={{0,1},{1,0},{2,3},{3,2},{4,5},{5,4},{6,7},{7,6},{8,9},{9,8},{10,11... | collective-permute-start | bytes 12582920 | tf_op jit(solution)/shard_map/ppermute | solution.py:731
  128.2 11.3 %collective-permute-start.14 = (f32[1024,1024]{1,0:T(8,128)S(1)}, f32[1024,1024]{1,0:T(8,128)S(1)}, u32[]{:S(2)}, u32[]{:S(2)}) collective-permute-start(f32[1024,1024]{1,0:T(8,128)S(1)} %pair.5), channel_id=1, source_target_pairs={{0,1},{1,0},{2,3},{3,2},{4,5},{5,4},{6,7},{7,6},{8,9},{9,8},{10,11... | collective-permute-start | bytes 12582920 | tf_op jit(solution)/shard_map/ppermute | solution.py:731
  128.7 14.2 %collective-permute-start.12 = (f32[128,1024]{1,0:T(8,128)S(1)}, f32[128,1024]{1,0:T(8,128)S(1)}, u32[]{:S(2)}, u32[]{:S(2)}) collective-permute-start(f32[128,1024]{1,0:T(8,128)S(1)} %get-tuple-element.247), channel_id=1, source_target_pairs={{0,2},{1,3},{2,0},{3,1},{4,6},{5,7},{6,4},{7,5},{8,10},{9,11},{10,... | collective-permute-start | bytes 1572872 | tf_op jit(solution)/shard_map/ppermute | solution.py:735
  135.3 50.1 %collective-permute-start.18 = (f32[512,1024]{1,0:T(8,128)S(1)}, f32[512,1024]{1,0:T(8,128)S(1)}, u32[]{:S(2)}, u32[]{:S(2)}) collective-permute-start(f32[512,1024]{1,0:T(8,128)S(1)} %get-tuple-element.292), channel_id=1, source_target_pairs={{0,4},{4,0},{8,12},{12,8},{16,20},{20,16},{24,28},{28,24},{1,5},{5... | collective-permute-start | bytes 6291464 | tf_op jit(solution)/shard_map/ppermute | solution.py:764
  141.3 47.7 %collective-permute-start.17 = (f32[512,1024]{1,0:T(8,128)S(1)}, f32[512,1024]{1,0:T(8,128)S(1)}, u32[]{:S(2)}, u32[]{:S(2)}) collective-permute-start(f32[512,1024]{1,0:T(8,128)S(1)} %get-tuple-element.291), channel_id=1, source_target_pairs={{0,8},{4,12},{8,0},{12,4},{16,24},{20,28},{24,16},{28,20},{1,9},{5... | collective-permute-start | bytes 6291464 | tf_op jit(solution)/shard_map/ppermute | solution.py:764
  148.3 15.5 %collective-permute-start.16 = (f32[544,256]{1,0:T(8,128)S(1)}, f32[544,256]{1,0:T(8,128)S(1)}, u32[]{:S(2)}, u32[]{:S(2)}) collective-permute-start(f32[544,256]{1,0:T(8,128)S(1)} %get-tuple-element.276), channel_id=1, source_target_pairs={{0,2},{1,3},{2,0},{3,1},{4,6},{5,7},{6,4},{7,5},{8,10},{9,11},{10,... | collective-permute-start | bytes 1671176 | tf_op jit(solution)/shard_map/ppermute | solution.py:735
  150.4 25.4 %collective-permute-start.19 = (f32[512,256]{1,0:T(8,128)S(1)}, f32[512,256]{1,0:T(8,128)S(1)}, u32[]{:S(2)}, u32[]{:S(2)}) collective-permute-start(f32[512,256]{1,0:T(8,128)S(1)} %get-tuple-element.293), channel_id=1, source_target_pairs={{0,2},{1,3},{2,0},{3,1},{4,6},{5,7},{6,4},{7,5},{8,10},{9,11},{10,... | collective-permute-start | bytes 1572872 | tf_op jit(solution)/shard_map/ppermute | solution.py:735
  151.2 34.2 %collective-permute-start.20 = (f32[512,256]{1,0:T(8,128)S(1)}, f32[512,256]{1,0:T(8,128)S(1)}, u32[]{:S(2)}, u32[]{:S(2)}) collective-permute-start(f32[512,256]{1,0:T(8,128)S(1)} %get-tuple-element.294), channel_id=1, source_target_pairs={{0,2},{1,3},{2,0},{3,1},{4,6},{5,7},{6,4},{7,5},{8,10},{9,11},{10,... | collective-permute-start | bytes 1572872 | tf_op jit(solution)/shard_map/ppermute | solution.py:735
  192.3 25.6 %collective-permute-start.23 = (f32[256,1024]{1,0:T(8,128)S(1)}, f32[256,1024]{1,0:T(8,128)S(1)}, u32[]{:S(2)}, u32[]{:S(2)}) collective-permute-start(f32[256,1024]{1,0:T(8,128)S(1)} %get-tuple-element.304), channel_id=1, source_target_pairs={{0,8},{4,12},{8,0},{12,4},{16,24},{20,28},{24,16},{28,20},{1,9},{5... | collective-permute-start | bytes 3145736 | tf_op jit(solution)/shard_map/ppermute | solution.py:764
  194.0 25.2 %collective-permute-start.22 = (f32[256,1024]{1,0:T(8,128)S(1)}, f32[256,1024]{1,0:T(8,128)S(1)}, u32[]{:S(2)}, u32[]{:S(2)}) collective-permute-start(f32[256,1024]{1,0:T(8,128)S(1)} %get-tuple-element.306), channel_id=1, source_target_pairs={{0,4},{4,0},{8,12},{12,8},{16,20},{20,16},{24,28},{28,24},{1,5},{5... | collective-permute-start | bytes 3145736 | tf_op jit(solution)/shard_map/ppermute | solution.py:764
  196.8 85.2 %collective-permute-start.31 = (f32[512,1024]{1,0:T(8,128)S(1)}, f32[512,1024]{1,0:T(8,128)S(1)}, u32[]{:S(2)}, u32[]{:S(2)}) collective-permute-start(f32[512,1024]{1,0:T(8,128)S(1)} %get-tuple-element.311), channel_id=1, source_target_pairs={{0,2},{1,3},{2,0},{3,1},{4,6},{5,7},{6,4},{7,5},{8,10},{9,11},{10,... | collective-permute-start | bytes 6291464 | tf_op jit(solution)/shard_map/ppermute | solution.py:735
  219.9 25.5 %collective-permute-start.27 = (f32[536,512]{1,0:T(8,128)S(1)}, f32[536,512]{1,0:T(8,128)S(1)}, u32[]{:S(2)}, u32[]{:S(2)}) collective-permute-start(f32[536,512]{1,0:T(8,128)S(1)} %get-tuple-element.325), channel_id=1, source_target_pairs={{0,4},{4,0},{8,12},{12,8},{16,20},{20,16},{24,28},{28,24},{1,5},{5... | collective-permute-start | bytes 3293192 | tf_op jit(solution)/shard_map/ppermute | solution.py:764
  221.5 48.6 %collective-permute-start.24 = (f32[512,512]{1,0:T(8,128)S(1)}, f32[512,512]{1,0:T(8,128)S(1)}, u32[]{:S(2)}, u32[]{:S(2)}) collective-permute-start(f32[512,512]{1,0:T(8,128)S(1)} %get-tuple-element.321), channel_id=1, source_target_pairs={{0,8},{4,12},{8,0},{12,4},{16,24},{20,28},{24,16},{28,20},{1,9},{5... | collective-permute-start | bytes 3145736 | tf_op jit(solution)/shard_map/ppermute | solution.py:764
  222.4 34.9 %collective-permute-start.26 = (f32[128,1024]{1,0:T(8,128)S(1)}, f32[128,1024]{1,0:T(8,128)S(1)}, u32[]{:S(2)}, u32[]{:S(2)}) collective-permute-start(f32[128,1024]{1,0:T(8,128)S(1)} %get-tuple-element.318), channel_id=1, source_target_pairs={{0,16},{4,20},{8,24},{12,28},{16,0},{20,4},{24,8},{28,12},{1,17},{... | collective-permute-start | bytes 1572872 | tf_op jit(solution)/shard_map/ppermute | solution.py:764
  225.0 43.5 %collective-permute-start.25 = (f32[128,1024]{1,0:T(8,128)S(1)}, f32[128,1024]{1,0:T(8,128)S(1)}, u32[]{:S(2)}, u32[]{:S(2)}) collective-permute-start(f32[128,1024]{1,0:T(8,128)S(1)} %get-tuple-element.320), channel_id=1, source_target_pairs={{0,16},{4,20},{8,24},{12,28},{16,0},{20,4},{24,8},{28,12},{1,17},{... | collective-permute-start | bytes 1572872 | tf_op jit(solution)/shard_map/ppermute | solution.py:764
  246.1 34.3 %collective-permute-start.29 = (f32[280,512]{1,0:T(8,128)S(1)}, f32[280,512]{1,0:T(8,128)S(1)}, u32[]{:S(2)}, u32[]{:S(2)}) collective-permute-start(f32[280,512]{1,0:T(8,128)S(1)} %get-tuple-element.328), channel_id=1, source_target_pairs={{0,8},{4,12},{8,0},{12,4},{16,24},{20,28},{24,16},{28,20},{1,9},{5... | collective-permute-start | bytes 1720328 | tf_op jit(solution)/shard_map/ppermute | solution.py:764
  270.7 10.6 %collective-permute-start.28 = (f32[256,512]{1,0:T(8,128)S(1)}, f32[256,512]{1,0:T(8,128)S(1)}, u32[]{:S(2)}, u32[]{:S(2)}) collective-permute-start(f32[256,512]{1,0:T(8,128)S(1)} %get-tuple-element.333), channel_id=1, source_target_pairs={{0,4},{4,0},{8,12},{12,8},{16,20},{20,16},{24,28},{28,24},{1,5},{5... | collective-permute-start | bytes 1572872 | tf_op jit(solution)/shard_map/ppermute | solution.py:764
  282.7 7.5 %collective-permute-start.32 = (f32[512,1024]{1,0:T(8,128)S(1)}, f32[512,1024]{1,0:T(8,128)}, u32[]{:S(2)}, u32[]{:S(2)}) collective-permute-start(f32[512,1024]{1,0:T(8,128)S(1)} %add.94.mine_ref), channel_id=1, source_target_pairs={{0,1},{1,0},{2,3},{3,2},{4,5},{5,4},{6,7},{7,6},{8,9},{9,8},{10,11... | collective-permute-start | bytes 6291464 | tf_op jit(solution)/shard_map/ppermute | solution.py:731
  282.7 11.2 %collective-permute-start.30 = (f32[512,1024]{1,0:T(8,128)}, f32[512,1024]{1,0:T(8,128)}, u32[]{:S(2)}, u32[]{:S(2)}) collective-permute-start(f32[512,1024]{1,0:T(8,128)} %get-tuple-element.340.near_ref), channel_id=1, source_target_pairs={{0,1},{1,0},{2,3},{3,2},{4,5},{5,4},{6,7},{7,6},{8,9},{9,8},{10,11... | collective-permute-start | bytes 6291464 | tf_op jit(solution)/shard_map/ppermute | solution.py:731
  284.1 24.1 %collective-permute-start.33 = (f32[152,512]{1,0:T(8,128)}, f32[152,512]{1,0:T(8,128)S(1)}, u32[]{:S(2)}, u32[]{:S(2)}) collective-permute-start(f32[152,512]{1,0:T(8,128)} %copy-done.23), channel_id=1, source_target_pairs={{0,16},{4,20},{8,24},{12,28},{16,0},{20,4},{24,8},{28,12},{1,17},{... | collective-permute-start | bytes 933896 | tf_op jit(solution)/shard_map/ppermute | solution.py:764
  290.2 22.9 %collective-permute-start.34 = (f32[128,512]{1,0:T(8,128)}, f32[128,512]{1,0:T(8,128)S(1)}, u32[]{:S(2)}, u32[]{:S(2)}) collective-permute-start(f32[128,512]{1,0:T(8,128)} %copy-done.24), channel_id=1, source_target_pairs={{0,16},{4,20},{8,24},{12,28},{16,0},{20,4},{24,8},{28,12},{1,17},{... | collective-permute-start | bytes 786440 | tf_op jit(solution)/shard_map/ppermute | solution.py:764
  (28 other events, 219.1 us)

commit v2 on v1

--- a/solution.py
+++ b/solution.py
@@ -1088,12 +1088,25 @@
         [shape(half, width)] * 2,
     )
     in_got = swap_core(in_away)
+    out_far = swap_core(line.hold(out_wide))
     line.mark(in_mine)
     in_kept, in_sent = whole(
         chip_kernel, "chip_sum", [in_mine, line.hold(in_got)], [shape(half, width)] * 2
     )
     in_got = swap_chip(in_sent)
     line.mark(in_sent)
+    out = whole(
+        round_place_kernel,
+        "round_place",
+        [out_wide, line.hold(out_far)],
+        [],
+        scalars=meta,
+        filled=[shape(slot_len, width, bf16)],
+        scratch=[pltpu.VMEM((slot_len, width), bf16)],
+        sems=4,
+        far=True,
+    )[0]
+    line.mark(out)
     vo_away, vo_kept = whole(
         functools.partial(vo_kernel, vo_sum.order[0]),
         "vo_grad",
@@ -1118,7 +1131,6 @@
         if bit == min(1, bits - 1):
             in_final = add(in_kept, line.hold(in_got))
             in_other = swap_core(in_final)
-            out_far = swap_core(line.hold(out_wide))
             line.mark(in_final)
             in_grad = whole(
                 place_kernel,
@@ -1131,18 +1143,6 @@
                 far=True,
             )[0]
             line.mark(in_grad)
-            out = whole(
-                round_place_kernel,
-                "round_place",
-                [out_wide, line.hold(out_far)],
-                [],
-                scalars=meta,
-                filled=[shape(slot_len, width, bf16)],
-                scratch=[pltpu.VMEM((slot_len, width), bf16)],
-                sems=4,
-                far=True,
-            )[0]
-            line.mark(out)
     qk_total, vo_total = qk_sum.finish(), vo_sum.finish()
     riding = qk_sum.extra
     row = riders // 2

time: 316 us -> 315 us (level)
  transfers between devices with their start and end apart: 35 -> 35, of which waited for: 27 -> 26; matrix products, arithmetic and copies ran while one was open for 2% -> 2% of each run, Pallas kernels for 32% -> 32%
where the time goes in v2:
time: 315 us; the launch traced here: 314 us
  waiting for transfers between devices  151 us (48%)
  Pallas kernels  109 us (35%)
  starting transfers between devices  38.1 us (12%)
  local copies, waits for them, and re-layouts  12.1 us (4%)
    ppermute x13, waiting for transfers between devices, dp_swap(): return lax.ppermute(value, 'dp', [(i, i ^ 1 << bit) for i in range(parts)])  84.6 us
    pallas_call x41, Pallas kernels, whole(): pl.pallas_call(kernel, in_specs=[pl.BlockSpec(memory_space=pltpu.SMEM)] *...  72.8 us
    ppermute x14, waiting for transfers between devices, swap_chip(): return lax.ppermute(value, 'mp', [(i, i ^ 2) for i in range(4)])  53.5 us
    pallas_call x2, Pallas kernels, attn_bwd(): pl.pallas_call(functools.partial(attn_bwd_kernel, bool(sums)), grid=(rows...  19.6 us
    ppermute x13, starting transfers between devices, dp_swap(): return lax.ppermute(value, 'dp', [(i, i ^ 1 << bit) for i in range(parts)])  18.6 us
    ppermute x14, starting transfers between devices, swap_chip(): return lax.ppermute(value, 'mp', [(i, i ^ 2) for i in range(4)])  18.1 us
    ppermute x8, waiting for transfers between devices, swap_core(): return lax.ppermute(value, 'mp', [(i, i ^ 1) for i in range(4)])  13.4 us
    pallas_call x2, Pallas kernels, attn_fwd(): pl.pallas_call(attn_fwd_kernel, grid=(rows // block,), in_specs=[pl.Block...  8.78 us
  transfers between devices with their start and end apart: 35, of which 26 were waited for; matrix products, arithmetic and copies ran while one was open for 2% of the time, Pallas kernels for 32%

profile of v2, /device:TPU:0, one launch (start us, length us, event | category | flops | bytes accessed | tf_op | source)
XLA Modules:
  0.0 314.2 jit_solution(845187568981649183)
XLA Ops:
  5.9 3.0 collective-permute-start
  8.9 5.6 %qkv.1 = (f32[8,256]{1,0:T(8,128)}, bf16[1024,1024]{1,0:T(8,128)(2,1)}, bf16[512,256]{1,0:T(8,128)(2,1)}, bf16[512,256]{1,0:T(8,128)(2,1)}, bf16[1024,256]{1,0:T(8,128)(2,1)}, /*index=5*/bf16[1024,256]{1,0:T(8,128)(2,1)}) custom-call(s32[13]{0:T(128)} %concatenate.30.meta_ref, bf16[1024,1024]{1,0:T(8,128)(2,1)} %all_ref, bf16[1024,256]{1,0:T(8,128)(2,1)} %qw_ref.3, ...), custom_call_target="tpu_custom_call" | custom-call | flops 1024 | bytes 1024 | tf_op jit(solution)/shard_map/qkv/pallas_call | solution.py:342
  17.5 4.4 %attn_fwd.2 = (f32[512,256]{1,0:T(8,128)S(1)}, f32[512,128]{1,0:T(8,128)S(1)}) custom-call(bf16[512,256]{1,0:T(8,128)(2,1)S(1)} %copy-done.16, bf16[1024,256]{1,0:T(8,128)(2,1)S(1)} %copy-done.3, bf16[1024,256]{1,0:T(8,128)(2,1)S(1)} %copy-done.5, f32[1,1024]{1,0:T(1,128)S(1)} %compare_select_fusion.bias_ref.refs_4_), custom_call_target="tpu_custom_call" | custom-call | flops 1024 | bytes 1024 | tf_op jit(solution)/shard_map/attn_fwd/pallas_call | solution.py:64
  25.9 4.4 %attn_fwd.3 = (bf16[512,256]{1,0:T(8,128)(2,1)S(1)}, f32[512,128]{1,0:T(8,128)S(1)}) custom-call(bf16[512,256]{1,0:T(8,128)(2,1)S(1)} %copy-done.18, bf16[1024,256]{1,0:T(8,128)(2,1)S(1)} %copy-done.3, bf16[1024,256]{1,0:T(8,128)(2,1)S(1)} %copy-done.5, f32[1,1024]{1,0:T(1,128)S(1)} %compare_select_fusion.bias_ref.refs_4_), custom_call_target="tpu_custom_call" | custom-call | flops 1024 | bytes 1024 | tf_op jit(solution)/shard_map/attn_fwd/pallas_call | solution.py:64
  31.1 6.7 %collective-permute-done.1.other_ref = f32[512,256]{1,0:T(8,128)S(1)} collective-permute-done((f32[512,256]{1,0:T(8,128)S(1)}, f32[512,256]{1,0:T(8,128)S(1)}, u32[]{:S(2)}, u32[]{:S(2)}) %collective-permute-start.1) | collective-permute-done | bytes 524320 | tf_op jit(solution)/shard_map/ppermute | solution.py:735
  45.5 5.2 %feed.3 = (bf16[512,1024]{1,0:T(8,128)(2,1)S(1)}, bf16[512,2048]{1,0:T(8,128)(2,1)S(1)}, f32[256,2048]{1,0:T(8,128)S(1)}, f32[128,1024]{1,0:T(8,128)S(1)}, f32[128,1024]{1,0:T(8,128)S(1)}) custom-call(f32[256,1024]{1,0:T(8,128)S(1)} %get-tuple-element.208.refs_0_, bf16[1024,1024]{1,0:T(8,128)(2,1)S(1)} %copy-done, ...), custom_call_target="tpu_custom_call" | custom-call | flops 1024 | bytes 1024 | tf_op jit(solution)/shard_map/feed/pallas_call | solution.py:184
  50.7 7.0 %collective-permute-done.6.refs_0_ = f32[128,1024]{1,0:T(8,128)S(1)} collective-permute-done((f32[128,1024]{1,0:T(8,128)S(1)}, f32[128,1024]{1,0:T(8,128)S(1)}, u32[]{:S(2)}, u32[]{:S(2)}) %collective-permute-start.6) | collective-permute-done | bytes 524320 | tf_op jit(solution)/shard_map/ppermute | solution.py:735
  57.7 3.7 %feed.4 = (bf16[512,1024]{1,0:T(8,128)(2,1)S(1)}, bf16[512,2048]{1,0:T(8,128)(2,1)S(1)}, f32[128,2048]{1,0:T(8,128)S(1)}, f32[128,1024]{1,0:T(8,128)S(1)}) custom-call(f32[128,1024]{1,0:T(8,128)S(1)} %collective-permute-done.6.refs_0_, bf16[1024,1024]{1,0:T(8,128)(2,1)S(1)} %copy-done, ...), custom_call_target="tpu_custom_call", output_to_operand_aliasing={{0}: (7, {}), {1}: (8, {})} | custom-call | flops 1024 | bytes 1024 | tf_op jit(solution)/shard_map/feed/pallas_call | solution.py:184
  62.7 6.2 %collective-permute-done.5.refs_0_ = f32[128,1024]{1,0:T(8,128)S(1)} collective-permute-done((f32[128,1024]{1,0:T(8,128)S(1)}, f32[128,1024]{1,0:T(8,128)S(1)}, u32[]{:S(2)}, u32[]{:S(2)}) %collective-permute-start.5) | collective-permute-done | bytes 524320 | tf_op jit(solution)/shard_map/ppermute | solution.py:735
  69.0 3.7 %feed.5 = (bf16[512,1024]{1,0:T(8,128)(2,1)S(1)}, bf16[512,2048]{1,0:T(8,128)(2,1)S(1)}, f32[128,2048]{1,0:T(8,128)S(1)}, f32[128,1024]{1,0:T(8,128)S(1)}) custom-call(f32[128,1024]{1,0:T(8,128)S(1)} %collective-permute-done.5.refs_0_, bf16[1024,1024]{1,0:T(8,128)(2,1)S(1)} %copy-done, ...), custom_call_target="tpu_custom_call", output_to_operand_aliasing={{0}: (7, {}), {1}: (8, {})} | custom-call | flops 1024 | bytes 1024 | tf_op jit(solution)/shard_map/feed/pallas_call | solution.py:184
  74.0 6.2 %collective-permute-done.8.refs_1_ = f32[128,1024]{1,0:T(8,128)S(1)} collective-permute-done((f32[128,1024]{1,0:T(8,128)S(1)}, f32[128,1024]{1,0:T(8,128)S(1)}, u32[]{:S(2)}, u32[]{:S(2)}) %collective-permute-start.8) | collective-permute-done | bytes 524320 | tf_op jit(solution)/shard_map/ppermute | solution.py:735
  81.5 6.2 %feed_back.4 = (f32[512,1024]{1,0:T(8,128)S(1)}, bf16[512,1024]{1,0:T(8,128)(2,1)S(1)}, bf16[512,2048]{1,0:T(8,128)(2,1)S(1)}, f32[128,1024]{1,0:T(8,128)S(1)}, ...) custom-call(s32[13]{0:T(128)S(1)} %copy-done.19, ...), custom_call_target="tpu_custom_call" | custom-call | flops 1024 | bytes 1024 | tf_op jit(solution)/shard_map/feed_back/pallas_call | solution.py:184
  87.7 3.7 %collective-permute-done.7.refs_1_ = f32[128,1024]{1,0:T(8,128)S(1)} collective-permute-done((f32[128,1024]{1,0:T(8,128)S(1)}, f32[128,1024]{1,0:T(8,128)S(1)}, u32[]{:S(2)}, u32[]{:S(2)}) %collective-permute-start.7) | collective-permute-done | bytes 524320 | tf_op jit(solution)/shard_map/ppermute | solution.py:735
  92.8 6.2 %feed_back.5 = (f32[512,1024]{1,0:T(8,128)S(1)}, bf16[512,1024]{1,0:T(8,128)(2,1)S(1)}, bf16[512,2048]{1,0:T(8,128)(2,1)S(1)}, f32[128,1024]{1,0:T(8,128)S(1)}, ...) custom-call(s32[13]{0:T(128)S(1)} %copy-done.19, ...), custom_call_target="tpu_custom_call", output_to_operand_aliasing={{0}: (10, {}), {1}: (11, {}), {2}: (12, {})} | custom-call | flops 1024 | bytes 1024 | tf_op jit(solution)/shard_map/feed_back/pallas_call | solution.py:184
  98.9 3.7 %collective-permute-done.10.y_ref = f32[128,1024]{1,0:T(8,128)S(1)} collective-permute-done((f32[128,1024]{1,0:T(8,128)S(1)}, f32[128,1024]{1,0:T(8,128)S(1)}, u32[]{:S(2)}, u32[]{:S(2)}) %collective-permute-start.10) | collective-permute-done | bytes 524320 | tf_op jit(solution)/shard_map/ppermute | solution.py:735
  102.7 6.0 %feed_back.6 = (f32[512,1024]{1,0:T(8,128)S(1)}, bf16[512,1024]{1,0:T(8,128)(2,1)S(1)}, bf16[512,2048]{1,0:T(8,128)(2,1)S(1)}, f32[128,1024]{1,0:T(8,128)S(1)}, ...) custom-call(s32[13]{0:T(128)S(1)} %copy-done.19, ...), custom_call_target="tpu_custom_call", output_to_operand_aliasing={{0}: (10, {}), {1}: (11, {}), {2}: (12, {})} | custom-call | flops 1024 | bytes 1024 | tf_op jit(solution)/shard_map/feed_back/pallas_call | solution.py:184
  109.8 4.1 %collective-permute-done.9.y_ref = f32[128,1024]{1,0:T(8,128)S(1)} collective-permute-done((f32[128,1024]{1,0:T(8,128)S(1)}, f32[128,1024]{1,0:T(8,128)S(1)}, u32[]{:S(2)}, u32[]{:S(2)}) %collective-permute-start.9) | collective-permute-done | bytes 524320 | tf_op jit(solution)/shard_map/ppermute | solution.py:735
  113.9 5.9 %feed_back.7 = (f32[512,1024]{1,0:T(8,128)S(1)}, bf16[512,1024]{1,0:T(8,128)(2,1)S(1)}, bf16[512,2048]{1,0:T(8,128)(2,1)S(1)}, f32[128,1024]{1,0:T(8,128)S(1)}, ...) custom-call(s32[13]{0:T(128)S(1)} %copy-done.19, ...), custom_call_target="tpu_custom_call", output_to_operand_aliasing={{0}: (10, {}), {1}: (11, {}), {2}: (12, {})} | custom-call | flops 1024 | bytes 1024 | tf_op jit(solution)/shard_map/feed_back/pallas_call | solution.py:184
  119.8 4.6 %collective-permute-done.11.refs_1_ = f32[128,1024]{1,0:T(8,128)S(1)} collective-permute-done((f32[128,1024]{1,0:T(8,128)S(1)}, f32[128,1024]{1,0:T(8,128)S(1)}, u32[]{:S(2)}, u32[]{:S(2)}) %collective-permute-start.11) | collective-permute-done | bytes 524320 | tf_op jit(solution)/shard_map/ppermute | solution.py:735
  129.9 3.5 %collective-permute-done.14.refs_0_ = f32[1024,1024]{1,0:T(8,128)S(1)} collective-permute-done((f32[1024,1024]{1,0:T(8,128)S(1)}, f32[1024,1024]{1,0:T(8,128)S(1)}, u32[]{:S(2)}, u32[]{:S(2)}) %collective-permute-start.14) | collective-permute-done | bytes 4194336 | tf_op jit(solution)/shard_map/ppermute | solution.py:731
  152.5 9.8 %attn_bwd.2 = (bf16[512,256]{1,0:T(8,128)(2,1)S(1)}, f32[1024,256]{1,0:T(8,128)S(1)}, f32[1024,256]{1,0:T(8,128)S(1)}) custom-call(bf16[512,256]{1,0:T(8,128)(2,1)S(1)} %copy-done.18, bf16[512,256]{1,0:T(8,128)(2,1)S(1)} %get-tuple-element.285.refs_1_, bf16[1024,256]{1,0:T(8,128)(2,1)S(1)} %copy-done.4, bf16[1024,256]{1,0:T(8,128)(2,1)S(1)} %copy-done.6, ...), custom_call_target="tpu_custom_call" | custom-call | flops 1024 | bytes 1024 | tf_op jit(solution)/shard_map/attn_bwd/pallas_call | solution.py:135
  163.8 9.8 %attn_bwd.3 = (bf16[512,256]{1,0:T(8,128)(2,1)S(1)}, bf16[1024,256]{1,0:T(8,128)(2,1)S(1)}, bf16[1024,256]{1,0:T(8,128)(2,1)S(1)}) custom-call(bf16[512,256]{1,0:T(8,128)(2,1)S(1)} %copy-done.17, f32[544,256]{1,0:T(8,128)S(1)} %collective-permute-done.20.refs_1_.far_sums_ref, bf16[1024,256]{1,0:T(8,128)(2,1)S(1)} %copy-done.4, ...), custom_call_target="tpu_custom_call" | custom-call | flops 1024 | bytes 1024 | tf_op jit(solution)/shard_map/attn_bwd/pallas_call | solution.py:135
  175.7 9.7 %collective-permute-done.19.got_b_ref = f32[512,256]{1,0:T(8,128)S(1)} collective-permute-done((f32[512,256]{1,0:T(8,128)S(1)}, f32[512,256]{1,0:T(8,128)S(1)}, u32[]{:S(2)}, u32[]{:S(2)}) %collective-permute-start.19) | collective-permute-done | bytes 524320 | tf_op jit(solution)/shard_map/ppermute | solution.py:735
  203.1 14.9 %collective-permute-done.25.got_ref = f32[256,1024]{1,0:T(8,128)S(1)} collective-permute-done((f32[256,1024]{1,0:T(8,128)S(1)}, f32[256,1024]{1,0:T(8,128)S(1)}, u32[]{:S(2)}, u32[]{:S(2)}) %collective-permute-start.25) | collective-permute-done | bytes 1048608 | tf_op jit(solution)/shard_map/ppermute | solution.py:764
  225.4 19.6 %collective-permute-done.29.got_ref = f32[536,512]{1,0:T(8,128)S(1)} collective-permute-done((f32[536,512]{1,0:T(8,128)S(1)}, f32[536,512]{1,0:T(8,128)S(1)}, u32[]{:S(2)}, u32[]{:S(2)}) %collective-permute-start.29) | collective-permute-done | bytes 1097760 | tf_op jit(solution)/shard_map/ppermute | solution.py:764
  247.1 10.3 %collective-permute-done.28.got_ref = f32[128,1024]{1,0:T(8,128)S(1)} collective-permute-done((f32[128,1024]{1,0:T(8,128)S(1)}, f32[128,1024]{1,0:T(8,128)S(1)}, u32[]{:S(2)}, u32[]{:S(2)}) %collective-permute-start.28) | collective-permute-done | bytes 524320 | tf_op jit(solution)/shard_map/ppermute | solution.py:764
  258.8 9.8 %collective-permute-done.27.got_ref = f32[128,1024]{1,0:T(8,128)S(1)} collective-permute-done((f32[128,1024]{1,0:T(8,128)S(1)}, f32[128,1024]{1,0:T(8,128)S(1)}, u32[]{:S(2)}, u32[]{:S(2)}) %collective-permute-start.27) | collective-permute-done | bytes 524320 | tf_op jit(solution)/shard_map/ppermute | solution.py:764
  271.3 8.7 %collective-permute-done.31.got_ref = f32[280,512]{1,0:T(8,128)S(1)} collective-permute-done((f32[280,512]{1,0:T(8,128)S(1)}, f32[280,512]{1,0:T(8,128)S(1)}, u32[]{:S(2)}, u32[]{:S(2)}) %collective-permute-start.31) | collective-permute-done | bytes 573472 | tf_op jit(solution)/shard_map/ppermute | solution.py:764
  282.8 3.4 %collective-permute-start.33 = (f32[152,512]{1,0:T(8,128)}, f32[152,512]{1,0:T(8,128)S(1)}, u32[]{:S(2)}, u32[]{:S(2)}) collective-permute-start(f32[152,512]{1,0:T(8,128)} %copy-done.23), channel_id=1, source_target_pairs={{0,16},{4,20},{8,24},{12,28},{16,0},{20,4},{24,8},{28,12},{1,17},{... | collective-permute-start | bytes 933896 | tf_op jit(solution)/shard_map/ppermute | solution.py:764
  288.9 3.7 %place.1 = f32[1024,1024]{1,0:T(8,128)} custom-call(s32[13]{0:T(128)S(1)} %copy-done.19, f32[512,1024]{1,0:T(8,128)S(1)} %add.94.mine_ref, f32[512,1024]{1,0:T(8,128)} %collective-permute-done.32.other_ref), custom_call_target="tpu_custom_call" | custom-call | flops 1024 | bytes 1024 | tf_op jit(solution)/shard_map/place/pallas_call | solution.py:184
  292.6 14.3 %collective-permute-done.33.got_ref = f32[152,512]{1,0:T(8,128)S(1)} collective-permute-done((f32[152,512]{1,0:T(8,128)}, f32[152,512]{1,0:T(8,128)S(1)}, u32[]{:S(2)}, u32[]{:S(2)}) %collective-permute-start.33) | collective-permute-done | bytes 311328 | tf_op jit(solution)/shard_map/ppermute | solution.py:764
  309.4 2.9 collective-permute-done.34.got_ref
  (154 shorter events, 94.7 us)
Async XLA Ops:
  5.9 16.1 %collective-permute-start = (f32[128,1024]{1,0:T(8,128)}, f32[128,1024]{1,0:T(8,128)S(1)}, u32[]{:S(2)}, u32[]{:S(2)}) collective-permute-start(f32[128,1024]{1,0:T(8,128)} %get-tuple-element.187), channel_id=1, source_target_pairs={{0,2},{1,3},{2,0},{3,1},{4,6},{5,7},{6,4},{7,5},{8,10},{9,11},{10,... | collective-permute-start | bytes 1572872 | tf_op jit(solution)/shard_map/ppermute | solution.py:735
  23.4 21.6 %collective-permute-start.4 = (f32[2056,1024]{1,0:T(8,128)S(1)}, f32[2056,1024]{1,0:T(8,128)S(1)}, u32[]{:S(2)}, u32[]{:S(2)}) collective-permute-start(f32[2056,1024]{1,0:T(8,128)S(1)} %widen.1), channel_id=1, source_target_pairs={{0,1},{1,0},{2,3},{3,2},{4,5},{5,4},{6,7},{7,6},{8,9},{9,8},{10,11... | collective-permute-start | bytes 25264136 | tf_op jit(solution)/shard_map/ppermute | solution.py:731
  23.5 14.3 %collective-permute-start.1 = (f32[512,256]{1,0:T(8,128)S(1)}, f32[512,256]{1,0:T(8,128)S(1)}, u32[]{:S(2)}, u32[]{:S(2)}) collective-permute-start(f32[512,256]{1,0:T(8,128)S(1)} %get-tuple-element.194), channel_id=1, source_target_pairs={{0,2},{1,3},{2,0},{3,1},{4,6},{5,7},{6,4},{7,5},{8,10},{9,11},{10,... | collective-permute-start | bytes 1572872 | tf_op jit(solution)/shard_map/ppermute | solution.py:735
  24.3 14.0 %collective-permute-start.2 = (f32[128,1024]{1,0:T(8,128)S(1)}, f32[128,1024]{1,0:T(8,128)S(1)}, u32[]{:S(2)}, u32[]{:S(2)}) collective-permute-start(f32[128,1024]{1,0:T(8,128)S(1)} %collective-permute-done.o_got_ref), channel_id=1, source_target_pairs={{0,4},{4,0},{8,12},{12,8},{16,20},{20,16},{24,28},{28,24},{1,5},{5... | collective-permute-start | bytes 1572872 | tf_op jit(solution)/shard_map/ppermute | solution.py:764
  42.9 14.8 %collective-permute-start.6 = (f32[128,1024]{1,0:T(8,128)S(1)}, f32[128,1024]{1,0:T(8,128)S(1)}, u32[]{:S(2)}, u32[]{:S(2)}) collective-permute-start(f32[128,1024]{1,0:T(8,128)S(1)} %get-tuple-element.209), channel_id=1, source_target_pairs={{0,2},{1,3},{2,0},{3,1},{4,6},{5,7},{6,4},{7,5},{8,10},{9,11},{10,... | collective-permute-start | bytes 1572872 | tf_op jit(solution)/shard_map/ppermute | solution.py:735
  44.2 24.8 %collective-permute-start.5 = (f32[128,1024]{1,0:T(8,128)S(1)}, f32[128,1024]{1,0:T(8,128)S(1)}, u32[]{:S(2)}, u32[]{:S(2)}) collective-permute-start(f32[128,1024]{1,0:T(8,128)S(1)} %get-tuple-element.215), channel_id=1, source_target_pairs={{0,2},{1,3},{2,0},{3,1},{4,6},{5,7},{6,4},{7,5},{8,10},{9,11},{10,... | collective-permute-start | bytes 1572872 | tf_op jit(solution)/shard_map/ppermute | solution.py:735
  61.4 18.8 %collective-permute-start.8 = (f32[128,1024]{1,0:T(8,128)S(1)}, f32[128,1024]{1,0:T(8,128)S(1)}, u32[]{:S(2)}, u32[]{:S(2)}) collective-permute-start(f32[128,1024]{1,0:T(8,128)S(1)} %get-tuple-element.220), channel_id=1, source_target_pairs={{0,2},{1,3},{2,0},{3,1},{4,6},{5,7},{6,4},{7,5},{8,10},{9,11},{10,... | collective-permute-start | bytes 1572872 | tf_op jit(solution)/shard_map/ppermute | solution.py:735
  72.7 18.7 %collective-permute-start.7 = (f32[128,1024]{1,0:T(8,128)S(1)}, f32[128,1024]{1,0:T(8,128)S(1)}, u32[]{:S(2)}, u32[]{:S(2)}) collective-permute-start(f32[128,1024]{1,0:T(8,128)S(1)} %get-tuple-element.224), channel_id=1, source_target_pairs={{0,2},{1,3},{2,0},{3,1},{4,6},{5,7},{6,4},{7,5},{8,10},{9,11},{10,... | collective-permute-start | bytes 1572872 | tf_op jit(solution)/shard_map/ppermute | solution.py:735
  80.3 22.4 %collective-permute-start.10 = (f32[128,1024]{1,0:T(8,128)S(1)}, f32[128,1024]{1,0:T(8,128)S(1)}, u32[]{:S(2)}, u32[]{:S(2)}) collective-permute-start(f32[128,1024]{1,0:T(8,128)S(1)} %add.91.y_ref), channel_id=1, source_target_pairs={{0,2},{1,3},{2,0},{3,1},{4,6},{5,7},{6,4},{7,5},{8,10},{9,11},{10,... | collective-permute-start | bytes 1572872 | tf_op jit(solution)/shard_map/ppermute | solution.py:735
  91.5 22.4 %collective-permute-start.9 = (f32[128,1024]{1,0:T(8,128)S(1)}, f32[128,1024]{1,0:T(8,128)S(1)}, u32[]{:S(2)}, u32[]{:S(2)}) collective-permute-start(f32[128,1024]{1,0:T(8,128)S(1)} %add.92.y_ref), channel_id=1, source_target_pairs={{0,2},{1,3},{2,0},{3,1},{4,6},{5,7},{6,4},{7,5},{8,10},{9,11},{10,... | collective-permute-start | bytes 1572872 | tf_op jit(solution)/shard_map/ppermute | solution.py:735
  108.7 15.6 %collective-permute-start.11 = (f32[128,1024]{1,0:T(8,128)S(1)}, f32[128,1024]{1,0:T(8,128)S(1)}, u32[]{:S(2)}, u32[]{:S(2)}) collective-permute-start(f32[128,1024]{1,0:T(8,128)S(1)} %get-tuple-element.238), channel_id=1, source_target_pairs={{0,2},{1,3},{2,0},{3,1},{4,6},{5,7},{6,4},{7,5},{8,10},{9,11},{10,... | collective-permute-start | bytes 1572872 | tf_op jit(solution)/shard_map/ppermute | solution.py:735
  126.2 7.2 %collective-permute-start.14 = (f32[1024,1024]{1,0:T(8,128)S(1)}, f32[1024,1024]{1,0:T(8,128)S(1)}, u32[]{:S(2)}, u32[]{:S(2)}) collective-permute-start(f32[1024,1024]{1,0:T(8,128)S(1)} %pair.4), channel_id=1, source_target_pairs={{0,1},{1,0},{2,3},{3,2},{4,5},{5,4},{6,7},{7,6},{8,9},{9,8},{10,11... | collective-permute-start | bytes 12582920 | tf_op jit(solution)/shard_map/ppermute | solution.py:731
  128.2 11.3 %collective-permute-start.12 = (f32[1024,1024]{1,0:T(8,128)S(1)}, f32[1024,1024]{1,0:T(8,128)S(1)}, u32[]{:S(2)}, u32[]{:S(2)}) collective-permute-start(f32[1024,1024]{1,0:T(8,128)S(1)} %pair.5), channel_id=1, source_target_pairs={{0,1},{1,0},{2,3},{3,2},{4,5},{5,4},{6,7},{7,6},{8,9},{9,8},{10,11... | collective-permute-start | bytes 12582920 | tf_op jit(solution)/shard_map/ppermute | solution.py:731
  128.7 14.2 %collective-permute-start.16 = (f32[128,1024]{1,0:T(8,128)S(1)}, f32[128,1024]{1,0:T(8,128)S(1)}, u32[]{:S(2)}, u32[]{:S(2)}) collective-permute-start(f32[128,1024]{1,0:T(8,128)S(1)} %get-tuple-element.248), channel_id=1, source_target_pairs={{0,2},{1,3},{2,0},{3,1},{4,6},{5,7},{6,4},{7,5},{8,10},{9,11},{10,... | collective-permute-start | bytes 1572872 | tf_op jit(solution)/shard_map/ppermute | solution.py:735
  135.3 50.1 %collective-permute-start.15 = (f32[512,1024]{1,0:T(8,128)S(1)}, f32[512,1024]{1,0:T(8,128)S(1)}, u32[]{:S(2)}, u32[]{:S(2)}) collective-permute-start(f32[512,1024]{1,0:T(8,128)S(1)} %get-tuple-element.258), channel_id=1, source_target_pairs={{0,4},{4,0},{8,12},{12,8},{16,20},{20,16},{24,28},{28,24},{1,5},{5... | collective-permute-start | bytes 6291464 | tf_op jit(solution)/shard_map/ppermute | solution.py:764
  141.3 47.7 %collective-permute-start.13 = (f32[512,1024]{1,0:T(8,128)S(1)}, f32[512,1024]{1,0:T(8,128)S(1)}, u32[]{:S(2)}, u32[]{:S(2)}) collective-permute-start(f32[512,1024]{1,0:T(8,128)S(1)} %get-tuple-element.255), channel_id=1, source_target_pairs={{0,8},{4,12},{8,0},{12,4},{16,24},{20,28},{24,16},{28,20},{1,9},{5... | collective-permute-start | bytes 6291464 | tf_op jit(solution)/shard_map/ppermute | solution.py:764
  148.3 15.5 %collective-permute-start.20 = (f32[544,256]{1,0:T(8,128)S(1)}, f32[544,256]{1,0:T(8,128)S(1)}, u32[]{:S(2)}, u32[]{:S(2)}) collective-permute-start(f32[544,256]{1,0:T(8,128)S(1)} %get-tuple-element.278), channel_id=1, source_target_pairs={{0,2},{1,3},{2,0},{3,1},{4,6},{5,7},{6,4},{7,5},{8,10},{9,11},{10,... | collective-permute-start | bytes 1671176 | tf_op jit(solution)/shard_map/ppermute | solution.py:735
  150.4 25.4 %collective-permute-start.18 = (f32[512,256]{1,0:T(8,128)S(1)}, f32[512,256]{1,0:T(8,128)S(1)}, u32[]{:S(2)}, u32[]{:S(2)}) collective-permute-start(f32[512,256]{1,0:T(8,128)S(1)} %get-tuple-element.281), channel_id=1, source_target_pairs={{0,2},{1,3},{2,0},{3,1},{4,6},{5,7},{6,4},{7,5},{8,10},{9,11},{10,... | collective-permute-start | bytes 1572872 | tf_op jit(solution)/shard_map/ppermute | solution.py:735
  151.2 34.2 %collective-permute-start.19 = (f32[512,256]{1,0:T(8,128)S(1)}, f32[512,256]{1,0:T(8,128)S(1)}, u32[]{:S(2)}, u32[]{:S(2)}) collective-permute-start(f32[512,256]{1,0:T(8,128)S(1)} %get-tuple-element.282), channel_id=1, source_target_pairs={{0,2},{1,3},{2,0},{3,1},{4,6},{5,7},{6,4},{7,5},{8,10},{9,11},{10,... | collective-permute-start | bytes 1572872 | tf_op jit(solution)/shard_map/ppermute | solution.py:735
  192.3 7.1 %collective-permute-start.21 = (f32[512,1024]{1,0:T(8,128)S(1)}, f32[512,1024]{1,0:T(8,128)S(1)}, u32[]{:S(2)}, u32[]{:S(2)}) collective-permute-start(f32[512,1024]{1,0:T(8,128)S(1)} %get-tuple-element.306.near_ref), channel_id=1, source_target_pairs={{0,1},{1,0},{2,3},{3,2},{4,5},{5,4},{6,7},{7,6},{8,9},{9,8},{10,11... | collective-permute-start | bytes 6291464 | tf_op jit(solution)/shard_map/ppermute | solution.py:731
  192.8 25.1 %collective-permute-start.25 = (f32[256,1024]{1,0:T(8,128)S(1)}, f32[256,1024]{1,0:T(8,128)S(1)}, u32[]{:S(2)}, u32[]{:S(2)}) collective-permute-start(f32[256,1024]{1,0:T(8,128)S(1)} %get-tuple-element.303), channel_id=1, source_target_pairs={{0,8},{4,12},{8,0},{12,4},{16,24},{20,28},{24,16},{28,20},{1,9},{5... | collective-permute-start | bytes 3145736 | tf_op jit(solution)/shard_map/ppermute | solution.py:764
  194.4 24.9 %collective-permute-start.24 = (f32[256,1024]{1,0:T(8,128)S(1)}, f32[256,1024]{1,0:T(8,128)S(1)}, u32[]{:S(2)}, u32[]{:S(2)}) collective-permute-start(f32[256,1024]{1,0:T(8,128)S(1)} %get-tuple-element.305), channel_id=1, source_target_pairs={{0,4},{4,0},{8,12},{12,8},{16,20},{20,16},{24,28},{28,24},{1,5},{5... | collective-permute-start | bytes 3145736 | tf_op jit(solution)/shard_map/ppermute | solution.py:764
  196.8 84.5 %collective-permute-start.23 = (f32[512,1024]{1,0:T(8,128)S(1)}, f32[512,1024]{1,0:T(8,128)S(1)}, u32[]{:S(2)}, u32[]{:S(2)}) collective-permute-start(f32[512,1024]{1,0:T(8,128)S(1)} %get-tuple-element.311), channel_id=1, source_target_pairs={{0,2},{1,3},{2,0},{3,1},{4,6},{5,7},{6,4},{7,5},{8,10},{9,11},{10,... | collective-permute-start | bytes 6291464 | tf_op jit(solution)/shard_map/ppermute | solution.py:735
  220.0 25.1 %collective-permute-start.29 = (f32[536,512]{1,0:T(8,128)S(1)}, f32[536,512]{1,0:T(8,128)S(1)}, u32[]{:S(2)}, u32[]{:S(2)}) collective-permute-start(f32[536,512]{1,0:T(8,128)S(1)} %get-tuple-element.328), channel_id=1, source_target_pairs={{0,4},{4,0},{8,12},{12,8},{16,20},{20,16},{24,28},{28,24},{1,5},{5... | collective-permute-start | bytes 3293192 | tf_op jit(solution)/shard_map/ppermute | solution.py:764
  221.5 48.5 %collective-permute-start.26 = (f32[512,512]{1,0:T(8,128)S(1)}, f32[512,512]{1,0:T(8,128)S(1)}, u32[]{:S(2)}, u32[]{:S(2)}) collective-permute-start(f32[512,512]{1,0:T(8,128)S(1)} %get-tuple-element.324), channel_id=1, source_target_pairs={{0,8},{4,12},{8,0},{12,4},{16,24},{20,28},{24,16},{28,20},{1,9},{5... | collective-permute-start | bytes 3145736 | tf_op jit(solution)/shard_map/ppermute | solution.py:764
  222.5 34.9 %collective-permute-start.28 = (f32[128,1024]{1,0:T(8,128)S(1)}, f32[128,1024]{1,0:T(8,128)S(1)}, u32[]{:S(2)}, u32[]{:S(2)}) collective-permute-start(f32[128,1024]{1,0:T(8,128)S(1)} %get-tuple-element.321), channel_id=1, source_target_pairs={{0,16},{4,20},{8,24},{12,28},{16,0},{20,4},{24,8},{28,12},{1,17},{... | collective-permute-start | bytes 1572872 | tf_op jit(solution)/shard_map/ppermute | solution.py:764
  225.1 43.5 %collective-permute-start.27 = (f32[128,1024]{1,0:T(8,128)S(1)}, f32[128,1024]{1,0:T(8,128)S(1)}, u32[]{:S(2)}, u32[]{:S(2)}) collective-permute-start(f32[128,1024]{1,0:T(8,128)S(1)} %get-tuple-element.323), channel_id=1, source_target_pairs={{0,16},{4,20},{8,24},{12,28},{16,0},{20,4},{24,8},{28,12},{1,17},{... | collective-permute-start | bytes 1572872 | tf_op jit(solution)/shard_map/ppermute | solution.py:764
  245.7 34.3 %collective-permute-start.31 = (f32[280,512]{1,0:T(8,128)S(1)}, f32[280,512]{1,0:T(8,128)S(1)}, u32[]{:S(2)}, u32[]{:S(2)}) collective-permute-start(f32[280,512]{1,0:T(8,128)S(1)} %get-tuple-element.331), channel_id=1, source_target_pairs={{0,8},{4,12},{8,0},{12,4},{16,24},{20,28},{24,16},{28,20},{1,9},{5... | collective-permute-start | bytes 1720328 | tf_op jit(solution)/shard_map/ppermute | solution.py:764
  270.7 9.9 %collective-permute-start.30 = (f32[256,512]{1,0:T(8,128)S(1)}, f32[256,512]{1,0:T(8,128)S(1)}, u32[]{:S(2)}, u32[]{:S(2)}) collective-permute-start(f32[256,512]{1,0:T(8,128)S(1)} %get-tuple-element.336), channel_id=1, source_target_pairs={{0,4},{4,0},{8,12},{12,8},{16,20},{20,16},{24,28},{28,24},{1,5},{5... | collective-permute-start | bytes 1572872 | tf_op jit(solution)/shard_map/ppermute | solution.py:764
  282.0 7.0 %collective-permute-start.32 = (f32[512,1024]{1,0:T(8,128)S(1)}, f32[512,1024]{1,0:T(8,128)}, u32[]{:S(2)}, u32[]{:S(2)}) collective-permute-start(f32[512,1024]{1,0:T(8,128)S(1)} %add.94.mine_ref), channel_id=1, source_target_pairs={{0,1},{1,0},{2,3},{3,2},{4,5},{5,4},{6,7},{7,6},{8,9},{9,8},{10,11... | collective-permute-start | bytes 6291464 | tf_op jit(solution)/shard_map/ppermute | solution.py:731
  282.8 24.1 %collective-permute-start.33 = (f32[152,512]{1,0:T(8,128)}, f32[152,512]{1,0:T(8,128)S(1)}, u32[]{:S(2)}, u32[]{:S(2)}) collective-permute-start(f32[152,512]{1,0:T(8,128)} %copy-done.23), channel_id=1, source_target_pairs={{0,16},{4,20},{8,24},{12,28},{16,0},{20,4},{24,8},{28,12},{1,17},{... | collective-permute-start | bytes 933896 | tf_op jit(solution)/shard_map/ppermute | solution.py:764
  288.9 23.4 %collective-permute-start.34 = (f32[128,512]{1,0:T(8,128)}, f32[128,512]{1,0:T(8,128)S(1)}, u32[]{:S(2)}, u32[]{:S(2)}) collective-permute-start(f32[128,512]{1,0:T(8,128)} %copy-done.24), channel_id=1, source_target_pairs={{0,16},{4,20},{8,24},{12,28},{16,0},{20,4},{24,8},{28,12},{1,17},{... | collective-permute-start | bytes 786440 | tf_op jit(solution)/shard_map/ppermute | solution.py:764
  (28 other events, 222.1 us)

commit v3 on v2

--- a/solution.py
+++ b/solution.py
@@ -1080,16 +1080,16 @@
     o_got = line.hold(*o_got)
     line.mark(*o_got)
     down_sum.step()
-    up_sum.step()
     in_mine, in_away = whole(
         input_kernel,
         "input_grad",
         [line.hold(grad_q_near), grad_q_far, grad_k, grad_v, q_weight, k_weight, v_weight, first_ext],
         [shape(half, width)] * 2,
     )
+    line.mark(in_mine)
+    up_sum.step()
     in_got = swap_core(in_away)
     out_far = swap_core(line.hold(out_wide))
-    line.mark(in_mine)
     in_kept, in_sent = whole(
         chip_kernel, "chip_sum", [in_mine, line.hold(in_got)], [shape(half, width)] * 2
     )

time: 315 us -> 313 us (level)
  transfers between devices with their start and end apart: 35 -> 35, of which waited for: 26 -> 26; matrix products, arithmetic and copies ran while one was open for 2% -> 2% of each run, Pallas kernels for 32% -> 33%
where the time goes in v3:
time: 313 us
  waiting for transfers between devices  151 us (48%)
  Pallas kernels  109 us (35%)
  starting transfers between devices  37.5 us (12%)
  local copies, waits for them, and re-layouts  12.1 us (4%)
    ppermute x13, waiting for transfers between devices, dp_swap(): return lax.ppermute(value, 'dp', [(i, i ^ 1 << bit) for i in range(parts)])  82.5 us
    pallas_call x41, Pallas kernels, whole(): pl.pallas_call(kernel, in_specs=[pl.BlockSpec(memory_space=pltpu.SMEM)] *...  72.6 us
    ppermute x14, waiting for transfers between devices, swap_chip(): return lax.ppermute(value, 'mp', [(i, i ^ 2) for i in range(4)])  54.8 us
    pallas_call x2, Pallas kernels, attn_bwd(): pl.pallas_call(functools.partial(attn_bwd_kernel, bool(sums)), grid=(rows...  19.6 us
    ppermute x14, starting transfers between devices, swap_chip(): return lax.ppermute(value, 'mp', [(i, i ^ 2) for i in range(4)])  18.2 us
    ppermute x13, starting transfers between devices, dp_swap(): return lax.ppermute(value, 'dp', [(i, i ^ 1 << bit) for i in range(parts)])  17.7 us
    ppermute x8, waiting for transfers between devices, swap_core(): return lax.ppermute(value, 'mp', [(i, i ^ 1) for i in range(4)])  13.6 us
    pallas_call x2, Pallas kernels, attn_fwd(): pl.pallas_call(attn_fwd_kernel, grid=(rows // block,), in_specs=[pl.Block...  8.78 us
  transfers between devices with their start and end apart: 35, of which 26 were waited for; matrix products, arithmetic and copies ran while one was open for 2% of the time, Pallas kernels for 33%

profile of v3, /device:TPU:0, one launch (start us, length us, event | category | flops | bytes accessed | tf_op | source)
XLA Modules:
  0.0 312.8 jit_solution(5940680337514499675)
XLA Ops:
  5.9 3.0 collective-permute-start
  8.9 5.6 %qkv.1 = (f32[8,256]{1,0:T(8,128)}, bf16[1024,1024]{1,0:T(8,128)(2,1)}, bf16[512,256]{1,0:T(8,128)(2,1)}, bf16[512,256]{1,0:T(8,128)(2,1)}, bf16[1024,256]{1,0:T(8,128)(2,1)}, /*index=5*/bf16[1024,256]{1,0:T(8,128)(2,1)}) custom-call(s32[13]{0:T(128)} %concatenate.30.meta_ref, bf16[1024,1024]{1,0:T(8,128)(2,1)} %all_ref, bf16[1024,256]{1,0:T(8,128)(2,1)} %qw_ref.3, ...), custom_call_target="tpu_custom_call" | custom-call | flops 1024 | bytes 1024 | tf_op jit(solution)/shard_map/qkv/pallas_call | solution.py:342
  17.5 4.4 %attn_fwd.2 = (f32[512,256]{1,0:T(8,128)S(1)}, f32[512,128]{1,0:T(8,128)S(1)}) custom-call(bf16[512,256]{1,0:T(8,128)(2,1)S(1)} %copy-done.16, bf16[1024,256]{1,0:T(8,128)(2,1)S(1)} %copy-done.3, bf16[1024,256]{1,0:T(8,128)(2,1)S(1)} %copy-done.5, f32[1,1024]{1,0:T(1,128)S(1)} %compare_select_fusion.bias_ref.refs_4_), custom_call_target="tpu_custom_call" | custom-call | flops 1024 | bytes 1024 | tf_op jit(solution)/shard_map/attn_fwd/pallas_call | solution.py:64
  25.9 4.4 %attn_fwd.3 = (bf16[512,256]{1,0:T(8,128)(2,1)S(1)}, f32[512,128]{1,0:T(8,128)S(1)}) custom-call(bf16[512,256]{1,0:T(8,128)(2,1)S(1)} %copy-done.18, bf16[1024,256]{1,0:T(8,128)(2,1)S(1)} %copy-done.3, bf16[1024,256]{1,0:T(8,128)(2,1)S(1)} %copy-done.5, f32[1,1024]{1,0:T(1,128)S(1)} %compare_select_fusion.bias_ref.refs_4_), custom_call_target="tpu_custom_call" | custom-call | flops 1024 | bytes 1024 | tf_op jit(solution)/shard_map/attn_fwd/pallas_call | solution.py:64
  31.1 6.7 %collective-permute-done.1.other_ref = f32[512,256]{1,0:T(8,128)S(1)} collective-permute-done((f32[512,256]{1,0:T(8,128)S(1)}, f32[512,256]{1,0:T(8,128)S(1)}, u32[]{:S(2)}, u32[]{:S(2)}) %collective-permute-start.1) | collective-permute-done | bytes 524320 | tf_op jit(solution)/shard_map/ppermute | solution.py:735
  45.5 5.2 %feed.3 = (bf16[512,1024]{1,0:T(8,128)(2,1)S(1)}, bf16[512,2048]{1,0:T(8,128)(2,1)S(1)}, f32[256,2048]{1,0:T(8,128)S(1)}, f32[128,1024]{1,0:T(8,128)S(1)}, f32[128,1024]{1,0:T(8,128)S(1)}) custom-call(f32[256,1024]{1,0:T(8,128)S(1)} %get-tuple-element.208.refs_0_, bf16[1024,1024]{1,0:T(8,128)(2,1)S(1)} %copy-done, ...), custom_call_target="tpu_custom_call" | custom-call | flops 1024 | bytes 1024 | tf_op jit(solution)/shard_map/feed/pallas_call | solution.py:184
  50.7 7.0 %collective-permute-done.6.refs_0_ = f32[128,1024]{1,0:T(8,128)S(1)} collective-permute-done((f32[128,1024]{1,0:T(8,128)S(1)}, f32[128,1024]{1,0:T(8,128)S(1)}, u32[]{:S(2)}, u32[]{:S(2)}) %collective-permute-start.6) | collective-permute-done | bytes 524320 | tf_op jit(solution)/shard_map/ppermute | solution.py:735
  57.7 3.7 %feed.4 = (bf16[512,1024]{1,0:T(8,128)(2,1)S(1)}, bf16[512,2048]{1,0:T(8,128)(2,1)S(1)}, f32[128,2048]{1,0:T(8,128)S(1)}, f32[128,1024]{1,0:T(8,128)S(1)}) custom-call(f32[128,1024]{1,0:T(8,128)S(1)} %collective-permute-done.6.refs_0_, bf16[1024,1024]{1,0:T(8,128)(2,1)S(1)} %copy-done, ...), custom_call_target="tpu_custom_call", output_to_operand_aliasing={{0}: (7, {}), {1}: (8, {})} | custom-call | flops 1024 | bytes 1024 | tf_op jit(solution)/shard_map/feed/pallas_call | solution.py:184
  62.7 6.2 %collective-permute-done.5.refs_0_ = f32[128,1024]{1,0:T(8,128)S(1)} collective-permute-done((f32[128,1024]{1,0:T(8,128)S(1)}, f32[128,1024]{1,0:T(8,128)S(1)}, u32[]{:S(2)}, u32[]{:S(2)}) %collective-permute-start.5) | collective-permute-done | bytes 524320 | tf_op jit(solution)/shard_map/ppermute | solution.py:735
  69.0 3.7 %feed.5 = (bf16[512,1024]{1,0:T(8,128)(2,1)S(1)}, bf16[512,2048]{1,0:T(8,128)(2,1)S(1)}, f32[128,2048]{1,0:T(8,128)S(1)}, f32[128,1024]{1,0:T(8,128)S(1)}) custom-call(f32[128,1024]{1,0:T(8,128)S(1)} %collective-permute-done.5.refs_0_, bf16[1024,1024]{1,0:T(8,128)(2,1)S(1)} %copy-done, ...), custom_call_target="tpu_custom_call", output_to_operand_aliasing={{0}: (7, {}), {1}: (8, {})} | custom-call | flops 1024 | bytes 1024 | tf_op jit(solution)/shard_map/feed/pallas_call | solution.py:184
  74.0 6.2 %collective-permute-done.8.refs_1_ = f32[128,1024]{1,0:T(8,128)S(1)} collective-permute-done((f32[128,1024]{1,0:T(8,128)S(1)}, f32[128,1024]{1,0:T(8,128)S(1)}, u32[]{:S(2)}, u32[]{:S(2)}) %collective-permute-start.8) | collective-permute-done | bytes 524320 | tf_op jit(solution)/shard_map/ppermute | solution.py:735
  81.5 6.2 %feed_back.4 = (f32[512,1024]{1,0:T(8,128)S(1)}, bf16[512,1024]{1,0:T(8,128)(2,1)S(1)}, bf16[512,2048]{1,0:T(8,128)(2,1)S(1)}, f32[128,1024]{1,0:T(8,128)S(1)}, ...) custom-call(s32[13]{0:T(128)S(1)} %copy-done.19, ...), custom_call_target="tpu_custom_call" | custom-call | flops 1024 | bytes 1024 | tf_op jit(solution)/shard_map/feed_back/pallas_call | solution.py:184
  87.7 3.7 %collective-permute-done.7.refs_1_ = f32[128,1024]{1,0:T(8,128)S(1)} collective-permute-done((f32[128,1024]{1,0:T(8,128)S(1)}, f32[128,1024]{1,0:T(8,128)S(1)}, u32[]{:S(2)}, u32[]{:S(2)}) %collective-permute-start.7) | collective-permute-done | bytes 524320 | tf_op jit(solution)/shard_map/ppermute | solution.py:735
  92.8 6.2 %feed_back.5 = (f32[512,1024]{1,0:T(8,128)S(1)}, bf16[512,1024]{1,0:T(8,128)(2,1)S(1)}, bf16[512,2048]{1,0:T(8,128)(2,1)S(1)}, f32[128,1024]{1,0:T(8,128)S(1)}, ...) custom-call(s32[13]{0:T(128)S(1)} %copy-done.19, ...), custom_call_target="tpu_custom_call", output_to_operand_aliasing={{0}: (10, {}), {1}: (11, {}), {2}: (12, {})} | custom-call | flops 1024 | bytes 1024 | tf_op jit(solution)/shard_map/feed_back/pallas_call | solution.py:184
  98.9 3.7 %collective-permute-done.10.y_ref = f32[128,1024]{1,0:T(8,128)S(1)} collective-permute-done((f32[128,1024]{1,0:T(8,128)S(1)}, f32[128,1024]{1,0:T(8,128)S(1)}, u32[]{:S(2)}, u32[]{:S(2)}) %collective-permute-start.10) | collective-permute-done | bytes 524320 | tf_op jit(solution)/shard_map/ppermute | solution.py:735
  102.7 5.9 %feed_back.6 = (f32[512,1024]{1,0:T(8,128)S(1)}, bf16[512,1024]{1,0:T(8,128)(2,1)S(1)}, bf16[512,2048]{1,0:T(8,128)(2,1)S(1)}, f32[128,1024]{1,0:T(8,128)S(1)}, ...) custom-call(s32[13]{0:T(128)S(1)} %copy-done.19, ...), custom_call_target="tpu_custom_call", output_to_operand_aliasing={{0}: (10, {}), {1}: (11, {}), {2}: (12, {})} | custom-call | flops 1024 | bytes 1024 | tf_op jit(solution)/shard_map/feed_back/pallas_call | solution.py:184
  109.8 4.1 %collective-permute-done.9.y_ref = f32[128,1024]{1,0:T(8,128)S(1)} collective-permute-done((f32[128,1024]{1,0:T(8,128)S(1)}, f32[128,1024]{1,0:T(8,128)S(1)}, u32[]{:S(2)}, u32[]{:S(2)}) %collective-permute-start.9) | collective-permute-done | bytes 524320 | tf_op jit(solution)/shard_map/ppermute | solution.py:735
  113.9 5.9 %feed_back.7 = (f32[512,1024]{1,0:T(8,128)S(1)}, bf16[512,1024]{1,0:T(8,128)(2,1)S(1)}, bf16[512,2048]{1,0:T(8,128)(2,1)S(1)}, f32[128,1024]{1,0:T(8,128)S(1)}, ...) custom-call(s32[13]{0:T(128)S(1)} %copy-done.19, ...), custom_call_target="tpu_custom_call", output_to_operand_aliasing={{0}: (10, {}), {1}: (11, {}), {2}: (12, {})} | custom-call | flops 1024 | bytes 1024 | tf_op jit(solution)/shard_map/feed_back/pallas_call | solution.py:184
  119.8 4.6 %collective-permute-done.11.refs_1_ = f32[128,1024]{1,0:T(8,128)S(1)} collective-permute-done((f32[128,1024]{1,0:T(8,128)S(1)}, f32[128,1024]{1,0:T(8,128)S(1)}, u32[]{:S(2)}, u32[]{:S(2)}) %collective-permute-start.11) | collective-permute-done | bytes 524320 | tf_op jit(solution)/shard_map/ppermute | solution.py:735
  129.9 3.5 %collective-permute-done.15.refs_0_ = f32[1024,1024]{1,0:T(8,128)S(1)} collective-permute-done((f32[1024,1024]{1,0:T(8,128)S(1)}, f32[1024,1024]{1,0:T(8,128)S(1)}, u32[]{:S(2)}, u32[]{:S(2)}) %collective-permute-start.15) | collective-permute-done | bytes 4194336 | tf_op jit(solution)/shard_map/ppermute | solution.py:731
  153.7 9.8 %attn_bwd.2 = (bf16[512,256]{1,0:T(8,128)(2,1)S(1)}, f32[1024,256]{1,0:T(8,128)S(1)}, f32[1024,256]{1,0:T(8,128)S(1)}) custom-call(bf16[512,256]{1,0:T(8,128)(2,1)S(1)} %copy-done.18, bf16[512,256]{1,0:T(8,128)(2,1)S(1)} %get-tuple-element.282.refs_1_, bf16[1024,256]{1,0:T(8,128)(2,1)S(1)} %copy-done.4, bf16[1024,256]{1,0:T(8,128)(2,1)S(1)} %copy-done.6, ...), custom_call_target="tpu_custom_call" | custom-call | flops 1024 | bytes 1024 | tf_op jit(solution)/shard_map/attn_bwd/pallas_call | solution.py:135
  165.1 9.8 %attn_bwd.3 = (bf16[512,256]{1,0:T(8,128)(2,1)S(1)}, bf16[1024,256]{1,0:T(8,128)(2,1)S(1)}, bf16[1024,256]{1,0:T(8,128)(2,1)S(1)}) custom-call(bf16[512,256]{1,0:T(8,128)(2,1)S(1)} %copy-done.17, f32[544,256]{1,0:T(8,128)S(1)} %collective-permute-done.20.refs_1_.far_sums_ref, bf16[1024,256]{1,0:T(8,128)(2,1)S(1)} %copy-done.4, ...), custom_call_target="tpu_custom_call" | custom-call | flops 1024 | bytes 1024 | tf_op jit(solution)/shard_map/attn_bwd/pallas_call | solution.py:135
  177.0 9.7 %collective-permute-done.19.got_b_ref = f32[512,256]{1,0:T(8,128)S(1)} collective-permute-done((f32[512,256]{1,0:T(8,128)S(1)}, f32[512,256]{1,0:T(8,128)S(1)}, u32[]{:S(2)}, u32[]{:S(2)}) %collective-permute-start.19) | collective-permute-done | bytes 524320 | tf_op jit(solution)/shard_map/ppermute | solution.py:735
  200.7 15.8 %collective-permute-done.25.got_ref = f32[256,1024]{1,0:T(8,128)S(1)} collective-permute-done((f32[256,1024]{1,0:T(8,128)S(1)}, f32[256,1024]{1,0:T(8,128)S(1)}, u32[]{:S(2)}, u32[]{:S(2)}) %collective-permute-start.25) | collective-permute-done | bytes 1048608 | tf_op jit(solution)/shard_map/ppermute | solution.py:764
  223.4 19.9 %collective-permute-done.29.got_ref = f32[536,512]{1,0:T(8,128)S(1)} collective-permute-done((f32[536,512]{1,0:T(8,128)S(1)}, f32[536,512]{1,0:T(8,128)S(1)}, u32[]{:S(2)}, u32[]{:S(2)}) %collective-permute-start.29) | collective-permute-done | bytes 1097760 | tf_op jit(solution)/shard_map/ppermute | solution.py:764
  245.4 10.0 %collective-permute-done.28.got_ref = f32[128,1024]{1,0:T(8,128)S(1)} collective-permute-done((f32[128,1024]{1,0:T(8,128)S(1)}, f32[128,1024]{1,0:T(8,128)S(1)}, u32[]{:S(2)}, u32[]{:S(2)}) %collective-permute-start.28) | collective-permute-done | bytes 524320 | tf_op jit(solution)/shard_map/ppermute | solution.py:764
  256.8 9.8 %collective-permute-done.27.got_ref = f32[128,1024]{1,0:T(8,128)S(1)} collective-permute-done((f32[128,1024]{1,0:T(8,128)S(1)}, f32[128,1024]{1,0:T(8,128)S(1)}, u32[]{:S(2)}, u32[]{:S(2)}) %collective-permute-start.27) | collective-permute-done | bytes 524320 | tf_op jit(solution)/shard_map/ppermute | solution.py:764
  269.3 9.0 %collective-permute-done.31.got_ref = f32[280,512]{1,0:T(8,128)S(1)} collective-permute-done((f32[280,512]{1,0:T(8,128)S(1)}, f32[280,512]{1,0:T(8,128)S(1)}, u32[]{:S(2)}, u32[]{:S(2)}) %collective-permute-start.31) | collective-permute-done | bytes 573472 | tf_op jit(solution)/shard_map/ppermute | solution.py:764
  281.3 3.4 %collective-permute-start.33 = (f32[152,512]{1,0:T(8,128)}, f32[152,512]{1,0:T(8,128)S(1)}, u32[]{:S(2)}, u32[]{:S(2)}) collective-permute-start(f32[152,512]{1,0:T(8,128)} %copy-done.23), channel_id=1, source_target_pairs={{0,16},{4,20},{8,24},{12,28},{16,0},{20,4},{24,8},{28,12},{1,17},{... | collective-permute-start | bytes 933896 | tf_op jit(solution)/shard_map/ppermute | solution.py:764
  287.5 3.7 %place.1 = f32[1024,1024]{1,0:T(8,128)} custom-call(s32[13]{0:T(128)S(1)} %copy-done.19, f32[512,1024]{1,0:T(8,128)S(1)} %add.94.mine_ref, f32[512,1024]{1,0:T(8,128)} %collective-permute-done.32.other_ref), custom_call_target="tpu_custom_call" | custom-call | flops 1024 | bytes 1024 | tf_op jit(solution)/shard_map/place/pallas_call | solution.py:184
  291.2 14.3 %collective-permute-done.33.got_ref = f32[152,512]{1,0:T(8,128)S(1)} collective-permute-done((f32[152,512]{1,0:T(8,128)}, f32[152,512]{1,0:T(8,128)S(1)}, u32[]{:S(2)}, u32[]{:S(2)}) %collective-permute-start.33) | collective-permute-done | bytes 311328 | tf_op jit(solution)/shard_map/ppermute | solution.py:764
  308.0 2.9 collective-permute-done.34.got_ref
  (154 shorter events, 92.2 us)
Async XLA Ops:
  5.9 16.1 %collective-permute-start = (f32[128,1024]{1,0:T(8,128)}, f32[128,1024]{1,0:T(8,128)S(1)}, u32[]{:S(2)}, u32[]{:S(2)}) collective-permute-start(f32[128,1024]{1,0:T(8,128)} %get-tuple-element.187), channel_id=1, source_target_pairs={{0,2},{1,3},{2,0},{3,1},{4,6},{5,7},{6,4},{7,5},{8,10},{9,11},{10,... | collective-permute-start | bytes 1572872 | tf_op jit(solution)/shard_map/ppermute | solution.py:735
  23.4 21.6 %collective-permute-start.4 = (f32[2056,1024]{1,0:T(8,128)S(1)}, f32[2056,1024]{1,0:T(8,128)S(1)}, u32[]{:S(2)}, u32[]{:S(2)}) collective-permute-start(f32[2056,1024]{1,0:T(8,128)S(1)} %widen.1), channel_id=1, source_target_pairs={{0,1},{1,0},{2,3},{3,2},{4,5},{5,4},{6,7},{7,6},{8,9},{9,8},{10,11... | collective-permute-start | bytes 25264136 | tf_op jit(solution)/shard_map/ppermute | solution.py:731
  23.5 14.3 %collective-permute-start.1 = (f32[512,256]{1,0:T(8,128)S(1)}, f32[512,256]{1,0:T(8,128)S(1)}, u32[]{:S(2)}, u32[]{:S(2)}) collective-permute-start(f32[512,256]{1,0:T(8,128)S(1)} %get-tuple-element.194), channel_id=1, source_target_pairs={{0,2},{1,3},{2,0},{3,1},{4,6},{5,7},{6,4},{7,5},{8,10},{9,11},{10,... | collective-permute-start | bytes 1572872 | tf_op jit(solution)/shard_map/ppermute | solution.py:735
  24.3 14.0 %collective-permute-start.2 = (f32[128,1024]{1,0:T(8,128)S(1)}, f32[128,1024]{1,0:T(8,128)S(1)}, u32[]{:S(2)}, u32[]{:S(2)}) collective-permute-start(f32[128,1024]{1,0:T(8,128)S(1)} %collective-permute-done.o_got_ref), channel_id=1, source_target_pairs={{0,4},{4,0},{8,12},{12,8},{16,20},{20,16},{24,28},{28,24},{1,5},{5... | collective-permute-start | bytes 1572872 | tf_op jit(solution)/shard_map/ppermute | solution.py:764
  42.9 14.8 %collective-permute-start.6 = (f32[128,1024]{1,0:T(8,128)S(1)}, f32[128,1024]{1,0:T(8,128)S(1)}, u32[]{:S(2)}, u32[]{:S(2)}) collective-permute-start(f32[128,1024]{1,0:T(8,128)S(1)} %get-tuple-element.209), channel_id=1, source_target_pairs={{0,2},{1,3},{2,0},{3,1},{4,6},{5,7},{6,4},{7,5},{8,10},{9,11},{10,... | collective-permute-start | bytes 1572872 | tf_op jit(solution)/shard_map/ppermute | solution.py:735
  44.2 24.8 %collective-permute-start.5 = (f32[128,1024]{1,0:T(8,128)S(1)}, f32[128,1024]{1,0:T(8,128)S(1)}, u32[]{:S(2)}, u32[]{:S(2)}) collective-permute-start(f32[128,1024]{1,0:T(8,128)S(1)} %get-tuple-element.215), channel_id=1, source_target_pairs={{0,2},{1,3},{2,0},{3,1},{4,6},{5,7},{6,4},{7,5},{8,10},{9,11},{10,... | collective-permute-start | bytes 1572872 | tf_op jit(solution)/shard_map/ppermute | solution.py:735
  61.4 18.8 %collective-permute-start.8 = (f32[128,1024]{1,0:T(8,128)S(1)}, f32[128,1024]{1,0:T(8,128)S(1)}, u32[]{:S(2)}, u32[]{:S(2)}) collective-permute-start(f32[128,1024]{1,0:T(8,128)S(1)} %get-tuple-element.220), channel_id=1, source_target_pairs={{0,2},{1,3},{2,0},{3,1},{4,6},{5,7},{6,4},{7,5},{8,10},{9,11},{10,... | collective-permute-start | bytes 1572872 | tf_op jit(solution)/shard_map/ppermute | solution.py:735
  72.7 18.7 %collective-permute-start.7 = (f32[128,1024]{1,0:T(8,128)S(1)}, f32[128,1024]{1,0:T(8,128)S(1)}, u32[]{:S(2)}, u32[]{:S(2)}) collective-permute-start(f32[128,1024]{1,0:T(8,128)S(1)} %get-tuple-element.224), channel_id=1, source_target_pairs={{0,2},{1,3},{2,0},{3,1},{4,6},{5,7},{6,4},{7,5},{8,10},{9,11},{10,... | collective-permute-start | bytes 1572872 | tf_op jit(solution)/shard_map/ppermute | solution.py:735
  80.3 22.4 %collective-permute-start.10 = (f32[128,1024]{1,0:T(8,128)S(1)}, f32[128,1024]{1,0:T(8,128)S(1)}, u32[]{:S(2)}, u32[]{:S(2)}) collective-permute-start(f32[128,1024]{1,0:T(8,128)S(1)} %add.91.y_ref), channel_id=1, source_target_pairs={{0,2},{1,3},{2,0},{3,1},{4,6},{5,7},{6,4},{7,5},{8,10},{9,11},{10,... | collective-permute-start | bytes 1572872 | tf_op jit(solution)/shard_map/ppermute | solution.py:735
  91.5 22.4 %collective-permute-start.9 = (f32[128,1024]{1,0:T(8,128)S(1)}, f32[128,1024]{1,0:T(8,128)S(1)}, u32[]{:S(2)}, u32[]{:S(2)}) collective-permute-start(f32[128,1024]{1,0:T(8,128)S(1)} %add.92.y_ref), channel_id=1, source_target_pairs={{0,2},{1,3},{2,0},{3,1},{4,6},{5,7},{6,4},{7,5},{8,10},{9,11},{10,... | collective-permute-start | bytes 1572872 | tf_op jit(solution)/shard_map/ppermute | solution.py:735
  108.5 15.8 %collective-permute-start.11 = (f32[128,1024]{1,0:T(8,128)S(1)}, f32[128,1024]{1,0:T(8,128)S(1)}, u32[]{:S(2)}, u32[]{:S(2)}) collective-permute-start(f32[128,1024]{1,0:T(8,128)S(1)} %get-tuple-element.238), channel_id=1, source_target_pairs={{0,2},{1,3},{2,0},{3,1},{4,6},{5,7},{6,4},{7,5},{8,10},{9,11},{10,... | collective-permute-start | bytes 1572872 | tf_op jit(solution)/shard_map/ppermute | solution.py:735
  126.2 7.2 %collective-permute-start.15 = (f32[1024,1024]{1,0:T(8,128)S(1)}, f32[1024,1024]{1,0:T(8,128)S(1)}, u32[]{:S(2)}, u32[]{:S(2)}) collective-permute-start(f32[1024,1024]{1,0:T(8,128)S(1)} %pair.4), channel_id=1, source_target_pairs={{0,1},{1,0},{2,3},{3,2},{4,5},{5,4},{6,7},{7,6},{8,9},{9,8},{10,11... | collective-permute-start | bytes 12582920 | tf_op jit(solution)/shard_map/ppermute | solution.py:731
  128.2 11.3 %collective-permute-start.12 = (f32[1024,1024]{1,0:T(8,128)S(1)}, f32[1024,1024]{1,0:T(8,128)S(1)}, u32[]{:S(2)}, u32[]{:S(2)}) collective-permute-start(f32[1024,1024]{1,0:T(8,128)S(1)} %pair.5), channel_id=1, source_target_pairs={{0,1},{1,0},{2,3},{3,2},{4,5},{5,4},{6,7},{7,6},{8,9},{9,8},{10,11... | collective-permute-start | bytes 12582920 | tf_op jit(solution)/shard_map/ppermute | solution.py:731
  128.7 13.9 %collective-permute-start.14 = (f32[128,1024]{1,0:T(8,128)S(1)}, f32[128,1024]{1,0:T(8,128)S(1)}, u32[]{:S(2)}, u32[]{:S(2)}) collective-permute-start(f32[128,1024]{1,0:T(8,128)S(1)} %get-tuple-element.248), channel_id=1, source_target_pairs={{0,2},{1,3},{2,0},{3,1},{4,6},{5,7},{6,4},{7,5},{8,10},{9,11},{10,... | collective-permute-start | bytes 1572872 | tf_op jit(solution)/shard_map/ppermute | solution.py:735
  135.3 51.4 %collective-permute-start.17 = (f32[512,1024]{1,0:T(8,128)S(1)}, f32[512,1024]{1,0:T(8,128)S(1)}, u32[]{:S(2)}, u32[]{:S(2)}) collective-permute-start(f32[512,1024]{1,0:T(8,128)S(1)} %get-tuple-element.285), channel_id=1, source_target_pairs={{0,4},{4,0},{8,12},{12,8},{16,20},{20,16},{24,28},{28,24},{1,5},{5... | collective-permute-start | bytes 6291464 | tf_op jit(solution)/shard_map/ppermute | solution.py:764
  142.6 47.4 %collective-permute-start.13 = (f32[512,1024]{1,0:T(8,128)S(1)}, f32[512,1024]{1,0:T(8,128)S(1)}, u32[]{:S(2)}, u32[]{:S(2)}) collective-permute-start(f32[512,1024]{1,0:T(8,128)S(1)} %get-tuple-element.255), channel_id=1, source_target_pairs={{0,8},{4,12},{8,0},{12,4},{16,24},{20,28},{24,16},{28,20},{1,9},{5... | collective-permute-start | bytes 6291464 | tf_op jit(solution)/shard_map/ppermute | solution.py:764
  149.6 15.5 %collective-permute-start.20 = (f32[544,256]{1,0:T(8,128)S(1)}, f32[544,256]{1,0:T(8,128)S(1)}, u32[]{:S(2)}, u32[]{:S(2)}) collective-permute-start(f32[544,256]{1,0:T(8,128)S(1)} %get-tuple-element.277), channel_id=1, source_target_pairs={{0,2},{1,3},{2,0},{3,1},{4,6},{5,7},{6,4},{7,5},{8,10},{9,11},{10,... | collective-permute-start | bytes 1671176 | tf_op jit(solution)/shard_map/ppermute | solution.py:735
  151.6 25.4 %collective-permute-start.18 = (f32[512,256]{1,0:T(8,128)S(1)}, f32[512,256]{1,0:T(8,128)S(1)}, u32[]{:S(2)}, u32[]{:S(2)}) collective-permute-start(f32[512,256]{1,0:T(8,128)S(1)} %get-tuple-element.286), channel_id=1, source_target_pairs={{0,2},{1,3},{2,0},{3,1},{4,6},{5,7},{6,4},{7,5},{8,10},{9,11},{10,... | collective-permute-start | bytes 1572872 | tf_op jit(solution)/shard_map/ppermute | solution.py:735
  152.5 34.2 %collective-permute-start.19 = (f32[512,256]{1,0:T(8,128)S(1)}, f32[512,256]{1,0:T(8,128)S(1)}, u32[]{:S(2)}, u32[]{:S(2)}) collective-permute-start(f32[512,256]{1,0:T(8,128)S(1)} %get-tuple-element.287), channel_id=1, source_target_pairs={{0,2},{1,3},{2,0},{3,1},{4,6},{5,7},{6,4},{7,5},{8,10},{9,11},{10,... | collective-permute-start | bytes 1572872 | tf_op jit(solution)/shard_map/ppermute | solution.py:735
  190.8 6.3 %collective-permute-start.21 = (f32[512,1024]{1,0:T(8,128)S(1)}, f32[512,1024]{1,0:T(8,128)S(1)}, u32[]{:S(2)}, u32[]{:S(2)}) collective-permute-start(f32[512,1024]{1,0:T(8,128)S(1)} %get-tuple-element.308.near_ref), channel_id=1, source_target_pairs={{0,1},{1,0},{2,3},{3,2},{4,5},{5,4},{6,7},{7,6},{8,9},{9,8},{10,11... | collective-permute-start | bytes 6291464 | tf_op jit(solution)/shard_map/ppermute | solution.py:731
  191.4 25.1 %collective-permute-start.25 = (f32[256,1024]{1,0:T(8,128)S(1)}, f32[256,1024]{1,0:T(8,128)S(1)}, u32[]{:S(2)}, u32[]{:S(2)}) collective-permute-start(f32[256,1024]{1,0:T(8,128)S(1)} %get-tuple-element.303), channel_id=1, source_target_pairs={{0,8},{4,12},{8,0},{12,4},{16,24},{20,28},{24,16},{28,20},{1,9},{5... | collective-permute-start | bytes 3145736 | tf_op jit(solution)/shard_map/ppermute | solution.py:764
  191.9 25.3 %collective-permute-start.24 = (f32[256,1024]{1,0:T(8,128)S(1)}, f32[256,1024]{1,0:T(8,128)S(1)}, u32[]{:S(2)}, u32[]{:S(2)}) collective-permute-start(f32[256,1024]{1,0:T(8,128)S(1)} %get-tuple-element.307), channel_id=1, source_target_pairs={{0,4},{4,0},{8,12},{12,8},{16,20},{20,16},{24,28},{28,24},{1,5},{5... | collective-permute-start | bytes 3145736 | tf_op jit(solution)/shard_map/ppermute | solution.py:764
  194.4 85.3 %collective-permute-start.23 = (f32[512,1024]{1,0:T(8,128)S(1)}, f32[512,1024]{1,0:T(8,128)S(1)}, u32[]{:S(2)}, u32[]{:S(2)}) collective-permute-start(f32[512,1024]{1,0:T(8,128)S(1)} %get-tuple-element.311), channel_id=1, source_target_pairs={{0,2},{1,3},{2,0},{3,1},{4,6},{5,7},{6,4},{7,5},{8,10},{9,11},{10,... | collective-permute-start | bytes 6291464 | tf_op jit(solution)/shard_map/ppermute | solution.py:735
  217.8 25.5 %collective-permute-start.29 = (f32[536,512]{1,0:T(8,128)S(1)}, f32[536,512]{1,0:T(8,128)S(1)}, u32[]{:S(2)}, u32[]{:S(2)}) collective-permute-start(f32[536,512]{1,0:T(8,128)S(1)} %get-tuple-element.328), channel_id=1, source_target_pairs={{0,4},{4,0},{8,12},{12,8},{16,20},{20,16},{24,28},{28,24},{1,5},{5... | collective-permute-start | bytes 3293192 | tf_op jit(solution)/shard_map/ppermute | solution.py:764
  219.4 48.6 %collective-permute-start.26 = (f32[512,512]{1,0:T(8,128)S(1)}, f32[512,512]{1,0:T(8,128)S(1)}, u32[]{:S(2)}, u32[]{:S(2)}) collective-permute-start(f32[512,512]{1,0:T(8,128)S(1)} %get-tuple-element.324), channel_id=1, source_target_pairs={{0,8},{4,12},{8,0},{12,4},{16,24},{20,28},{24,16},{28,20},{1,9},{5... | collective-permute-start | bytes 3145736 | tf_op jit(solution)/shard_map/ppermute | solution.py:764
  220.5 34.9 %collective-permute-start.28 = (f32[128,1024]{1,0:T(8,128)S(1)}, f32[128,1024]{1,0:T(8,128)S(1)}, u32[]{:S(2)}, u32[]{:S(2)}) collective-permute-start(f32[128,1024]{1,0:T(8,128)S(1)} %get-tuple-element.321), channel_id=1, source_target_pairs={{0,16},{4,20},{8,24},{12,28},{16,0},{20,4},{24,8},{28,12},{1,17},{... | collective-permute-start | bytes 1572872 | tf_op jit(solution)/shard_map/ppermute | solution.py:764
  223.1 43.6 %collective-permute-start.27 = (f32[128,1024]{1,0:T(8,128)S(1)}, f32[128,1024]{1,0:T(8,128)S(1)}, u32[]{:S(2)}, u32[]{:S(2)}) collective-permute-start(f32[128,1024]{1,0:T(8,128)S(1)} %get-tuple-element.323), channel_id=1, source_target_pairs={{0,16},{4,20},{8,24},{12,28},{16,0},{20,4},{24,8},{28,12},{1,17},{... | collective-permute-start | bytes 1572872 | tf_op jit(solution)/shard_map/ppermute | solution.py:764
  244.0 34.3 %collective-permute-start.31 = (f32[280,512]{1,0:T(8,128)S(1)}, f32[280,512]{1,0:T(8,128)S(1)}, u32[]{:S(2)}, u32[]{:S(2)}) collective-permute-start(f32[280,512]{1,0:T(8,128)S(1)} %get-tuple-element.331), channel_id=1, source_target_pairs={{0,8},{4,12},{8,0},{12,4},{16,24},{20,28},{24,16},{28,20},{1,9},{5... | collective-permute-start | bytes 1720328 | tf_op jit(solution)/shard_map/ppermute | solution.py:764
  268.7 10.4 %collective-permute-start.30 = (f32[256,512]{1,0:T(8,128)S(1)}, f32[256,512]{1,0:T(8,128)S(1)}, u32[]{:S(2)}, u32[]{:S(2)}) collective-permute-start(f32[256,512]{1,0:T(8,128)S(1)} %get-tuple-element.336), channel_id=1, source_target_pairs={{0,4},{4,0},{8,12},{12,8},{16,20},{20,16},{24,28},{28,24},{1,5},{5... | collective-permute-start | bytes 1572872 | tf_op jit(solution)/shard_map/ppermute | solution.py:764
  280.5 7.0 %collective-permute-start.32 = (f32[512,1024]{1,0:T(8,128)S(1)}, f32[512,1024]{1,0:T(8,128)}, u32[]{:S(2)}, u32[]{:S(2)}) collective-permute-start(f32[512,1024]{1,0:T(8,128)S(1)} %add.94.mine_ref), channel_id=1, source_target_pairs={{0,1},{1,0},{2,3},{3,2},{4,5},{5,4},{6,7},{7,6},{8,9},{9,8},{10,11... | collective-permute-start | bytes 6291464 | tf_op jit(solution)/shard_map/ppermute | solution.py:731
  281.3 24.2 %collective-permute-start.33 = (f32[152,512]{1,0:T(8,128)}, f32[152,512]{1,0:T(8,128)S(1)}, u32[]{:S(2)}, u32[]{:S(2)}) collective-permute-start(f32[152,512]{1,0:T(8,128)} %copy-done.23), channel_id=1, source_target_pairs={{0,16},{4,20},{8,24},{12,28},{16,0},{20,4},{24,8},{28,12},{1,17},{... | collective-permute-start | bytes 933896 | tf_op jit(solution)/shard_map/ppermute | solution.py:764
  287.5 23.4 %collective-permute-start.34 = (f32[128,512]{1,0:T(8,128)}, f32[128,512]{1,0:T(8,128)S(1)}, u32[]{:S(2)}, u32[]{:S(2)}) collective-permute-start(f32[128,512]{1,0:T(8,128)} %copy-done.24), channel_id=1, source_target_pairs={{0,16},{4,20},{8,24},{12,28},{16,0},{20,4},{24,8},{28,12},{1,17},{... | collective-permute-start | bytes 786440 | tf_op jit(solution)/shard_map/ppermute | solution.py:764
  (28 other events, 218.9 us)

commit v4 on v3

--- a/solution.py
+++ b/solution.py
@@ -985,8 +985,6 @@
     *filled, part, ub_d, mark_d = back_rows(False, 1, line.hold(chip_b), slope_b, 0, filled)
     got_b = swap_chip(part)
     line.mark(part)
-    back_a = add(back_a, line.hold(got_a))
-    line.mark(back_a)
     out_wide, grad_fed, grad_pre = filled
 
     def in_order(value, fixed, order):
@@ -1009,6 +1007,8 @@
     down_other = pair(1, down_sum, line.hold(gf_cols), act)[0]
     down_given = swap_core(down_other)
     line.mark(down_other)
+    back_a = add(back_a, line.hold(got_a))
+    line.mark(back_a)
     up_other = pair(1, up_sum, lo_cols, line.hold(grad_pre))[0]
     up_given = swap_core(up_other)
     line.mark(up_other)

time: 313 us -> 312 us (level)
  transfers between devices with their start and end apart: 35 -> 35, of which waited for: 26 -> 28; matrix products, arithmetic and copies ran while one was open for 2% -> 2% of each run, Pallas kernels for 33% -> 34%
where the time goes in v4:
time: 312 us; the launch traced here: 311 us
  waiting for transfers between devices  149 us (48%)
  Pallas kernels  109 us (35%)
  starting transfers between devices  37.3 us (12%)
  local copies, waits for them, and re-layouts  12.1 us (4%)
    ppermute x13, waiting for transfers between devices, dp_swap(): return lax.ppermute(value, 'dp', [(i, i ^ 1 << bit) for i in range(parts)])  83.2 us
    pallas_call x41, Pallas kernels, whole(): pl.pallas_call(kernel, in_specs=[pl.BlockSpec(memory_space=pltpu.SMEM)] *...  72.7 us
    ppermute x14, waiting for transfers between devices, swap_chip(): return lax.ppermute(value, 'mp', [(i, i ^ 2) for i in range(4)])  55 us
    pallas_call x2, Pallas kernels, attn_bwd(): pl.pallas_call(functools.partial(attn_bwd_kernel, bool(sums)), grid=(rows...  19.6 us
    ppermute x14, starting transfers between devices, swap_chip(): return lax.ppermute(value, 'mp', [(i, i ^ 2) for i in range(4)])  18.5 us
    ppermute x13, starting transfers between devices, dp_swap(): return lax.ppermute(value, 'dp', [(i, i ^ 1 << bit) for i in range(parts)])  17.9 us
    ppermute x8, waiting for transfers between devices, swap_core(): return lax.ppermute(value, 'mp', [(i, i ^ 1) for i in range(4)])  11.2 us
    pallas_call x2, Pallas kernels, attn_fwd(): pl.pallas_call(attn_fwd_kernel, grid=(rows // block,), in_specs=[pl.Block...  8.78 us
  transfers between devices with their start and end apart: 35, of which 28 were waited for; matrix products, arithmetic and copies ran while one was open for 2% of the time, Pallas kernels for 34%

profile of v4, /device:TPU:0, one launch (start us, length us, event | category | flops | bytes accessed | tf_op | source)
XLA Modules:
  0.0 311.4 jit_solution(17780869782589649651)
XLA Ops:
  5.9 3.0 collective-permute-start
  8.9 5.6 %qkv.1 = (f32[8,256]{1,0:T(8,128)}, bf16[1024,1024]{1,0:T(8,128)(2,1)}, bf16[512,256]{1,0:T(8,128)(2,1)}, bf16[512,256]{1,0:T(8,128)(2,1)}, bf16[1024,256]{1,0:T(8,128)(2,1)}, /*index=5*/bf16[1024,256]{1,0:T(8,128)(2,1)}) custom-call(s32[13]{0:T(128)} %concatenate.30.meta_ref, bf16[1024,1024]{1,0:T(8,128)(2,1)} %all_ref, bf16[1024,256]{1,0:T(8,128)(2,1)} %qw_ref.3, ...), custom_call_target="tpu_custom_call" | custom-call | flops 1024 | bytes 1024 | tf_op jit(solution)/shard_map/qkv/pallas_call | solution.py:342
  17.5 4.4 %attn_fwd.2 = (f32[512,256]{1,0:T(8,128)S(1)}, f32[512,128]{1,0:T(8,128)S(1)}) custom-call(bf16[512,256]{1,0:T(8,128)(2,1)S(1)} %copy-done.16, bf16[1024,256]{1,0:T(8,128)(2,1)S(1)} %copy-done.3, bf16[1024,256]{1,0:T(8,128)(2,1)S(1)} %copy-done.5, f32[1,1024]{1,0:T(1,128)S(1)} %compare_select_fusion.bias_ref.refs_4_), custom_call_target="tpu_custom_call" | custom-call | flops 1024 | bytes 1024 | tf_op jit(solution)/shard_map/attn_fwd/pallas_call | solution.py:64
  25.9 4.4 %attn_fwd.3 = (bf16[512,256]{1,0:T(8,128)(2,1)S(1)}, f32[512,128]{1,0:T(8,128)S(1)}) custom-call(bf16[512,256]{1,0:T(8,128)(2,1)S(1)} %copy-done.18, bf16[1024,256]{1,0:T(8,128)(2,1)S(1)} %copy-done.3, bf16[1024,256]{1,0:T(8,128)(2,1)S(1)} %copy-done.5, f32[1,1024]{1,0:T(1,128)S(1)} %compare_select_fusion.bias_ref.refs_4_), custom_call_target="tpu_custom_call" | custom-call | flops 1024 | bytes 1024 | tf_op jit(solution)/shard_map/attn_fwd/pallas_call | solution.py:64
  31.1 6.7 %collective-permute-done.1.other_ref = f32[512,256]{1,0:T(8,128)S(1)} collective-permute-done((f32[512,256]{1,0:T(8,128)S(1)}, f32[512,256]{1,0:T(8,128)S(1)}, u32[]{:S(2)}, u32[]{:S(2)}) %collective-permute-start.1) | collective-permute-done | bytes 524320 | tf_op jit(solution)/shard_map/ppermute | solution.py:735
  45.5 5.2 %feed.3 = (bf16[512,1024]{1,0:T(8,128)(2,1)S(1)}, bf16[512,2048]{1,0:T(8,128)(2,1)S(1)}, f32[256,2048]{1,0:T(8,128)S(1)}, f32[128,1024]{1,0:T(8,128)S(1)}, f32[128,1024]{1,0:T(8,128)S(1)}) custom-call(f32[256,1024]{1,0:T(8,128)S(1)} %get-tuple-element.208.refs_0_, bf16[1024,1024]{1,0:T(8,128)(2,1)S(1)} %copy-done, ...), custom_call_target="tpu_custom_call" | custom-call | flops 1024 | bytes 1024 | tf_op jit(solution)/shard_map/feed/pallas_call | solution.py:184
  50.7 7.0 %collective-permute-done.6.refs_0_ = f32[128,1024]{1,0:T(8,128)S(1)} collective-permute-done((f32[128,1024]{1,0:T(8,128)S(1)}, f32[128,1024]{1,0:T(8,128)S(1)}, u32[]{:S(2)}, u32[]{:S(2)}) %collective-permute-start.6) | collective-permute-done | bytes 524320 | tf_op jit(solution)/shard_map/ppermute | solution.py:735
  57.7 3.7 %feed.4 = (bf16[512,1024]{1,0:T(8,128)(2,1)S(1)}, bf16[512,2048]{1,0:T(8,128)(2,1)S(1)}, f32[128,2048]{1,0:T(8,128)S(1)}, f32[128,1024]{1,0:T(8,128)S(1)}) custom-call(f32[128,1024]{1,0:T(8,128)S(1)} %collective-permute-done.6.refs_0_, bf16[1024,1024]{1,0:T(8,128)(2,1)S(1)} %copy-done, ...), custom_call_target="tpu_custom_call", output_to_operand_aliasing={{0}: (7, {}), {1}: (8, {})} | custom-call | flops 1024 | bytes 1024 | tf_op jit(solution)/shard_map/feed/pallas_call | solution.py:184
  62.7 6.2 %collective-permute-done.5.refs_0_ = f32[128,1024]{1,0:T(8,128)S(1)} collective-permute-done((f32[128,1024]{1,0:T(8,128)S(1)}, f32[128,1024]{1,0:T(8,128)S(1)}, u32[]{:S(2)}, u32[]{:S(2)}) %collective-permute-start.5) | collective-permute-done | bytes 524320 | tf_op jit(solution)/shard_map/ppermute | solution.py:735
  69.0 3.7 %feed.5 = (bf16[512,1024]{1,0:T(8,128)(2,1)S(1)}, bf16[512,2048]{1,0:T(8,128)(2,1)S(1)}, f32[128,2048]{1,0:T(8,128)S(1)}, f32[128,1024]{1,0:T(8,128)S(1)}) custom-call(f32[128,1024]{1,0:T(8,128)S(1)} %collective-permute-done.5.refs_0_, bf16[1024,1024]{1,0:T(8,128)(2,1)S(1)} %copy-done, ...), custom_call_target="tpu_custom_call", output_to_operand_aliasing={{0}: (7, {}), {1}: (8, {})} | custom-call | flops 1024 | bytes 1024 | tf_op jit(solution)/shard_map/feed/pallas_call | solution.py:184
  74.0 6.2 %collective-permute-done.8.refs_1_ = f32[128,1024]{1,0:T(8,128)S(1)} collective-permute-done((f32[128,1024]{1,0:T(8,128)S(1)}, f32[128,1024]{1,0:T(8,128)S(1)}, u32[]{:S(2)}, u32[]{:S(2)}) %collective-permute-start.8) | collective-permute-done | bytes 524320 | tf_op jit(solution)/shard_map/ppermute | solution.py:735
  81.5 6.3 %feed_back.4 = (f32[512,1024]{1,0:T(8,128)S(1)}, bf16[512,1024]{1,0:T(8,128)(2,1)S(1)}, bf16[512,2048]{1,0:T(8,128)(2,1)S(1)}, f32[128,1024]{1,0:T(8,128)S(1)}, ...) custom-call(s32[13]{0:T(128)S(1)} %copy-done.19, ...), custom_call_target="tpu_custom_call" | custom-call | flops 1024 | bytes 1024 | tf_op jit(solution)/shard_map/feed_back/pallas_call | solution.py:184
  87.8 3.6 %collective-permute-done.7.refs_1_ = f32[128,1024]{1,0:T(8,128)S(1)} collective-permute-done((f32[128,1024]{1,0:T(8,128)S(1)}, f32[128,1024]{1,0:T(8,128)S(1)}, u32[]{:S(2)}, u32[]{:S(2)}) %collective-permute-start.7) | collective-permute-done | bytes 524320 | tf_op jit(solution)/shard_map/ppermute | solution.py:735
  92.8 6.0 %feed_back.5 = (f32[512,1024]{1,0:T(8,128)S(1)}, bf16[512,1024]{1,0:T(8,128)(2,1)S(1)}, bf16[512,2048]{1,0:T(8,128)(2,1)S(1)}, f32[128,1024]{1,0:T(8,128)S(1)}, ...) custom-call(s32[13]{0:T(128)S(1)} %copy-done.19, ...), custom_call_target="tpu_custom_call", output_to_operand_aliasing={{0}: (10, {}), {1}: (11, {}), {2}: (12, {})} | custom-call | flops 1024 | bytes 1024 | tf_op jit(solution)/shard_map/feed_back/pallas_call | solution.py:184
  98.8 3.9 %collective-permute-done.10.y_ref = f32[128,1024]{1,0:T(8,128)S(1)} collective-permute-done((f32[128,1024]{1,0:T(8,128)S(1)}, f32[128,1024]{1,0:T(8,128)S(1)}, u32[]{:S(2)}, u32[]{:S(2)}) %collective-permute-start.10) | collective-permute-done | bytes 524320 | tf_op jit(solution)/shard_map/ppermute | solution.py:735
  102.7 5.9 %feed_back.6 = (f32[512,1024]{1,0:T(8,128)S(1)}, bf16[512,1024]{1,0:T(8,128)(2,1)S(1)}, bf16[512,2048]{1,0:T(8,128)(2,1)S(1)}, f32[128,1024]{1,0:T(8,128)S(1)}, ...) custom-call(s32[13]{0:T(128)S(1)} %copy-done.19, ...), custom_call_target="tpu_custom_call", output_to_operand_aliasing={{0}: (10, {}), {1}: (11, {}), {2}: (12, {})} | custom-call | flops 1024 | bytes 1024 | tf_op jit(solution)/shard_map/feed_back/pallas_call | solution.py:184
  110.0 3.9 %collective-permute-done.9.y_ref = f32[128,1024]{1,0:T(8,128)S(1)} collective-permute-done((f32[128,1024]{1,0:T(8,128)S(1)}, f32[128,1024]{1,0:T(8,128)S(1)}, u32[]{:S(2)}, u32[]{:S(2)}) %collective-permute-start.9) | collective-permute-done | bytes 524320 | tf_op jit(solution)/shard_map/ppermute | solution.py:735
  113.9 6.0 %feed_back.7 = (f32[512,1024]{1,0:T(8,128)S(1)}, bf16[512,1024]{1,0:T(8,128)(2,1)S(1)}, bf16[512,2048]{1,0:T(8,128)(2,1)S(1)}, f32[128,1024]{1,0:T(8,128)S(1)}, ...) custom-call(s32[13]{0:T(128)S(1)} %copy-done.19, ...), custom_call_target="tpu_custom_call", output_to_operand_aliasing={{0}: (10, {}), {1}: (11, {}), {2}: (12, {})} | custom-call | flops 1024 | bytes 1024 | tf_op jit(solution)/shard_map/feed_back/pallas_call | solution.py:184
  136.9 3.8 %collective-permute-done.14.refs_6_ = f32[128,1024]{1,0:T(8,128)S(1)} collective-permute-done((f32[128,1024]{1,0:T(8,128)S(1)}, f32[128,1024]{1,0:T(8,128)S(1)}, u32[]{:S(2)}, u32[]{:S(2)}) %collective-permute-start.14) | collective-permute-done | bytes 524320 | tf_op jit(solution)/shard_map/ppermute | solution.py:735
  143.2 2.7 collective-permute-done.16.sib_ref
  151.8 9.8 %attn_bwd.2 = (bf16[512,256]{1,0:T(8,128)(2,1)S(1)}, f32[1024,256]{1,0:T(8,128)S(1)}, f32[1024,256]{1,0:T(8,128)S(1)}) custom-call(bf16[512,256]{1,0:T(8,128)(2,1)S(1)} %copy-done.18, bf16[512,256]{1,0:T(8,128)(2,1)S(1)} %get-tuple-element.282.refs_1_, bf16[1024,256]{1,0:T(8,128)(2,1)S(1)} %copy-done.4, bf16[1024,256]{1,0:T(8,128)(2,1)S(1)} %copy-done.6, ...), custom_call_target="tpu_custom_call" | custom-call | flops 1024 | bytes 1024 | tf_op jit(solution)/shard_map/attn_bwd/pallas_call | solution.py:135
  163.1 9.8 %attn_bwd.3 = (bf16[512,256]{1,0:T(8,128)(2,1)S(1)}, bf16[1024,256]{1,0:T(8,128)(2,1)S(1)}, bf16[1024,256]{1,0:T(8,128)(2,1)S(1)}) custom-call(bf16[512,256]{1,0:T(8,128)(2,1)S(1)} %copy-done.17, f32[544,256]{1,0:T(8,128)S(1)} %collective-permute-done.20.refs_1_.far_sums_ref, bf16[1024,256]{1,0:T(8,128)(2,1)S(1)} %copy-done.4, ...), custom_call_target="tpu_custom_call" | custom-call | flops 1024 | bytes 1024 | tf_op jit(solution)/shard_map/attn_bwd/pallas_call | solution.py:135
  175.0 9.7 %collective-permute-done.19.got_b_ref = f32[512,256]{1,0:T(8,128)S(1)} collective-permute-done((f32[512,256]{1,0:T(8,128)S(1)}, f32[512,256]{1,0:T(8,128)S(1)}, u32[]{:S(2)}, u32[]{:S(2)}) %collective-permute-start.19) | collective-permute-done | bytes 524320 | tf_op jit(solution)/shard_map/ppermute | solution.py:735
  198.7 15.8 %collective-permute-done.25.got_ref = f32[256,1024]{1,0:T(8,128)S(1)} collective-permute-done((f32[256,1024]{1,0:T(8,128)S(1)}, f32[256,1024]{1,0:T(8,128)S(1)}, u32[]{:S(2)}, u32[]{:S(2)}) %collective-permute-start.25) | collective-permute-done | bytes 1048608 | tf_op jit(solution)/shard_map/ppermute | solution.py:764
  221.7 20.0 %collective-permute-done.29.got_ref = f32[536,512]{1,0:T(8,128)S(1)} collective-permute-done((f32[536,512]{1,0:T(8,128)S(1)}, f32[536,512]{1,0:T(8,128)S(1)}, u32[]{:S(2)}, u32[]{:S(2)}) %collective-permute-start.29) | collective-permute-done | bytes 1097760 | tf_op jit(solution)/shard_map/ppermute | solution.py:764
  243.8 9.9 %collective-permute-done.28.got_ref = f32[128,1024]{1,0:T(8,128)S(1)} collective-permute-done((f32[128,1024]{1,0:T(8,128)S(1)}, f32[128,1024]{1,0:T(8,128)S(1)}, u32[]{:S(2)}, u32[]{:S(2)}) %collective-permute-start.28) | collective-permute-done | bytes 524320 | tf_op jit(solution)/shard_map/ppermute | solution.py:764
  255.1 9.8 %collective-permute-done.27.got_ref = f32[128,1024]{1,0:T(8,128)S(1)} collective-permute-done((f32[128,1024]{1,0:T(8,128)S(1)}, f32[128,1024]{1,0:T(8,128)S(1)}, u32[]{:S(2)}, u32[]{:S(2)}) %collective-permute-start.27) | collective-permute-done | bytes 524320 | tf_op jit(solution)/shard_map/ppermute | solution.py:764
  267.7 9.1 %collective-permute-done.31.got_ref = f32[280,512]{1,0:T(8,128)S(1)} collective-permute-done((f32[280,512]{1,0:T(8,128)S(1)}, f32[280,512]{1,0:T(8,128)S(1)}, u32[]{:S(2)}, u32[]{:S(2)}) %collective-permute-start.31) | collective-permute-done | bytes 573472 | tf_op jit(solution)/shard_map/ppermute | solution.py:764
  279.9 3.4 %collective-permute-start.33 = (f32[152,512]{1,0:T(8,128)}, f32[152,512]{1,0:T(8,128)S(1)}, u32[]{:S(2)}, u32[]{:S(2)}) collective-permute-start(f32[152,512]{1,0:T(8,128)} %copy-done.23), channel_id=1, source_target_pairs={{0,16},{4,20},{8,24},{12,28},{16,0},{20,4},{24,8},{28,12},{1,17},{... | collective-permute-start | bytes 933896 | tf_op jit(solution)/shard_map/ppermute | solution.py:764
  286.1 3.7 %place.1 = f32[1024,1024]{1,0:T(8,128)} custom-call(s32[13]{0:T(128)S(1)} %copy-done.19, f32[512,1024]{1,0:T(8,128)S(1)} %add.94.mine_ref, f32[512,1024]{1,0:T(8,128)} %collective-permute-done.32.other_ref), custom_call_target="tpu_custom_call" | custom-call | flops 1024 | bytes 1024 | tf_op jit(solution)/shard_map/place/pallas_call | solution.py:184
  289.8 14.3 %collective-permute-done.33.got_ref = f32[152,512]{1,0:T(8,128)S(1)} collective-permute-done((f32[152,512]{1,0:T(8,128)}, f32[152,512]{1,0:T(8,128)S(1)}, u32[]{:S(2)}, u32[]{:S(2)}) %collective-permute-start.33) | collective-permute-done | bytes 311328 | tf_op jit(solution)/shard_map/ppermute | solution.py:764
  306.6 2.9 collective-permute-done.34.got_ref
  (154 shorter events, 92.3 us)
Async XLA Ops:
  5.9 16.1 %collective-permute-start = (f32[128,1024]{1,0:T(8,128)}, f32[128,1024]{1,0:T(8,128)S(1)}, u32[]{:S(2)}, u32[]{:S(2)}) collective-permute-start(f32[128,1024]{1,0:T(8,128)} %get-tuple-element.187), channel_id=1, source_target_pairs={{0,2},{1,3},{2,0},{3,1},{4,6},{5,7},{6,4},{7,5},{8,10},{9,11},{10,... | collective-permute-start | bytes 1572872 | tf_op jit(solution)/shard_map/ppermute | solution.py:735
  23.4 21.6 %collective-permute-start.4 = (f32[2056,1024]{1,0:T(8,128)S(1)}, f32[2056,1024]{1,0:T(8,128)S(1)}, u32[]{:S(2)}, u32[]{:S(2)}) collective-permute-start(f32[2056,1024]{1,0:T(8,128)S(1)} %widen.1), channel_id=1, source_target_pairs={{0,1},{1,0},{2,3},{3,2},{4,5},{5,4},{6,7},{7,6},{8,9},{9,8},{10,11... | collective-permute-start | bytes 25264136 | tf_op jit(solution)/shard_map/ppermute | solution.py:731
  23.5 14.3 %collective-permute-start.1 = (f32[512,256]{1,0:T(8,128)S(1)}, f32[512,256]{1,0:T(8,128)S(1)}, u32[]{:S(2)}, u32[]{:S(2)}) collective-permute-start(f32[512,256]{1,0:T(8,128)S(1)} %get-tuple-element.194), channel_id=1, source_target_pairs={{0,2},{1,3},{2,0},{3,1},{4,6},{5,7},{6,4},{7,5},{8,10},{9,11},{10,... | collective-permute-start | bytes 1572872 | tf_op jit(solution)/shard_map/ppermute | solution.py:735
  24.3 14.0 %collective-permute-start.2 = (f32[128,1024]{1,0:T(8,128)S(1)}, f32[128,1024]{1,0:T(8,128)S(1)}, u32[]{:S(2)}, u32[]{:S(2)}) collective-permute-start(f32[128,1024]{1,0:T(8,128)S(1)} %collective-permute-done.o_got_ref), channel_id=1, source_target_pairs={{0,4},{4,0},{8,12},{12,8},{16,20},{20,16},{24,28},{28,24},{1,5},{5... | collective-permute-start | bytes 1572872 | tf_op jit(solution)/shard_map/ppermute | solution.py:764
  42.9 14.8 %collective-permute-start.6 = (f32[128,1024]{1,0:T(8,128)S(1)}, f32[128,1024]{1,0:T(8,128)S(1)}, u32[]{:S(2)}, u32[]{:S(2)}) collective-permute-start(f32[128,1024]{1,0:T(8,128)S(1)} %get-tuple-element.209), channel_id=1, source_target_pairs={{0,2},{1,3},{2,0},{3,1},{4,6},{5,7},{6,4},{7,5},{8,10},{9,11},{10,... | collective-permute-start | bytes 1572872 | tf_op jit(solution)/shard_map/ppermute | solution.py:735
  44.2 24.8 %collective-permute-start.5 = (f32[128,1024]{1,0:T(8,128)S(1)}, f32[128,1024]{1,0:T(8,128)S(1)}, u32[]{:S(2)}, u32[]{:S(2)}) collective-permute-start(f32[128,1024]{1,0:T(8,128)S(1)} %get-tuple-element.215), channel_id=1, source_target_pairs={{0,2},{1,3},{2,0},{3,1},{4,6},{5,7},{6,4},{7,5},{8,10},{9,11},{10,... | collective-permute-start | bytes 1572872 | tf_op jit(solution)/shard_map/ppermute | solution.py:735
  61.4 18.8 %collective-permute-start.8 = (f32[128,1024]{1,0:T(8,128)S(1)}, f32[128,1024]{1,0:T(8,128)S(1)}, u32[]{:S(2)}, u32[]{:S(2)}) collective-permute-start(f32[128,1024]{1,0:T(8,128)S(1)} %get-tuple-element.220), channel_id=1, source_target_pairs={{0,2},{1,3},{2,0},{3,1},{4,6},{5,7},{6,4},{7,5},{8,10},{9,11},{10,... | collective-permute-start | bytes 1572872 | tf_op jit(solution)/shard_map/ppermute | solution.py:735
  72.7 18.7 %collective-permute-start.7 = (f32[128,1024]{1,0:T(8,128)S(1)}, f32[128,1024]{1,0:T(8,128)S(1)}, u32[]{:S(2)}, u32[]{:S(2)}) collective-permute-start(f32[128,1024]{1,0:T(8,128)S(1)} %get-tuple-element.224), channel_id=1, source_target_pairs={{0,2},{1,3},{2,0},{3,1},{4,6},{5,7},{6,4},{7,5},{8,10},{9,11},{10,... | collective-permute-start | bytes 1572872 | tf_op jit(solution)/shard_map/ppermute | solution.py:735
  80.3 22.4 %collective-permute-start.10 = (f32[128,1024]{1,0:T(8,128)S(1)}, f32[128,1024]{1,0:T(8,128)S(1)}, u32[]{:S(2)}, u32[]{:S(2)}) collective-permute-start(f32[128,1024]{1,0:T(8,128)S(1)} %add.91.y_ref), channel_id=1, source_target_pairs={{0,2},{1,3},{2,0},{3,1},{4,6},{5,7},{6,4},{7,5},{8,10},{9,11},{10,... | collective-permute-start | bytes 1572872 | tf_op jit(solution)/shard_map/ppermute | solution.py:735
  91.5 22.4 %collective-permute-start.9 = (f32[128,1024]{1,0:T(8,128)S(1)}, f32[128,1024]{1,0:T(8,128)S(1)}, u32[]{:S(2)}, u32[]{:S(2)}) collective-permute-start(f32[128,1024]{1,0:T(8,128)S(1)} %add.92.y_ref), channel_id=1, source_target_pairs={{0,2},{1,3},{2,0},{3,1},{4,6},{5,7},{6,4},{7,5},{8,10},{9,11},{10,... | collective-permute-start | bytes 1572872 | tf_op jit(solution)/shard_map/ppermute | solution.py:735
  108.5 15.8 %collective-permute-start.11 = (f32[128,1024]{1,0:T(8,128)S(1)}, f32[128,1024]{1,0:T(8,128)S(1)}, u32[]{:S(2)}, u32[]{:S(2)}) collective-permute-start(f32[128,1024]{1,0:T(8,128)S(1)} %get-tuple-element.238), channel_id=1, source_target_pairs={{0,2},{1,3},{2,0},{3,1},{4,6},{5,7},{6,4},{7,5},{8,10},{9,11},{10,... | collective-permute-start | bytes 1572872 | tf_op jit(solution)/shard_map/ppermute | solution.py:735
  121.8 7.2 %collective-permute-start.15 = (f32[1024,1024]{1,0:T(8,128)S(1)}, f32[1024,1024]{1,0:T(8,128)S(1)}, u32[]{:S(2)}, u32[]{:S(2)}) collective-permute-start(f32[1024,1024]{1,0:T(8,128)S(1)} %pair.4), channel_id=1, source_target_pairs={{0,1},{1,0},{2,3},{3,2},{4,5},{5,4},{6,7},{7,6},{8,9},{9,8},{10,11... | collective-permute-start | bytes 12582920 | tf_op jit(solution)/shard_map/ppermute | solution.py:731
  126.2 8.8 %collective-permute-start.12 = (f32[1024,1024]{1,0:T(8,128)S(1)}, f32[1024,1024]{1,0:T(8,128)S(1)}, u32[]{:S(2)}, u32[]{:S(2)}) collective-permute-start(f32[1024,1024]{1,0:T(8,128)S(1)} %pair.5), channel_id=1, source_target_pairs={{0,1},{1,0},{2,3},{3,2},{4,5},{5,4},{6,7},{7,6},{8,9},{9,8},{10,11... | collective-permute-start | bytes 12582920 | tf_op jit(solution)/shard_map/ppermute | solution.py:731
  126.3 14.3 %collective-permute-start.14 = (f32[128,1024]{1,0:T(8,128)S(1)}, f32[128,1024]{1,0:T(8,128)S(1)}, u32[]{:S(2)}, u32[]{:S(2)}) collective-permute-start(f32[128,1024]{1,0:T(8,128)S(1)} %get-tuple-element.248), channel_id=1, source_target_pairs={{0,2},{1,3},{2,0},{3,1},{4,6},{5,7},{6,4},{7,5},{8,10},{9,11},{10,... | collective-permute-start | bytes 1572872 | tf_op jit(solution)/shard_map/ppermute | solution.py:735
  130.9 53.9 %collective-permute-start.17 = (f32[512,1024]{1,0:T(8,128)S(1)}, f32[512,1024]{1,0:T(8,128)S(1)}, u32[]{:S(2)}, u32[]{:S(2)}) collective-permute-start(f32[512,1024]{1,0:T(8,128)S(1)} %get-tuple-element.285), channel_id=1, source_target_pairs={{0,4},{4,0},{8,12},{12,8},{16,20},{20,16},{24,28},{28,24},{1,5},{5... | collective-permute-start | bytes 6291464 | tf_op jit(solution)/shard_map/ppermute | solution.py:764
  140.7 47.4 %collective-permute-start.13 = (f32[512,1024]{1,0:T(8,128)S(1)}, f32[512,1024]{1,0:T(8,128)S(1)}, u32[]{:S(2)}, u32[]{:S(2)}) collective-permute-start(f32[512,1024]{1,0:T(8,128)S(1)} %get-tuple-element.255), channel_id=1, source_target_pairs={{0,8},{4,12},{8,0},{12,4},{16,24},{20,28},{24,16},{28,20},{1,9},{5... | collective-permute-start | bytes 6291464 | tf_op jit(solution)/shard_map/ppermute | solution.py:764
  147.6 15.5 %collective-permute-start.20 = (f32[544,256]{1,0:T(8,128)S(1)}, f32[544,256]{1,0:T(8,128)S(1)}, u32[]{:S(2)}, u32[]{:S(2)}) collective-permute-start(f32[544,256]{1,0:T(8,128)S(1)} %get-tuple-element.277), channel_id=1, source_target_pairs={{0,2},{1,3},{2,0},{3,1},{4,6},{5,7},{6,4},{7,5},{8,10},{9,11},{10,... | collective-permute-start | bytes 1671176 | tf_op jit(solution)/shard_map/ppermute | solution.py:735
  149.6 25.4 %collective-permute-start.18 = (f32[512,256]{1,0:T(8,128)S(1)}, f32[512,256]{1,0:T(8,128)S(1)}, u32[]{:S(2)}, u32[]{:S(2)}) collective-permute-start(f32[512,256]{1,0:T(8,128)S(1)} %get-tuple-element.286), channel_id=1, source_target_pairs={{0,2},{1,3},{2,0},{3,1},{4,6},{5,7},{6,4},{7,5},{8,10},{9,11},{10,... | collective-permute-start | bytes 1572872 | tf_op jit(solution)/shard_map/ppermute | solution.py:735
  150.5 34.2 %collective-permute-start.19 = (f32[512,256]{1,0:T(8,128)S(1)}, f32[512,256]{1,0:T(8,128)S(1)}, u32[]{:S(2)}, u32[]{:S(2)}) collective-permute-start(f32[512,256]{1,0:T(8,128)S(1)} %get-tuple-element.287), channel_id=1, source_target_pairs={{0,2},{1,3},{2,0},{3,1},{4,6},{5,7},{6,4},{7,5},{8,10},{9,11},{10,... | collective-permute-start | bytes 1572872 | tf_op jit(solution)/shard_map/ppermute | solution.py:735
  188.8 6.3 %collective-permute-start.21 = (f32[512,1024]{1,0:T(8,128)S(1)}, f32[512,1024]{1,0:T(8,128)S(1)}, u32[]{:S(2)}, u32[]{:S(2)}) collective-permute-start(f32[512,1024]{1,0:T(8,128)S(1)} %get-tuple-element.308.near_ref), channel_id=1, source_target_pairs={{0,1},{1,0},{2,3},{3,2},{4,5},{5,4},{6,7},{7,6},{8,9},{9,8},{10,11... | collective-permute-start | bytes 6291464 | tf_op jit(solution)/shard_map/ppermute | solution.py:731
  189.4 25.1 %collective-permute-start.25 = (f32[256,1024]{1,0:T(8,128)S(1)}, f32[256,1024]{1,0:T(8,128)S(1)}, u32[]{:S(2)}, u32[]{:S(2)}) collective-permute-start(f32[256,1024]{1,0:T(8,128)S(1)} %get-tuple-element.303), channel_id=1, source_target_pairs={{0,8},{4,12},{8,0},{12,4},{16,24},{20,28},{24,16},{28,20},{1,9},{5... | collective-permute-start | bytes 3145736 | tf_op jit(solution)/shard_map/ppermute | solution.py:764
  190.4 25.2 %collective-permute-start.24 = (f32[256,1024]{1,0:T(8,128)S(1)}, f32[256,1024]{1,0:T(8,128)S(1)}, u32[]{:S(2)}, u32[]{:S(2)}) collective-permute-start(f32[256,1024]{1,0:T(8,128)S(1)} %get-tuple-element.307), channel_id=1, source_target_pairs={{0,4},{4,0},{8,12},{12,8},{16,20},{20,16},{24,28},{28,24},{1,5},{5... | collective-permute-start | bytes 3145736 | tf_op jit(solution)/shard_map/ppermute | solution.py:764
  192.5 85.9 %collective-permute-start.23 = (f32[512,1024]{1,0:T(8,128)S(1)}, f32[512,1024]{1,0:T(8,128)S(1)}, u32[]{:S(2)}, u32[]{:S(2)}) collective-permute-start(f32[512,1024]{1,0:T(8,128)S(1)} %get-tuple-element.311), channel_id=1, source_target_pairs={{0,2},{1,3},{2,0},{3,1},{4,6},{5,7},{6,4},{7,5},{8,10},{9,11},{10,... | collective-permute-start | bytes 6291464 | tf_op jit(solution)/shard_map/ppermute | solution.py:735
  216.3 25.5 %collective-permute-start.29 = (f32[536,512]{1,0:T(8,128)S(1)}, f32[536,512]{1,0:T(8,128)S(1)}, u32[]{:S(2)}, u32[]{:S(2)}) collective-permute-start(f32[536,512]{1,0:T(8,128)S(1)} %get-tuple-element.328), channel_id=1, source_target_pairs={{0,4},{4,0},{8,12},{12,8},{16,20},{20,16},{24,28},{28,24},{1,5},{5... | collective-permute-start | bytes 3293192 | tf_op jit(solution)/shard_map/ppermute | solution.py:764
  217.9 48.6 %collective-permute-start.26 = (f32[512,512]{1,0:T(8,128)S(1)}, f32[512,512]{1,0:T(8,128)S(1)}, u32[]{:S(2)}, u32[]{:S(2)}) collective-permute-start(f32[512,512]{1,0:T(8,128)S(1)} %get-tuple-element.324), channel_id=1, source_target_pairs={{0,8},{4,12},{8,0},{12,4},{16,24},{20,28},{24,16},{28,20},{1,9},{5... | collective-permute-start | bytes 3145736 | tf_op jit(solution)/shard_map/ppermute | solution.py:764
  218.8 34.9 %collective-permute-start.28 = (f32[128,1024]{1,0:T(8,128)S(1)}, f32[128,1024]{1,0:T(8,128)S(1)}, u32[]{:S(2)}, u32[]{:S(2)}) collective-permute-start(f32[128,1024]{1,0:T(8,128)S(1)} %get-tuple-element.321), channel_id=1, source_target_pairs={{0,16},{4,20},{8,24},{12,28},{16,0},{20,4},{24,8},{28,12},{1,17},{... | collective-permute-start | bytes 1572872 | tf_op jit(solution)/shard_map/ppermute | solution.py:764
  221.4 43.5 %collective-permute-start.27 = (f32[128,1024]{1,0:T(8,128)S(1)}, f32[128,1024]{1,0:T(8,128)S(1)}, u32[]{:S(2)}, u32[]{:S(2)}) collective-permute-start(f32[128,1024]{1,0:T(8,128)S(1)} %get-tuple-element.323), channel_id=1, source_target_pairs={{0,16},{4,20},{8,24},{12,28},{16,0},{20,4},{24,8},{28,12},{1,17},{... | collective-permute-start | bytes 1572872 | tf_op jit(solution)/shard_map/ppermute | solution.py:764
  242.5 34.3 %collective-permute-start.31 = (f32[280,512]{1,0:T(8,128)S(1)}, f32[280,512]{1,0:T(8,128)S(1)}, u32[]{:S(2)}, u32[]{:S(2)}) collective-permute-start(f32[280,512]{1,0:T(8,128)S(1)} %get-tuple-element.331), channel_id=1, source_target_pairs={{0,8},{4,12},{8,0},{12,4},{16,24},{20,28},{24,16},{28,20},{1,9},{5... | collective-permute-start | bytes 1720328 | tf_op jit(solution)/shard_map/ppermute | solution.py:764
  267.1 10.6 %collective-permute-start.30 = (f32[256,512]{1,0:T(8,128)S(1)}, f32[256,512]{1,0:T(8,128)S(1)}, u32[]{:S(2)}, u32[]{:S(2)}) collective-permute-start(f32[256,512]{1,0:T(8,128)S(1)} %get-tuple-element.336), channel_id=1, source_target_pairs={{0,4},{4,0},{8,12},{12,8},{16,20},{20,16},{24,28},{28,24},{1,5},{5... | collective-permute-start | bytes 1572872 | tf_op jit(solution)/shard_map/ppermute | solution.py:764
  279.0 7.0 %collective-permute-start.32 = (f32[512,1024]{1,0:T(8,128)S(1)}, f32[512,1024]{1,0:T(8,128)}, u32[]{:S(2)}, u32[]{:S(2)}) collective-permute-start(f32[512,1024]{1,0:T(8,128)S(1)} %add.94.mine_ref), channel_id=1, source_target_pairs={{0,1},{1,0},{2,3},{3,2},{4,5},{5,4},{6,7},{7,6},{8,9},{9,8},{10,11... | collective-permute-start | bytes 6291464 | tf_op jit(solution)/shard_map/ppermute | solution.py:731
  279.9 24.2 %collective-permute-start.33 = (f32[152,512]{1,0:T(8,128)}, f32[152,512]{1,0:T(8,128)S(1)}, u32[]{:S(2)}, u32[]{:S(2)}) collective-permute-start(f32[152,512]{1,0:T(8,128)} %copy-done.23), channel_id=1, source_target_pairs={{0,16},{4,20},{8,24},{12,28},{16,0},{20,4},{24,8},{28,12},{1,17},{... | collective-permute-start | bytes 933896 | tf_op jit(solution)/shard_map/ppermute | solution.py:764
  286.1 23.4 %collective-permute-start.34 = (f32[128,512]{1,0:T(8,128)}, f32[128,512]{1,0:T(8,128)S(1)}, u32[]{:S(2)}, u32[]{:S(2)}) collective-permute-start(f32[128,512]{1,0:T(8,128)} %copy-done.24), channel_id=1, source_target_pairs={{0,16},{4,20},{8,24},{12,28},{16,0},{20,4},{24,8},{28,12},{1,17},{... | collective-permute-start | bytes 786440 | tf_op jit(solution)/shard_map/ppermute | solution.py:764
  (28 other events, 219.1 us)

commit v5 on v4

--- a/solution.py
+++ b/solution.py
@@ -1080,16 +1080,16 @@
     o_got = line.hold(*o_got)
     line.mark(*o_got)
     down_sum.step()
+    up_sum.step()
     in_mine, in_away = whole(
         input_kernel,
         "input_grad",
         [line.hold(grad_q_near), grad_q_far, grad_k, grad_v, q_weight, k_weight, v_weight, first_ext],
         [shape(half, width)] * 2,
     )
-    line.mark(in_mine)
-    up_sum.step()
     in_got = swap_core(in_away)
     out_far = swap_core(line.hold(out_wide))
+    line.mark(in_mine)
     in_kept, in_sent = whole(
         chip_kernel, "chip_sum", [in_mine, line.hold(in_got)], [shape(half, width)] * 2
     )

time: 312 us -> 310 us (level)
  transfers between devices with their start and end apart: 35 -> 35, of which waited for: 28 -> 27; matrix products, arithmetic and copies ran while one was open for 2% -> 2% of each run, Pallas kernels for 34% -> 33%
where the time goes in v5:
time: 310 us
  waiting for transfers between devices  147 us (47%)
  Pallas kernels  109 us (35%)
  starting transfers between devices  38.2 us (12%)
  local copies, waits for them, and re-layouts  12.1 us (4%)
    ppermute x13, waiting for transfers between devices, dp_swap(): return lax.ppermute(value, 'dp', [(i, i ^ 1 << bit) for i in range(parts)])  82.2 us
    pallas_call x41, Pallas kernels, whole(): pl.pallas_call(kernel, in_specs=[pl.BlockSpec(memory_space=pltpu.SMEM)] *...  72.6 us
    ppermute x14, waiting for transfers between devices, swap_chip(): return lax.ppermute(value, 'mp', [(i, i ^ 2) for i in range(4)])  53.7 us
    pallas_call x2, Pallas kernels, attn_bwd(): pl.pallas_call(functools.partial(attn_bwd_kernel, bool(sums)), grid=(rows...  19.6 us
    ppermute x13, starting transfers between devices, dp_swap(): return lax.ppermute(value, 'dp', [(i, i ^ 1 << bit) for i in range(parts)])  18.8 us
    ppermute x14, starting transfers between devices, swap_chip(): return lax.ppermute(value, 'mp', [(i, i ^ 2) for i in range(4)])  18.5 us
    ppermute x8, waiting for transfers between devices, swap_core(): return lax.ppermute(value, 'mp', [(i, i ^ 1) for i in range(4)])  11 us
    pallas_call x2, Pallas kernels, attn_fwd(): pl.pallas_call(attn_fwd_kernel, grid=(rows // block,), in_specs=[pl.Block...  8.78 us
  transfers between devices with their start and end apart: 35, of which 27 were waited for; matrix products, arithmetic and copies ran while one was open for 2% of the time, Pallas kernels for 33%

profile of v5, /device:TPU:0, one launch (start us, length us, event | category | flops | bytes accessed | tf_op | source)
XLA Modules:
  0.0 309.6 jit_solution(11426354001603691877)
XLA Ops:
  5.9 3.0 collective-permute-start
  8.9 5.6 %qkv.1 = (f32[8,256]{1,0:T(8,128)}, bf16[1024,1024]{1,0:T(8,128)(2,1)}, bf16[512,256]{1,0:T(8,128)(2,1)}, bf16[512,256]{1,0:T(8,128)(2,1)}, bf16[1024,256]{1,0:T(8,128)(2,1)}, /*index=5*/bf16[1024,256]{1,0:T(8,128)(2,1)}) custom-call(s32[13]{0:T(128)} %concatenate.30.meta_ref, bf16[1024,1024]{1,0:T(8,128)(2,1)} %all_ref, bf16[1024,256]{1,0:T(8,128)(2,1)} %qw_ref.3, ...), custom_call_target="tpu_custom_call" | custom-call | flops 1024 | bytes 1024 | tf_op jit(solution)/shard_map/qkv/pallas_call | solution.py:342
  17.5 4.4 %attn_fwd.2 = (f32[512,256]{1,0:T(8,128)S(1)}, f32[512,128]{1,0:T(8,128)S(1)}) custom-call(bf16[512,256]{1,0:T(8,128)(2,1)S(1)} %copy-done.16, bf16[1024,256]{1,0:T(8,128)(2,1)S(1)} %copy-done.3, bf16[1024,256]{1,0:T(8,128)(2,1)S(1)} %copy-done.5, f32[1,1024]{1,0:T(1,128)S(1)} %compare_select_fusion.bias_ref.refs_4_), custom_call_target="tpu_custom_call" | custom-call | flops 1024 | bytes 1024 | tf_op jit(solution)/shard_map/attn_fwd/pallas_call | solution.py:64
  25.9 4.4 %attn_fwd.3 = (bf16[512,256]{1,0:T(8,128)(2,1)S(1)}, f32[512,128]{1,0:T(8,128)S(1)}) custom-call(bf16[512,256]{1,0:T(8,128)(2,1)S(1)} %copy-done.18, bf16[1024,256]{1,0:T(8,128)(2,1)S(1)} %copy-done.3, bf16[1024,256]{1,0:T(8,128)(2,1)S(1)} %copy-done.5, f32[1,1024]{1,0:T(1,128)S(1)} %compare_select_fusion.bias_ref.refs_4_), custom_call_target="tpu_custom_call" | custom-call | flops 1024 | bytes 1024 | tf_op jit(solution)/shard_map/attn_fwd/pallas_call | solution.py:64
  31.1 6.7 %collective-permute-done.1.other_ref = f32[512,256]{1,0:T(8,128)S(1)} collective-permute-done((f32[512,256]{1,0:T(8,128)S(1)}, f32[512,256]{1,0:T(8,128)S(1)}, u32[]{:S(2)}, u32[]{:S(2)}) %collective-permute-start.1) | collective-permute-done | bytes 524320 | tf_op jit(solution)/shard_map/ppermute | solution.py:735
  45.5 5.2 %feed.3 = (bf16[512,1024]{1,0:T(8,128)(2,1)S(1)}, bf16[512,2048]{1,0:T(8,128)(2,1)S(1)}, f32[256,2048]{1,0:T(8,128)S(1)}, f32[128,1024]{1,0:T(8,128)S(1)}, f32[128,1024]{1,0:T(8,128)S(1)}) custom-call(f32[256,1024]{1,0:T(8,128)S(1)} %get-tuple-element.208.refs_0_, bf16[1024,1024]{1,0:T(8,128)(2,1)S(1)} %copy-done, ...), custom_call_target="tpu_custom_call" | custom-call | flops 1024 | bytes 1024 | tf_op jit(solution)/shard_map/feed/pallas_call | solution.py:184
  50.7 7.0 %collective-permute-done.6.refs_0_ = f32[128,1024]{1,0:T(8,128)S(1)} collective-permute-done((f32[128,1024]{1,0:T(8,128)S(1)}, f32[128,1024]{1,0:T(8,128)S(1)}, u32[]{:S(2)}, u32[]{:S(2)}) %collective-permute-start.6) | collective-permute-done | bytes 524320 | tf_op jit(solution)/shard_map/ppermute | solution.py:735
  57.7 3.7 %feed.4 = (bf16[512,1024]{1,0:T(8,128)(2,1)S(1)}, bf16[512,2048]{1,0:T(8,128)(2,1)S(1)}, f32[128,2048]{1,0:T(8,128)S(1)}, f32[128,1024]{1,0:T(8,128)S(1)}) custom-call(f32[128,1024]{1,0:T(8,128)S(1)} %collective-permute-done.6.refs_0_, bf16[1024,1024]{1,0:T(8,128)(2,1)S(1)} %copy-done, ...), custom_call_target="tpu_custom_call", output_to_operand_aliasing={{0}: (7, {}), {1}: (8, {})} | custom-call | flops 1024 | bytes 1024 | tf_op jit(solution)/shard_map/feed/pallas_call | solution.py:184
  62.7 6.2 %collective-permute-done.5.refs_0_ = f32[128,1024]{1,0:T(8,128)S(1)} collective-permute-done((f32[128,1024]{1,0:T(8,128)S(1)}, f32[128,1024]{1,0:T(8,128)S(1)}, u32[]{:S(2)}, u32[]{:S(2)}) %collective-permute-start.5) | collective-permute-done | bytes 524320 | tf_op jit(solution)/shard_map/ppermute | solution.py:735
  69.0 3.7 %feed.5 = (bf16[512,1024]{1,0:T(8,128)(2,1)S(1)}, bf16[512,2048]{1,0:T(8,128)(2,1)S(1)}, f32[128,2048]{1,0:T(8,128)S(1)}, f32[128,1024]{1,0:T(8,128)S(1)}) custom-call(f32[128,1024]{1,0:T(8,128)S(1)} %collective-permute-done.5.refs_0_, bf16[1024,1024]{1,0:T(8,128)(2,1)S(1)} %copy-done, ...), custom_call_target="tpu_custom_call", output_to_operand_aliasing={{0}: (7, {}), {1}: (8, {})} | custom-call | flops 1024 | bytes 1024 | tf_op jit(solution)/shard_map/feed/pallas_call | solution.py:184
  74.0 6.2 %collective-permute-done.8.refs_1_ = f32[128,1024]{1,0:T(8,128)S(1)} collective-permute-done((f32[128,1024]{1,0:T(8,128)S(1)}, f32[128,1024]{1,0:T(8,128)S(1)}, u32[]{:S(2)}, u32[]{:S(2)}) %collective-permute-start.8) | collective-permute-done | bytes 524320 | tf_op jit(solution)/shard_map/ppermute | solution.py:735
  81.5 6.2 %feed_back.4 = (f32[512,1024]{1,0:T(8,128)S(1)}, bf16[512,1024]{1,0:T(8,128)(2,1)S(1)}, bf16[512,2048]{1,0:T(8,128)(2,1)S(1)}, f32[128,1024]{1,0:T(8,128)S(1)}, ...) custom-call(s32[13]{0:T(128)S(1)} %copy-done.19, ...), custom_call_target="tpu_custom_call" | custom-call | flops 1024 | bytes 1024 | tf_op jit(solution)/shard_map/feed_back/pallas_call | solution.py:184
  87.7 3.7 %collective-permute-done.7.refs_1_ = f32[128,1024]{1,0:T(8,128)S(1)} collective-permute-done((f32[128,1024]{1,0:T(8,128)S(1)}, f32[128,1024]{1,0:T(8,128)S(1)}, u32[]{:S(2)}, u32[]{:S(2)}) %collective-permute-start.7) | collective-permute-done | bytes 524320 | tf_op jit(solution)/shard_map/ppermute | solution.py:735
  92.8 6.2 %feed_back.5 = (f32[512,1024]{1,0:T(8,128)S(1)}, bf16[512,1024]{1,0:T(8,128)(2,1)S(1)}, bf16[512,2048]{1,0:T(8,128)(2,1)S(1)}, f32[128,1024]{1,0:T(8,128)S(1)}, ...) custom-call(s32[13]{0:T(128)S(1)} %copy-done.19, ...), custom_call_target="tpu_custom_call", output_to_operand_aliasing={{0}: (10, {}), {1}: (11, {}), {2}: (12, {})} | custom-call | flops 1024 | bytes 1024 | tf_op jit(solution)/shard_map/feed_back/pallas_call | solution.py:184
  98.9 3.7 %collective-permute-done.10.y_ref = f32[128,1024]{1,0:T(8,128)S(1)} collective-permute-done((f32[128,1024]{1,0:T(8,128)S(1)}, f32[128,1024]{1,0:T(8,128)S(1)}, u32[]{:S(2)}, u32[]{:S(2)}) %collective-permute-start.10) | collective-permute-done | bytes 524320 | tf_op jit(solution)/shard_map/ppermute | solution.py:735
  102.7 5.9 %feed_back.6 = (f32[512,1024]{1,0:T(8,128)S(1)}, bf16[512,1024]{1,0:T(8,128)(2,1)S(1)}, bf16[512,2048]{1,0:T(8,128)(2,1)S(1)}, f32[128,1024]{1,0:T(8,128)S(1)}, ...) custom-call(s32[13]{0:T(128)S(1)} %copy-done.19, ...), custom_call_target="tpu_custom_call", output_to_operand_aliasing={{0}: (10, {}), {1}: (11, {}), {2}: (12, {})} | custom-call | flops 1024 | bytes 1024 | tf_op jit(solution)/shard_map/feed_back/pallas_call | solution.py:184
  109.8 4.1 %collective-permute-done.9.y_ref = f32[128,1024]{1,0:T(8,128)S(1)} collective-permute-done((f32[128,1024]{1,0:T(8,128)S(1)}, f32[128,1024]{1,0:T(8,128)S(1)}, u32[]{:S(2)}, u32[]{:S(2)}) %collective-permute-start.9) | collective-permute-done | bytes 524320 | tf_op jit(solution)/shard_map/ppermute | solution.py:735
  113.9 5.9 %feed_back.7 = (f32[512,1024]{1,0:T(8,128)S(1)}, bf16[512,1024]{1,0:T(8,128)(2,1)S(1)}, bf16[512,2048]{1,0:T(8,128)(2,1)S(1)}, f32[128,1024]{1,0:T(8,128)S(1)}, ...) custom-call(s32[13]{0:T(128)S(1)} %copy-done.19, ...), custom_call_target="tpu_custom_call", output_to_operand_aliasing={{0}: (10, {}), {1}: (11, {}), {2}: (12, {})} | custom-call | flops 1024 | bytes 1024 | tf_op jit(solution)/shard_map/feed_back/pallas_call | solution.py:184
  121.7 2.7 collective-permute-done.11.refs_1_
  141.6 2.7 collective-permute-done.17.sib_ref
  150.2 9.8 %attn_bwd.2 = (bf16[512,256]{1,0:T(8,128)(2,1)S(1)}, f32[1024,256]{1,0:T(8,128)S(1)}, f32[1024,256]{1,0:T(8,128)S(1)}) custom-call(bf16[512,256]{1,0:T(8,128)(2,1)S(1)} %copy-done.18, bf16[512,256]{1,0:T(8,128)(2,1)S(1)} %get-tuple-element.285.refs_1_, bf16[1024,256]{1,0:T(8,128)(2,1)S(1)} %copy-done.4, bf16[1024,256]{1,0:T(8,128)(2,1)S(1)} %copy-done.6, ...), custom_call_target="tpu_custom_call" | custom-call | flops 1024 | bytes 1024 | tf_op jit(solution)/shard_map/attn_bwd/pallas_call | solution.py:135
  161.5 9.8 %attn_bwd.3 = (bf16[512,256]{1,0:T(8,128)(2,1)S(1)}, bf16[1024,256]{1,0:T(8,128)(2,1)S(1)}, bf16[1024,256]{1,0:T(8,128)(2,1)S(1)}) custom-call(bf16[512,256]{1,0:T(8,128)(2,1)S(1)} %copy-done.17, f32[544,256]{1,0:T(8,128)S(1)} %collective-permute-done.20.refs_1_.far_sums_ref, bf16[1024,256]{1,0:T(8,128)(2,1)S(1)} %copy-done.4, ...), custom_call_target="tpu_custom_call" | custom-call | flops 1024 | bytes 1024 | tf_op jit(solution)/shard_map/attn_bwd/pallas_call | solution.py:135
  173.4 9.7 %collective-permute-done.19.got_b_ref = f32[512,256]{1,0:T(8,128)S(1)} collective-permute-done((f32[512,256]{1,0:T(8,128)S(1)}, f32[512,256]{1,0:T(8,128)S(1)}, u32[]{:S(2)}, u32[]{:S(2)}) %collective-permute-start.19) | collective-permute-done | bytes 524320 | tf_op jit(solution)/shard_map/ppermute | solution.py:735
  198.5 14.9 %collective-permute-done.25.got_ref = f32[256,1024]{1,0:T(8,128)S(1)} collective-permute-done((f32[256,1024]{1,0:T(8,128)S(1)}, f32[256,1024]{1,0:T(8,128)S(1)}, u32[]{:S(2)}, u32[]{:S(2)}) %collective-permute-start.25) | collective-permute-done | bytes 1048608 | tf_op jit(solution)/shard_map/ppermute | solution.py:764
  220.8 19.8 %collective-permute-done.29.got_ref = f32[536,512]{1,0:T(8,128)S(1)} collective-permute-done((f32[536,512]{1,0:T(8,128)S(1)}, f32[536,512]{1,0:T(8,128)S(1)}, u32[]{:S(2)}, u32[]{:S(2)}) %collective-permute-start.29) | collective-permute-done | bytes 1097760 | tf_op jit(solution)/shard_map/ppermute | solution.py:764
  242.6 10.1 %collective-permute-done.28.got_ref = f32[128,1024]{1,0:T(8,128)S(1)} collective-permute-done((f32[128,1024]{1,0:T(8,128)S(1)}, f32[128,1024]{1,0:T(8,128)S(1)}, u32[]{:S(2)}, u32[]{:S(2)}) %collective-permute-start.28) | collective-permute-done | bytes 524320 | tf_op jit(solution)/shard_map/ppermute | solution.py:764
  254.2 9.8 %collective-permute-done.27.got_ref = f32[128,1024]{1,0:T(8,128)S(1)} collective-permute-done((f32[128,1024]{1,0:T(8,128)S(1)}, f32[128,1024]{1,0:T(8,128)S(1)}, u32[]{:S(2)}, u32[]{:S(2)}) %collective-permute-start.27) | collective-permute-done | bytes 524320 | tf_op jit(solution)/shard_map/ppermute | solution.py:764
  266.8 8.5 %collective-permute-done.31.got_ref = f32[280,512]{1,0:T(8,128)S(1)} collective-permute-done((f32[280,512]{1,0:T(8,128)S(1)}, f32[280,512]{1,0:T(8,128)S(1)}, u32[]{:S(2)}, u32[]{:S(2)}) %collective-permute-start.31) | collective-permute-done | bytes 573472 | tf_op jit(solution)/shard_map/ppermute | solution.py:764
  278.2 3.4 %collective-permute-start.33 = (f32[152,512]{1,0:T(8,128)}, f32[152,512]{1,0:T(8,128)S(1)}, u32[]{:S(2)}, u32[]{:S(2)}) collective-permute-start(f32[152,512]{1,0:T(8,128)} %copy-done.23), channel_id=1, source_target_pairs={{0,16},{4,20},{8,24},{12,28},{16,0},{20,4},{24,8},{28,12},{1,17},{... | collective-permute-start | bytes 933896 | tf_op jit(solution)/shard_map/ppermute | solution.py:764
  284.3 3.7 %place.1 = f32[1024,1024]{1,0:T(8,128)} custom-call(s32[13]{0:T(128)S(1)} %copy-done.19, f32[512,1024]{1,0:T(8,128)S(1)} %add.94.mine_ref, f32[512,1024]{1,0:T(8,128)} %collective-permute-done.32.other_ref), custom_call_target="tpu_custom_call" | custom-call | flops 1024 | bytes 1024 | tf_op jit(solution)/shard_map/place/pallas_call | solution.py:184
  288.0 14.3 %collective-permute-done.33.got_ref = f32[152,512]{1,0:T(8,128)S(1)} collective-permute-done((f32[152,512]{1,0:T(8,128)}, f32[152,512]{1,0:T(8,128)S(1)}, u32[]{:S(2)}, u32[]{:S(2)}) %collective-permute-start.33) | collective-permute-done | bytes 311328 | tf_op jit(solution)/shard_map/ppermute | solution.py:764
  304.8 2.9 collective-permute-done.34.got_ref
  (154 shorter events, 93.1 us)
Async XLA Ops:
  5.9 16.1 %collective-permute-start = (f32[128,1024]{1,0:T(8,128)}, f32[128,1024]{1,0:T(8,128)S(1)}, u32[]{:S(2)}, u32[]{:S(2)}) collective-permute-start(f32[128,1024]{1,0:T(8,128)} %get-tuple-element.187), channel_id=1, source_target_pairs={{0,2},{1,3},{2,0},{3,1},{4,6},{5,7},{6,4},{7,5},{8,10},{9,11},{10,... | collective-permute-start | bytes 1572872 | tf_op jit(solution)/shard_map/ppermute | solution.py:735
  23.4 21.6 %collective-permute-start.4 = (f32[2056,1024]{1,0:T(8,128)S(1)}, f32[2056,1024]{1,0:T(8,128)S(1)}, u32[]{:S(2)}, u32[]{:S(2)}) collective-permute-start(f32[2056,1024]{1,0:T(8,128)S(1)} %widen.1), channel_id=1, source_target_pairs={{0,1},{1,0},{2,3},{3,2},{4,5},{5,4},{6,7},{7,6},{8,9},{9,8},{10,11... | collective-permute-start | bytes 25264136 | tf_op jit(solution)/shard_map/ppermute | solution.py:731
  23.5 14.3 %collective-permute-start.1 = (f32[512,256]{1,0:T(8,128)S(1)}, f32[512,256]{1,0:T(8,128)S(1)}, u32[]{:S(2)}, u32[]{:S(2)}) collective-permute-start(f32[512,256]{1,0:T(8,128)S(1)} %get-tuple-element.194), channel_id=1, source_target_pairs={{0,2},{1,3},{2,0},{3,1},{4,6},{5,7},{6,4},{7,5},{8,10},{9,11},{10,... | collective-permute-start | bytes 1572872 | tf_op jit(solution)/shard_map/ppermute | solution.py:735
  24.3 14.0 %collective-permute-start.2 = (f32[128,1024]{1,0:T(8,128)S(1)}, f32[128,1024]{1,0:T(8,128)S(1)}, u32[]{:S(2)}, u32[]{:S(2)}) collective-permute-start(f32[128,1024]{1,0:T(8,128)S(1)} %collective-permute-done.o_got_ref), channel_id=1, source_target_pairs={{0,4},{4,0},{8,12},{12,8},{16,20},{20,16},{24,28},{28,24},{1,5},{5... | collective-permute-start | bytes 1572872 | tf_op jit(solution)/shard_map/ppermute | solution.py:764
  42.9 14.8 %collective-permute-start.6 = (f32[128,1024]{1,0:T(8,128)S(1)}, f32[128,1024]{1,0:T(8,128)S(1)}, u32[]{:S(2)}, u32[]{:S(2)}) collective-permute-start(f32[128,1024]{1,0:T(8,128)S(1)} %get-tuple-element.209), channel_id=1, source_target_pairs={{0,2},{1,3},{2,0},{3,1},{4,6},{5,7},{6,4},{7,5},{8,10},{9,11},{10,... | collective-permute-start | bytes 1572872 | tf_op jit(solution)/shard_map/ppermute | solution.py:735
  44.2 24.8 %collective-permute-start.5 = (f32[128,1024]{1,0:T(8,128)S(1)}, f32[128,1024]{1,0:T(8,128)S(1)}, u32[]{:S(2)}, u32[]{:S(2)}) collective-permute-start(f32[128,1024]{1,0:T(8,128)S(1)} %get-tuple-element.215), channel_id=1, source_target_pairs={{0,2},{1,3},{2,0},{3,1},{4,6},{5,7},{6,4},{7,5},{8,10},{9,11},{10,... | collective-permute-start | bytes 1572872 | tf_op jit(solution)/shard_map/ppermute | solution.py:735
  61.4 18.8 %collective-permute-start.8 = (f32[128,1024]{1,0:T(8,128)S(1)}, f32[128,1024]{1,0:T(8,128)S(1)}, u32[]{:S(2)}, u32[]{:S(2)}) collective-permute-start(f32[128,1024]{1,0:T(8,128)S(1)} %get-tuple-element.220), channel_id=1, source_target_pairs={{0,2},{1,3},{2,0},{3,1},{4,6},{5,7},{6,4},{7,5},{8,10},{9,11},{10,... | collective-permute-start | bytes 1572872 | tf_op jit(solution)/shard_map/ppermute | solution.py:735
  72.7 18.7 %collective-permute-start.7 = (f32[128,1024]{1,0:T(8,128)S(1)}, f32[128,1024]{1,0:T(8,128)S(1)}, u32[]{:S(2)}, u32[]{:S(2)}) collective-permute-start(f32[128,1024]{1,0:T(8,128)S(1)} %get-tuple-element.224), channel_id=1, source_target_pairs={{0,2},{1,3},{2,0},{3,1},{4,6},{5,7},{6,4},{7,5},{8,10},{9,11},{10,... | collective-permute-start | bytes 1572872 | tf_op jit(solution)/shard_map/ppermute | solution.py:735
  80.3 22.4 %collective-permute-start.10 = (f32[128,1024]{1,0:T(8,128)S(1)}, f32[128,1024]{1,0:T(8,128)S(1)}, u32[]{:S(2)}, u32[]{:S(2)}) collective-permute-start(f32[128,1024]{1,0:T(8,128)S(1)} %add.91.y_ref), channel_id=1, source_target_pairs={{0,2},{1,3},{2,0},{3,1},{4,6},{5,7},{6,4},{7,5},{8,10},{9,11},{10,... | collective-permute-start | bytes 1572872 | tf_op jit(solution)/shard_map/ppermute | solution.py:735
  91.5 22.4 %collective-permute-start.9 = (f32[128,1024]{1,0:T(8,128)S(1)}, f32[128,1024]{1,0:T(8,128)S(1)}, u32[]{:S(2)}, u32[]{:S(2)}) collective-permute-start(f32[128,1024]{1,0:T(8,128)S(1)} %add.92.y_ref), channel_id=1, source_target_pairs={{0,2},{1,3},{2,0},{3,1},{4,6},{5,7},{6,4},{7,5},{8,10},{9,11},{10,... | collective-permute-start | bytes 1572872 | tf_op jit(solution)/shard_map/ppermute | solution.py:735
  108.5 15.8 %collective-permute-start.11 = (f32[128,1024]{1,0:T(8,128)S(1)}, f32[128,1024]{1,0:T(8,128)S(1)}, u32[]{:S(2)}, u32[]{:S(2)}) collective-permute-start(f32[128,1024]{1,0:T(8,128)S(1)} %get-tuple-element.238), channel_id=1, source_target_pairs={{0,2},{1,3},{2,0},{3,1},{4,6},{5,7},{6,4},{7,5},{8,10},{9,11},{10,... | collective-permute-start | bytes 1572872 | tf_op jit(solution)/shard_map/ppermute | solution.py:735
  121.6 7.2 %collective-permute-start.14 = (f32[1024,1024]{1,0:T(8,128)S(1)}, f32[1024,1024]{1,0:T(8,128)S(1)}, u32[]{:S(2)}, u32[]{:S(2)}) collective-permute-start(f32[1024,1024]{1,0:T(8,128)S(1)} %pair.4), channel_id=1, source_target_pairs={{0,1},{1,0},{2,3},{3,2},{4,5},{5,4},{6,7},{7,6},{8,9},{9,8},{10,11... | collective-permute-start | bytes 12582920 | tf_op jit(solution)/shard_map/ppermute | solution.py:731
  126.2 8.6 %collective-permute-start.12 = (f32[1024,1024]{1,0:T(8,128)S(1)}, f32[1024,1024]{1,0:T(8,128)S(1)}, u32[]{:S(2)}, u32[]{:S(2)}) collective-permute-start(f32[1024,1024]{1,0:T(8,128)S(1)} %pair.5), channel_id=1, source_target_pairs={{0,1},{1,0},{2,3},{3,2},{4,5},{5,4},{6,7},{7,6},{8,9},{9,8},{10,11... | collective-permute-start | bytes 12582920 | tf_op jit(solution)/shard_map/ppermute | solution.py:731
  126.3 14.3 %collective-permute-start.16 = (f32[128,1024]{1,0:T(8,128)S(1)}, f32[128,1024]{1,0:T(8,128)S(1)}, u32[]{:S(2)}, u32[]{:S(2)}) collective-permute-start(f32[128,1024]{1,0:T(8,128)S(1)} %get-tuple-element.248), channel_id=1, source_target_pairs={{0,2},{1,3},{2,0},{3,1},{4,6},{5,7},{6,4},{7,5},{8,10},{9,11},{10,... | collective-permute-start | bytes 1572872 | tf_op jit(solution)/shard_map/ppermute | solution.py:735
  130.7 52.5 %collective-permute-start.15 = (f32[512,1024]{1,0:T(8,128)S(1)}, f32[512,1024]{1,0:T(8,128)S(1)}, u32[]{:S(2)}, u32[]{:S(2)}) collective-permute-start(f32[512,1024]{1,0:T(8,128)S(1)} %get-tuple-element.258), channel_id=1, source_target_pairs={{0,4},{4,0},{8,12},{12,8},{16,20},{20,16},{24,28},{28,24},{1,5},{5... | collective-permute-start | bytes 6291464 | tf_op jit(solution)/shard_map/ppermute | solution.py:764
  136.7 47.8 %collective-permute-start.13 = (f32[512,1024]{1,0:T(8,128)S(1)}, f32[512,1024]{1,0:T(8,128)S(1)}, u32[]{:S(2)}, u32[]{:S(2)}) collective-permute-start(f32[512,1024]{1,0:T(8,128)S(1)} %get-tuple-element.255), channel_id=1, source_target_pairs={{0,8},{4,12},{8,0},{12,4},{16,24},{20,28},{24,16},{28,20},{1,9},{5... | collective-permute-start | bytes 6291464 | tf_op jit(solution)/shard_map/ppermute | solution.py:764
  146.0 15.5 %collective-permute-start.20 = (f32[544,256]{1,0:T(8,128)S(1)}, f32[544,256]{1,0:T(8,128)S(1)}, u32[]{:S(2)}, u32[]{:S(2)}) collective-permute-start(f32[544,256]{1,0:T(8,128)S(1)} %get-tuple-element.278), channel_id=1, source_target_pairs={{0,2},{1,3},{2,0},{3,1},{4,6},{5,7},{6,4},{7,5},{8,10},{9,11},{10,... | collective-permute-start | bytes 1671176 | tf_op jit(solution)/shard_map/ppermute | solution.py:735
  148.0 25.4 %collective-permute-start.18 = (f32[512,256]{1,0:T(8,128)S(1)}, f32[512,256]{1,0:T(8,128)S(1)}, u32[]{:S(2)}, u32[]{:S(2)}) collective-permute-start(f32[512,256]{1,0:T(8,128)S(1)} %get-tuple-element.281), channel_id=1, source_target_pairs={{0,2},{1,3},{2,0},{3,1},{4,6},{5,7},{6,4},{7,5},{8,10},{9,11},{10,... | collective-permute-start | bytes 1572872 | tf_op jit(solution)/shard_map/ppermute | solution.py:735
  148.9 34.2 %collective-permute-start.19 = (f32[512,256]{1,0:T(8,128)S(1)}, f32[512,256]{1,0:T(8,128)S(1)}, u32[]{:S(2)}, u32[]{:S(2)}) collective-permute-start(f32[512,256]{1,0:T(8,128)S(1)} %get-tuple-element.282), channel_id=1, source_target_pairs={{0,2},{1,3},{2,0},{3,1},{4,6},{5,7},{6,4},{7,5},{8,10},{9,11},{10,... | collective-permute-start | bytes 1572872 | tf_op jit(solution)/shard_map/ppermute | solution.py:735
  187.7 7.1 %collective-permute-start.21 = (f32[512,1024]{1,0:T(8,128)S(1)}, f32[512,1024]{1,0:T(8,128)S(1)}, u32[]{:S(2)}, u32[]{:S(2)}) collective-permute-start(f32[512,1024]{1,0:T(8,128)S(1)} %get-tuple-element.306.near_ref), channel_id=1, source_target_pairs={{0,1},{1,0},{2,3},{3,2},{4,5},{5,4},{6,7},{7,6},{8,9},{9,8},{10,11... | collective-permute-start | bytes 6291464 | tf_op jit(solution)/shard_map/ppermute | solution.py:731
  188.2 25.1 %collective-permute-start.25 = (f32[256,1024]{1,0:T(8,128)S(1)}, f32[256,1024]{1,0:T(8,128)S(1)}, u32[]{:S(2)}, u32[]{:S(2)}) collective-permute-start(f32[256,1024]{1,0:T(8,128)S(1)} %get-tuple-element.303), channel_id=1, source_target_pairs={{0,8},{4,12},{8,0},{12,4},{16,24},{20,28},{24,16},{28,20},{1,9},{5... | collective-permute-start | bytes 3145736 | tf_op jit(solution)/shard_map/ppermute | solution.py:764
  190.0 24.9 %collective-permute-start.24 = (f32[256,1024]{1,0:T(8,128)S(1)}, f32[256,1024]{1,0:T(8,128)S(1)}, u32[]{:S(2)}, u32[]{:S(2)}) collective-permute-start(f32[256,1024]{1,0:T(8,128)S(1)} %get-tuple-element.305), channel_id=1, source_target_pairs={{0,4},{4,0},{8,12},{12,8},{16,20},{20,16},{24,28},{28,24},{1,5},{5... | collective-permute-start | bytes 3145736 | tf_op jit(solution)/shard_map/ppermute | solution.py:764
  192.2 84.5 %collective-permute-start.23 = (f32[512,1024]{1,0:T(8,128)S(1)}, f32[512,1024]{1,0:T(8,128)S(1)}, u32[]{:S(2)}, u32[]{:S(2)}) collective-permute-start(f32[512,1024]{1,0:T(8,128)S(1)} %get-tuple-element.311), channel_id=1, source_target_pairs={{0,2},{1,3},{2,0},{3,1},{4,6},{5,7},{6,4},{7,5},{8,10},{9,11},{10,... | collective-permute-start | bytes 6291464 | tf_op jit(solution)/shard_map/ppermute | solution.py:735
  215.5 25.1 %collective-permute-start.29 = (f32[536,512]{1,0:T(8,128)S(1)}, f32[536,512]{1,0:T(8,128)S(1)}, u32[]{:S(2)}, u32[]{:S(2)}) collective-permute-start(f32[536,512]{1,0:T(8,128)S(1)} %get-tuple-element.328), channel_id=1, source_target_pairs={{0,4},{4,0},{8,12},{12,8},{16,20},{20,16},{24,28},{28,24},{1,5},{5... | collective-permute-start | bytes 3293192 | tf_op jit(solution)/shard_map/ppermute | solution.py:764
  216.9 48.5 %collective-permute-start.26 = (f32[512,512]{1,0:T(8,128)S(1)}, f32[512,512]{1,0:T(8,128)S(1)}, u32[]{:S(2)}, u32[]{:S(2)}) collective-permute-start(f32[512,512]{1,0:T(8,128)S(1)} %get-tuple-element.324), channel_id=1, source_target_pairs={{0,8},{4,12},{8,0},{12,4},{16,24},{20,28},{24,16},{28,20},{1,9},{5... | collective-permute-start | bytes 3145736 | tf_op jit(solution)/shard_map/ppermute | solution.py:764
  217.9 34.9 %collective-permute-start.28 = (f32[128,1024]{1,0:T(8,128)S(1)}, f32[128,1024]{1,0:T(8,128)S(1)}, u32[]{:S(2)}, u32[]{:S(2)}) collective-permute-start(f32[128,1024]{1,0:T(8,128)S(1)} %get-tuple-element.321), channel_id=1, source_target_pairs={{0,16},{4,20},{8,24},{12,28},{16,0},{20,4},{24,8},{28,12},{1,17},{... | collective-permute-start | bytes 1572872 | tf_op jit(solution)/shard_map/ppermute | solution.py:764
  220.4 43.5 %collective-permute-start.27 = (f32[128,1024]{1,0:T(8,128)S(1)}, f32[128,1024]{1,0:T(8,128)S(1)}, u32[]{:S(2)}, u32[]{:S(2)}) collective-permute-start(f32[128,1024]{1,0:T(8,128)S(1)} %get-tuple-element.323), channel_id=1, source_target_pairs={{0,16},{4,20},{8,24},{12,28},{16,0},{20,4},{24,8},{28,12},{1,17},{... | collective-permute-start | bytes 1572872 | tf_op jit(solution)/shard_map/ppermute | solution.py:764
  241.3 34.1 %collective-permute-start.31 = (f32[280,512]{1,0:T(8,128)S(1)}, f32[280,512]{1,0:T(8,128)S(1)}, u32[]{:S(2)}, u32[]{:S(2)}) collective-permute-start(f32[280,512]{1,0:T(8,128)S(1)} %get-tuple-element.331), channel_id=1, source_target_pairs={{0,8},{4,12},{8,0},{12,4},{16,24},{20,28},{24,16},{28,20},{1,9},{5... | collective-permute-start | bytes 1720328 | tf_op jit(solution)/shard_map/ppermute | solution.py:764
  266.1 9.9 %collective-permute-start.30 = (f32[256,512]{1,0:T(8,128)S(1)}, f32[256,512]{1,0:T(8,128)S(1)}, u32[]{:S(2)}, u32[]{:S(2)}) collective-permute-start(f32[256,512]{1,0:T(8,128)S(1)} %get-tuple-element.336), channel_id=1, source_target_pairs={{0,4},{4,0},{8,12},{12,8},{16,20},{20,16},{24,28},{28,24},{1,5},{5... | collective-permute-start | bytes 1572872 | tf_op jit(solution)/shard_map/ppermute | solution.py:764
  277.3 6.9 %collective-permute-start.32 = (f32[512,1024]{1,0:T(8,128)S(1)}, f32[512,1024]{1,0:T(8,128)}, u32[]{:S(2)}, u32[]{:S(2)}) collective-permute-start(f32[512,1024]{1,0:T(8,128)S(1)} %add.94.mine_ref), channel_id=1, source_target_pairs={{0,1},{1,0},{2,3},{3,2},{4,5},{5,4},{6,7},{7,6},{8,9},{9,8},{10,11... | collective-permute-start | bytes 6291464 | tf_op jit(solution)/shard_map/ppermute | solution.py:731
  278.2 24.1 %collective-permute-start.33 = (f32[152,512]{1,0:T(8,128)}, f32[152,512]{1,0:T(8,128)S(1)}, u32[]{:S(2)}, u32[]{:S(2)}) collective-permute-start(f32[152,512]{1,0:T(8,128)} %copy-done.23), channel_id=1, source_target_pairs={{0,16},{4,20},{8,24},{12,28},{16,0},{20,4},{24,8},{28,12},{1,17},{... | collective-permute-start | bytes 933896 | tf_op jit(solution)/shard_map/ppermute | solution.py:764
  284.3 23.4 %collective-permute-start.34 = (f32[128,512]{1,0:T(8,128)}, f32[128,512]{1,0:T(8,128)S(1)}, u32[]{:S(2)}, u32[]{:S(2)}) collective-permute-start(f32[128,512]{1,0:T(8,128)} %copy-done.24), channel_id=1, source_target_pairs={{0,16},{4,20},{8,24},{12,28},{16,0},{20,4},{24,8},{28,12},{1,17},{... | collective-permute-start | bytes 786440 | tf_op jit(solution)/shard_map/ppermute | solution.py:764
  (28 other events, 219.8 us)
